TPU v7x, 512 devices: a whole 4x8x8 slice. The times are simulated.
512 devices in a mesh: row: 16 (over y, core), col: 32 (over x, z).
Axes of the slice: x: 4, y: 8, z: 8, core: 2. Of those that a mesh axis runs over, the one named last changes fastest.
Arguments:
- rhs: bfloat16 [4, 16, 32, 64, 256], P(None, 'row', 'col'), may hold values from -6 to 6
- dinv: float32 [4, 16, 32, 64, 64], P(None, 'row', 'col'), may hold values from -1.5 to 1.5, as said below
- lower: bfloat16 [6, 16, 32, 32, 64, 128], P(None, 'row', 'col'), may hold values from -0.0625 to 0.0625
- sources: int32 [6, 16, 32, 32, 2], P(None, 'row', 'col'), may hold values from -1 to 15, as said below
Outputs:
- solution: float32 [4, 16, 32, 64, 256], P(None, 'row', 'col')
Inputs may be any that keep to these rules, and one draw needn't show every extreme that they name: `dinv`: lower triangular. `sources`: for each level pair, holder and target, the live entries are distinct; in every level pair every device has a target with all 2 entries live.
All inputs are finite; a program needn't handle non-finite values.
Results may differ from a plain program's by a relative error of at most 0.002.
Values may be sent and summed in bfloat16 or wider, within the bound.
No kernel may reach another device: no remote copies, remote signals or barrier semaphores. Data moves between devices by JAX's collectives and lax.ppermute only.
A program may use at most 64 MiB of HBM per device.

v0:
```python
import jax
import jax.numpy as jnp
from jax import lax
from jax.sharding import PartitionSpec as P


def level_terms(blocks, indices, gathered):
    clipped = jnp.maximum(indices, 0)
    picked = jnp.take(gathered, clipped, axis=0)
    picked = jnp.where((indices >= 0)[:, :, None, None], picked, jnp.zeros((), gathered.dtype))
    peer_count, per_count, block_rows, rhs_width = picked.shape
    picked = picked.reshape(peer_count, per_count * block_rows, rhs_width)
    return jnp.einsum("qik,qkn->qin", blocks, picked, preferred_element_type=jnp.float32)


def on_device(rhs, dinv, lower, sources):
    levels = rhs.shape[0]
    block_rows = rhs.shape[3]
    rhs_width = rhs.shape[4]
    owned_acc = [jnp.zeros((block_rows, rhs_width), jnp.float32) for section in range(levels)]
    results = []
    pair_index = 0
    for section in range(levels):
        residual = rhs[section, 0, 0].astype(jnp.float32) - owned_acc[section]
        solution = jnp.dot(
            dinv[section, 0, 0],
            residual,
            precision=lax.Precision.HIGHEST,
            preferred_element_type=jnp.float32,
        )
        results.append(solution)
        if section + 1 < levels:
            solved = solution.astype(jnp.bfloat16)
            gathered = lax.all_gather(solved[None], "row", axis=0, tiled=True)
            partials = []
            for target in range(section + 1, levels):
                partials.append(
                    level_terms(lower[pair_index, 0, 0], sources[pair_index, 0, 0], gathered)
                )
                pair_index += 1
            arrived = lax.all_to_all(
                jnp.stack(partials, axis=1), "col", split_axis=0, concat_axis=0, tiled=True
            )
            summed = jnp.sum(arrived, axis=0)
            for position, target in enumerate(range(section + 1, levels)):
                owned_acc[target] = owned_acc[target] + summed[position]
    stacked = jnp.stack(results)
    return stacked[:, None, None]


def solution(mesh):
    in_specs = (
        P(None, "row", "col", None, None),
        P(None, "row", "col", None, None),
        P(None, "row", "col", None, None, None),
        P(None, "row", "col", None, None),
    )
    out_specs = P(None, "row", "col", None, None)
    return jax.shard_map(
        on_device, mesh=mesh, in_specs=in_specs, out_specs=out_specs, check_vma=False
    )
```

profile of v0, /device:TPU:1, one launch (start us, length us, event | category | flops | bytes accessed | tf_op | source)
XLA Modules:
  0.0 408.4 jit_solution(15218348629130027261)
XLA Ops:
  0.0 0.8 compare_and_fusion
  0.8 0.8 compare_bitcast_fusion
  1.8 0.9 fusion.46
  2.7 22.4 %all-gather = bf16[1024,256]{1,0:T(8,128)(2,1)S(1)} all-gather(bf16[64,256]{1,0:T(8,128)(2,1)S(1)} %get-tuple-element.34), channel_id=2, replica_groups=mesh['row'=16,'col'=32] {'row'}, dimensions={0}, use_global_device_ids=true | all-gather | bytes 557056 | tf_op jit(solution)/shard_map/all_gather | solution.py:34
  25.6 2.0 gather_fusion.1
  27.6 0.7 gather_fusion
  28.5 1.9 select_select_fusion.4
  30.4 2.8 convolution_bitcast_fusion.4
  33.6 2.8 convolution_bitcast_fusion.5
  36.5 0.7 gather_fusion.2
  37.8 1.6 convolution_bitcast_fusion.3
  39.5 0.6 copy-done.1
  40.2 0.8 pad_maximum_fusion
  41.0 3.4 copy.52
  44.4 10.9 %all-to-all-start = ((f32[32,3,64,256]{3,2,1,0:T(8,128)}), f32[32,3,64,256]{3,2,1,0:T(8,128)}, u32[]{:S(2)}, u32[]{:S(2)}) async-start(f32[32,3,64,256]{3,2,1,0:T(8,128)} %copy.52), calls=%async_computation | async-start | bytes 12582912 | tf_op jit(solution)/shard_map/all_to_all | solution.py:41
  56.2 141.8 %all-to-all-done = f32[32,3,64,256]{3,2,1,0:T(8,128)} async-done(((f32[32,3,64,256]{3,2,1,0:T(8,128)}), f32[32,3,64,256]{3,2,1,0:T(8,128)}, u32[]{:S(2)}, u32[]{:S(2)}) %all-to-all-start) | async-done | bytes 6291488 | tf_op jit(solution)/shard_map/all_to_all | solution.py:41
  197.9 3.2 reduce_sum.29
  201.4 17.2 %all-gather.1 = bf16[1024,256]{1,0:T(8,128)(2,1)S(1)} all-gather(bf16[64,256]{1,0:T(8,128)(2,1)S(1)} %get-tuple-element.36), channel_id=3, replica_groups=mesh['row'=16,'col'=32] {'row'}, dimensions={0}, use_global_device_ids=true | all-gather | bytes 557056 | tf_op jit(solution)/shard_map/all_gather | solution.py:34
  218.5 0.7 gather_fusion.3
  219.6 2.8 convolution_bitcast_fusion.2
  222.4 0.7 gather_fusion.4
  223.4 1.6 convolution_bitcast_fusion.1
  225.2 0.5 pad_maximum_fusion.1
  225.7 2.3 copy.59
  227.9 7.5 %all-to-all-start.1 = ((f32[32,2,64,256]{3,2,1,0:T(8,128)}), f32[32,2,64,256]{3,2,1,0:T(8,128)}, u32[]{:S(2)}, u32[]{:S(2)}) async-start(f32[32,2,64,256]{3,2,1,0:T(8,128)} %copy.59), calls=%async_computation.1 | async-start | bytes 8388608 | tf_op jit(solution)/shard_map/all_to_all | solution.py:41
  235.8 93.9 %all-to-all-done.1 = f32[32,2,64,256]{3,2,1,0:T(8,128)} async-done(((f32[32,2,64,256]{3,2,1,0:T(8,128)}), f32[32,2,64,256]{3,2,1,0:T(8,128)}, u32[]{:S(2)}, u32[]{:S(2)}) %all-to-all-start.1) | async-done | bytes 4194336 | tf_op jit(solution)/shard_map/all_to_all | solution.py:41
  329.7 2.5 reduce_sum.30
  332.4 18.1 %all-gather.2 = bf16[1024,256]{1,0:T(8,128)(2,1)S(1)} all-gather(bf16[64,256]{1,0:T(8,128)(2,1)S(1)} %get-tuple-element.38), channel_id=4, replica_groups=mesh['row'=16,'col'=32] {'row'}, dimensions={0}, use_global_device_ids=true | all-gather | bytes 557056 | tf_op jit(solution)/shard_map/all_gather | solution.py:34
  350.5 0.7 gather_fusion.5
  351.5 1.5 convolution_bitcast_fusion
  353.0 54.3 %all_to_all.15 = f32[32,1,64,256]{3,2,1,0:T(8,128)S(1)} all-to-all(f32[32,1,64,256]{3,2,1,0:T(8,128)S(1)} %convolution_bitcast_fusion), channel_id=1, replica_groups=mesh['row'=16,'col'=32] {'col'}, dimensions={0} | all-to-all | bytes 4194304 | tf_op jit(solution)/shard_map/all_to_all | solution.py:41
  407.6 0.7 maximum_bitcast_fusion
  (48 shorter events, 5.0 us)
Async XLA Ops:
  37.8 1.7 copy-start
  37.8 2.4 copy-start.1
  44.4 153.5 %all-to-all-start = ((f32[32,3,64,256]{3,2,1,0:T(8,128)}), f32[32,3,64,256]{3,2,1,0:T(8,128)}, u32[]{:S(2)}, u32[]{:S(2)}) async-start(f32[32,3,64,256]{3,2,1,0:T(8,128)} %copy.52), calls=%async_computation | async-start | bytes 12582912 | tf_op jit(solution)/shard_map/all_to_all | solution.py:41
  56.1 145.0 %copy-start.3 = (f32[4,1,1,64,64]{4,3,2,1,0:T(8,128)S(1)}, f32[4,1,1,64,64]{4,3,2,1,0:T(8,128)}, u32[]{:S(2)}) copy-start(f32[4,1,1,64,64]{4,3,2,1,0:T(8,128)} %param.7) | copy-start | bytes 196612
  56.1 145.0 %copy-start.4 = (bf16[4,1,1,64,256]{4,3,2,1,0:T(8,128)(2,1)S(1)}, bf16[4,1,1,64,256]{4,3,2,1,0:T(8,128)(2,1)}, u32[]{:S(2)}) copy-start(bf16[4,1,1,64,256]{4,3,2,1,0:T(8,128)(2,1)} %param.6) | copy-start | bytes 393220
  223.4 1.7 copy-start.2
  227.9 101.8 %all-to-all-start.1 = ((f32[32,2,64,256]{3,2,1,0:T(8,128)}), f32[32,2,64,256]{3,2,1,0:T(8,128)}, u32[]{:S(2)}, u32[]{:S(2)}) async-start(f32[32,2,64,256]{3,2,1,0:T(8,128)} %copy.59), calls=%async_computation.1 | async-start | bytes 8388608 | tf_op jit(solution)/shard_map/all_to_all | solution.py:41
where the time goes:
time: 411 us; the launch traced here: 408 us
  waiting for transfers between devices  236 us (57%)
  blocking collectives  112 us (27%)
  starting transfers between devices  18.4 us (4%)
  matrix products  14.7 us (4%)
  local copies, waits for them, and re-layouts  14.4 us (4%)
  other arithmetic  12.9 us (3%)
    all_to_all x2, waiting for transfers between devices, on_device(): lax.all_to_all(jnp.stack(partials, axis=1), 'col', split_axis=0, concat_a...  236 us
    all_gather x3, blocking collectives, on_device(): gathered = lax.all_gather(solved[None], 'row', axis=0, tiled=True)  57.7 us
    all_to_all x1, blocking collectives, on_device(): lax.all_to_all(jnp.stack(partials, axis=1), 'col', split_axis=0, concat_a...  54.3 us
    all_to_all x2, starting transfers between devices, on_device(): lax.all_to_all(jnp.stack(partials, axis=1), 'col', split_axis=0, concat_a...  18.4 us
    dot_general x6, matrix products, level_terms(): jnp.einsum('qik,qkn->qin', blocks, picked, preferred_element_type=jnp.flo...  13.2 us
  transfers between devices with their start and end apart: 2, of which 2 were waited for; matrix products, arithmetic and copies ran while one was open for 0% of the time, Pallas kernels for 0%

commit v1 on v0

v1 whole, which is shorter than its diff:
```python
import jax
import jax.numpy as jnp
from jax import lax
from jax.sharding import PartitionSpec as P


def level_terms(blocks, indices, gathered):
    clipped = jnp.maximum(indices, 0)
    picked = jnp.take(gathered, clipped, axis=0)
    picked = jnp.where((indices >= 0)[:, :, None, None], picked, jnp.zeros((), gathered.dtype))
    peer_count, per_count, block_rows, rhs_width = picked.shape
    picked = picked.reshape(peer_count, per_count * block_rows, rhs_width)
    return jnp.einsum("qik,qkn->qin", blocks, picked, preferred_element_type=jnp.float32)


def on_device(rhs, dinv, lower, sources):
    levels = rhs.shape[0]
    pair_of = {}
    for section in range(levels):
        for target in range(section + 1, levels):
            pair_of[section, target] = len(pair_of)
    gathered = []
    results = []
    for section in range(levels):
        residual = rhs[section, 0, 0].astype(jnp.float32)
        if section:
            partial = None
            for earlier in range(section):
                pair = pair_of[earlier, section]
                term = level_terms(lower[pair, 0, 0], sources[pair, 0, 0], gathered[earlier])
                partial = term if partial is None else partial + term
            arrived = lax.all_to_all(
                partial.astype(jnp.bfloat16), "col", split_axis=0, concat_axis=0, tiled=True
            )
            residual = residual - jnp.sum(arrived.astype(jnp.float32), axis=0)
        solution = jnp.dot(
            dinv[section, 0, 0],
            residual,
            precision=lax.Precision.HIGHEST,
            preferred_element_type=jnp.float32,
        )
        results.append(solution)
        if section + 1 < levels:
            solved = solution.astype(jnp.bfloat16)
            gathered.append(lax.all_gather(solved[None], "row", axis=0, tiled=True))
    return jnp.stack(results)[:, None, None]


def solution(mesh):
    in_specs = (
        P(None, "row", "col", None, None),
        P(None, "row", "col", None, None),
        P(None, "row", "col", None, None, None),
        P(None, "row", "col", None, None),
    )
    out_specs = P(None, "row", "col", None, None)
    return jax.shard_map(
        on_device, mesh=mesh, in_specs=in_specs, out_specs=out_specs, check_vma=False
    )
```

time: 411 us -> 184 us (0.45)
  waiting for transfers between devices: 236 us -> 32.5 us
  blocking collectives: 112 us -> 93.7 us
    all_to_all x2, waiting for transfers between devices: 236 us -> 32.5 us  [on_device(): lax.all_to_all(partial.astype(jnp.bfloat16), 'col', split_axis=0, concat_...]
    all_to_all x1, blocking collectives: 54.3 us -> 29.9 us  [on_device(): lax.all_to_all(partial.astype(jnp.bfloat16), 'col', split_axis=0, concat_...]
    all_gather x3, blocking collectives: 57.7 us -> 63.8 us  [on_device(): gathered.append(lax.all_gather(solved[None], 'row', axis=0, tiled=True))]
    another operation x2 -> x0, local copies, waits for them, and re-layouts: 5.69 us -> none  [on_device(): jnp.stack(partials, axis=1)]
  transfers between devices with their start and end apart: 2 -> 2, of which waited for: 2 -> 2; matrix products, arithmetic and copies ran while one was open for 0% -> 10% of each run, Pallas kernels for 0% -> 0%
where the time goes in v1:
time: 184 us; the launch traced here: 181 us
  blocking collectives  93.7 us (51%)
  waiting for transfers between devices  32.5 us (18%)
  matrix products  16.8 us (9%)
  starting transfers between devices  15.9 us (9%)
  local copies, waits for them, and re-layouts  12.6 us (7%)
  other arithmetic  9.61 us (5%)
    all_gather x3, blocking collectives, on_device(): gathered.append(lax.all_gather(solved[None], 'row', axis=0, tiled=True))  63.8 us
    all_to_all x2, waiting for transfers between devices, on_device(): lax.all_to_all(partial.astype(jnp.bfloat16), 'col', split_axis=0, concat_...  32.5 us
    all_to_all x1, blocking collectives, on_device(): lax.all_to_all(partial.astype(jnp.bfloat16), 'col', split_axis=0, concat_...  29.9 us
    all_to_all x2, starting transfers between devices, on_device(): lax.all_to_all(partial.astype(jnp.bfloat16), 'col', split_axis=0, concat_...  15.9 us
    dot_general x6, matrix products, level_terms(): jnp.einsum('qik,qkn->qin', blocks, picked, preferred_element_type=jnp.flo...  15.3 us
    gather x6, local copies, waits for them, and re-layouts, level_terms(): picked = jnp.take(gathered, clipped, axis=0)  4.08 us
  transfers between devices with their start and end apart: 2, of which 2 were waited for; matrix products, arithmetic and copies ran while one was open for 10% of the time, Pallas kernels for 0%

profile of v1, /device:TPU:1, one launch (start us, length us, event | category | flops | bytes accessed | tf_op | source)
XLA Modules:
  0.0 181.5 jit_solution(16684669490472690284)
XLA Ops:
  0.0 1.3 compare_and_fusion.1
  1.3 1.4 compare_bitcast_fusion.1
  2.9 0.9 fusion.40
  3.8 22.4 %all-gather = bf16[1024,256]{1,0:T(8,128)(2,1)S(1)} all-gather(bf16[64,256]{1,0:T(8,128)(2,1)S(1)} %get-tuple-element.34), channel_id=2, replica_groups=mesh['row'=16,'col'=32] {'row'}, dimensions={0}, use_global_device_ids=true | all-gather | bytes 557056 | tf_op jit(solution)/shard_map/all_gather | solution.py:45
  26.5 0.7 gather_fusion
  27.5 2.5 %fusion = bf16[32,64,256]{2,1,0:T(8,128)(2,1)} fusion(bf16[32,128,256]{2,1,0:T(8,128)(2,1)S(1)} %bitcast.153, bf16[6,1,1,32,64,128]{5,4,3,2,1,0:T(8,128)(2,1)} %param.8), kind=kOutput, calls=%fused_computation.18 | convolution fusion | flops 134742016 | bytes 3670016 | tf_op jit(solution)/shard_map/qik,qkn->qin/dot_general | solution.py:13
  30.0 10.9 %all-to-all-start = ((bf16[32,64,256]{2,1,0:T(8,128)(2,1)}), bf16[32,64,256]{2,1,0:T(8,128)(2,1)}, u32[]{:S(2)}, u32[]{:S(2)}) async-start(bf16[32,64,256]{2,1,0:T(8,128)(2,1)} %fusion), calls=%async_computation | async-start | bytes 2097152 | tf_op jit(solution)/shard_map/all_to_all | solution.py:32
  41.6 0.7 gather_fusion.1
  42.8 2.9 %fusion.9 = f32[32,256,64]{1,2,0:T(8,128)} fusion(bf16[32,128,256]{2,1,0:T(8,128)(2,1)S(1)} %bitcast.159, bf16[6,1,1,32,64,128]{5,4,3,2,1,0:T(8,128)(2,1)} %param.8), kind=kOutput, calls=%fused_computation.28 | convolution fusion | flops 134217728 | bytes 4718592 | tf_op jit(solution)/shard_map/qik,qkn->qin/dot_general | solution.py:13
  45.7 20.5 %all-to-all-done = bf16[32,64,256]{2,1,0:T(8,128)(2,1)} async-done(((bf16[32,64,256]{2,1,0:T(8,128)(2,1)}), bf16[32,64,256]{2,1,0:T(8,128)(2,1)}, u32[]{:S(2)}, u32[]{:S(2)}) %all-to-all-start) | async-done | bytes 1048608 | tf_op jit(solution)/shard_map/all_to_all | solution.py:32
  66.2 1.4 convert_reduce_fusion.2
  67.8 20.5 %all-gather.1 = bf16[1024,256]{1,0:T(8,128)(2,1)S(1)} all-gather(bf16[64,256]{1,0:T(8,128)(2,1)S(1)} %get-tuple-element.36), channel_id=3, replica_groups=mesh['row'=16,'col'=32] {'row'}, dimensions={0}, use_global_device_ids=true | all-gather | bytes 557056 | tf_op jit(solution)/shard_map/all_gather | solution.py:45
  88.3 0.7 gather_fusion.2
  89.3 1.2 copy-done.2
  90.6 2.6 %fusion.1 = bf16[32,64,256]{2,1,0:T(8,128)(2,1)} fusion(f32[32,256,64]{1,2,0:T(8,128)S(1)} %copy-done.2, bf16[32,128,256]{2,1,0:T(8,128)(2,1)S(1)} %bitcast.164, bf16[6,1,1,32,64,128]{5,4,3,2,1,0:T(8,128)(2,1)} %param.8), kind=kOutput, calls=%fused_computation.19 | convolution fusion | flops 135266304 | bytes 5767168 | tf_op jit(solution)/shard_map/qik,qkn->qin/dot_general | solution.py:13
  93.2 5.0 %all-to-all-start.1 = ((bf16[32,64,256]{2,1,0:T(8,128)(2,1)}), bf16[32,64,256]{2,1,0:T(8,128)(2,1)}, u32[]{:S(2)}, u32[]{:S(2)}) async-start(bf16[32,64,256]{2,1,0:T(8,128)(2,1)} %fusion.1), calls=%async_computation.1 | async-start | bytes 2097152 | tf_op jit(solution)/shard_map/all_to_all | solution.py:32
  98.3 0.7 reshape.172
  100.0 0.7 copy.36
  100.9 0.7 gather_fusion.3
  101.6 0.7 copy.34
  102.3 0.8 copy.33
  104.7 2.8 %fusion.6 = f32[32,256,64]{1,2,0:T(8,128)} fusion(bf16[32,128,256]{2,1,0:T(8,128)(2,1)S(1)} %bitcast.161, bf16[6,1,1,32,64,128]{5,4,3,2,1,0:T(8,128)(2,1)} %param.8), kind=kOutput, calls=%fused_computation.25 | convolution fusion | flops 134217728 | bytes 4718592 | tf_op jit(solution)/shard_map/qik,qkn->qin/dot_general | solution.py:13
  107.5 0.7 gather_fusion.4
  108.6 2.8 %fusion.4 = f32[32,256,64]{1,2,0:T(8,128)} fusion(bf16[32,128,256]{2,1,0:T(8,128)(2,1)S(1)} %bitcast.162, bf16[6,1,1,32,64,128]{5,4,3,2,1,0:T(8,128)(2,1)} %param.8), kind=kOutput, calls=%fused_computation.23 | convolution fusion | flops 134217728 | bytes 4718592 | tf_op jit(solution)/shard_map/qik,qkn->qin/dot_general | solution.py:13
  111.4 12.0 %all-to-all-done.1 = bf16[32,64,256]{2,1,0:T(8,128)(2,1)} async-done(((bf16[32,64,256]{2,1,0:T(8,128)(2,1)}), bf16[32,64,256]{2,1,0:T(8,128)(2,1)}, u32[]{:S(2)}, u32[]{:S(2)}) %all-to-all-start.1) | async-done | bytes 1048608 | tf_op jit(solution)/shard_map/all_to_all | solution.py:32
  123.4 1.4 convert_reduce_fusion.1
  125.0 20.9 %all-gather.2 = bf16[1024,256]{1,0:T(8,128)(2,1)S(1)} all-gather(bf16[64,256]{1,0:T(8,128)(2,1)S(1)} %get-tuple-element.38), channel_id=4, replica_groups=mesh['row'=16,'col'=32] {'row'}, dimensions={0}, use_global_device_ids=true | all-gather | bytes 557056 | tf_op jit(solution)/shard_map/all_gather | solution.py:45
  145.9 0.7 gather_fusion.5
  146.9 1.2 copy-done
  148.8 1.7 fusion.2
  150.5 29.9 %all_to_all.15 = bf16[32,64,256]{2,1,0:T(8,128)(2,1)S(1)} all-to-all(bf16[32,64,256]{2,1,0:T(8,128)(2,1)S(1)} %fusion.2), channel_id=1, replica_groups=mesh['row'=16,'col'=32] {'col'}, dimensions={0} | all-to-all | bytes 2097152 | tf_op jit(solution)/shard_map/all_to_all | solution.py:32
  180.7 0.7 maximum_bitcast_fusion
  (58 shorter events, 7.2 us)
Async XLA Ops:
  30.0 36.2 %all-to-all-start = ((bf16[32,64,256]{2,1,0:T(8,128)(2,1)}), bf16[32,64,256]{2,1,0:T(8,128)(2,1)}, u32[]{:S(2)}, u32[]{:S(2)}) async-start(bf16[32,64,256]{2,1,0:T(8,128)(2,1)} %fusion), calls=%async_computation | async-start | bytes 2097152 | tf_op jit(solution)/shard_map/all_to_all | solution.py:32
  42.8 24.8 %copy-start.3 = (f32[4,1,1,64,64]{4,3,2,1,0:T(8,128)S(1)}, f32[4,1,1,64,64]{4,3,2,1,0:T(8,128)}, u32[]{:S(2)}) copy-start(f32[4,1,1,64,64]{4,3,2,1,0:T(8,128)} %param.7) | copy-start | bytes 196612
  42.8 24.8 %copy-start.4 = (bf16[4,1,1,64,256]{4,3,2,1,0:T(8,128)(2,1)S(1)}, bf16[4,1,1,64,256]{4,3,2,1,0:T(8,128)(2,1)}, u32[]{:S(2)}) copy-start(bf16[4,1,1,64,256]{4,3,2,1,0:T(8,128)(2,1)} %param.6) | copy-start | bytes 393220
  89.0 1.6 copy-start.2
  93.2 5.0 %copy-start.7 = (s32[32,2]{0,1:T(2,128)S(1)}, s32[32,2]{0,1:T(2,128)}, u32[]{:S(2)}) copy-start(s32[32,2]{0,1:T(2,128)} %get-tuple-element.33) | copy-start | bytes 772
  93.2 5.8 %copy-start.9 = (pred[32,2]{0,1:T(4,128)(4,1)S(1)}, pred[32,2]{0,1:T(4,128)(4,1)}, u32[]{:S(2)}) copy-start(pred[32,2]{0,1:T(4,128)(4,1)} %get-tuple-element.32) | copy-start | bytes 196
  93.2 5.9 %copy-start.11 = (pred[32,2]{0,1:T(4,128)(4,1)S(1)}, pred[32,2]{0,1:T(4,128)(4,1)}, u32[]{:S(2)}) copy-start(pred[32,2]{0,1:T(4,128)(4,1)} %get-tuple-element.23) | copy-start | bytes 196
  93.2 6.7 %copy-start.8 = (pred[32,2]{0,1:T(4,128)(4,1)S(1)}, pred[32,2]{0,1:T(4,128)(4,1)}, u32[]{:S(2)}) copy-start(pred[32,2]{0,1:T(4,128)(4,1)} %get-tuple-element.6) | copy-start | bytes 196
  93.2 6.8 %copy-start.10 = (pred[32,2]{0,1:T(4,128)(4,1)S(1)}, pred[32,2]{0,1:T(4,128)(4,1)}, u32[]{:S(2)}) copy-start(pred[32,2]{0,1:T(4,128)(4,1)} %get-tuple-element.18) | copy-start | bytes 196
  93.2 7.5 %copy-start.6 = (s32[32,2]{0,1:T(2,128)S(1)}, s32[32,2]{0,1:T(2,128)}, u32[]{:S(2)}) copy-start(s32[32,2]{0,1:T(2,128)} %get-tuple-element.31) | copy-start | bytes 772
  93.2 30.2 %all-to-all-start.1 = ((bf16[32,64,256]{2,1,0:T(8,128)(2,1)}), bf16[32,64,256]{2,1,0:T(8,128)(2,1)}, u32[]{:S(2)}, u32[]{:S(2)}) async-start(bf16[32,64,256]{2,1,0:T(8,128)(2,1)} %fusion.1), calls=%async_computation.1 | async-start | bytes 2097152 | tf_op jit(solution)/shard_map/all_to_all | solution.py:32
  107.5 0.7 copy-start.5
  146.6 1.6 copy-start
  146.6 2.2 %copy-start.1 = (f32[32,256,64]{1,2,0:T(8,128)S(1)}, f32[32,256,64]{1,2,0:T(8,128)}, u32[]{:S(2)}) copy-start(f32[32,256,64]{1,2,0:T(8,128)} %fusion.4) | copy-start | bytes 6291460

commit v2 on v1

v2 whole, which is shorter than its diff:
```python
import functools

import jax
import jax.numpy as jnp
from jax import lax
from jax.experimental import pallas as pl
from jax.experimental.pallas import tpu as pltpu
from jax.sharding import PartitionSpec as P

LANES = 128
PAD = 8
VMEM = pl.BlockSpec(memory_space=pltpu.VMEM)


def terms_kernel(pairs, sources_ref, lower_ref, *refs):
    gathered, out_ref = refs[:-1], refs[-1]
    _, targets, block_rows, depth = lower_ref.shape
    per = depth // block_rows
    halves = gathered[0].shape[2] // LANES
    tail = halves * block_rows

    def one(target, carry):
        factors, picked = [], []
        for block, pair in zip(gathered, pairs):
            factors.append(lower_ref[pair, target])
            for entry in range(per):
                source = sources_ref[(pair * targets + target) * per + entry]
                rows = block[jnp.maximum(source, 0)]
                picked.append(jnp.where(source >= 0, rows, jnp.zeros_like(rows)))
        term = jnp.dot(
            jnp.concatenate(factors, axis=1),
            jnp.concatenate(picked, axis=0),
            preferred_element_type=jnp.float32,
        )
        powers = []
        for half in range(halves):
            part = term[:, half * LANES : (half + 1) * LANES]
            largest = jnp.max(jnp.abs(part), axis=0, keepdims=True)
            power = jnp.ceil(jnp.log2(jnp.maximum(largest * 1.001, 1e-30)))
            coded = jnp.floor(part * jnp.exp2(15.0 - power) + 0.5)
            out_ref[target, half * block_rows : (half + 1) * block_rows, :] = coded.astype(
                jnp.int32
            ).astype(jnp.int16)
            powers.append(jnp.broadcast_to(power, (PAD // halves, LANES)))
        powers = jnp.concatenate(powers, axis=0)
        out_ref[target, tail : tail + PAD, :] = powers.astype(jnp.int32).astype(jnp.int16)
        return carry

    lax.fori_loop(0, targets, one, 0, unroll=8)


def local_terms(pairs, sources, lower, gathered):
    _, targets, block_rows, _ = lower.shape
    halves = gathered[0].shape[2] // LANES
    rows = halves * block_rows + PAD
    return pl.pallas_call(
        functools.partial(terms_kernel, pairs),
        out_shape=jax.ShapeDtypeStruct((targets, rows, LANES), jnp.int16),
        in_specs=[pl.BlockSpec(memory_space=pltpu.SMEM)] + [VMEM] * (1 + len(gathered)),
        out_specs=VMEM,
        name="local_terms",
    )(sources, lower, *gathered)


def solve_level(section, rhs_ref, dinv_ref, arrived_ref):
    peers, _, _ = arrived_ref.shape
    block_rows, width = rhs_ref.shape[1:]
    halves = width // LANES
    tail = halves * block_rows

    def add(peer, sums):
        scales = arrived_ref[peer, tail : tail + PAD, :].astype(jnp.int32).astype(jnp.float32)
        scales = jnp.exp2(scales - 15.0)
        added = []
        for half in range(halves):
            coded = arrived_ref[peer, half * block_rows : (half + 1) * block_rows, :]
            first = half * (PAD // halves)
            scale = scales[first : first + 1, :]
            added.append(sums[half] + coded.astype(jnp.int32).astype(jnp.float32) * scale)
        return tuple(added)

    zero = jnp.zeros((block_rows, LANES), jnp.float32)
    sums = lax.fori_loop(0, peers, add, (zero,) * halves, unroll=4)
    residual = rhs_ref[section].astype(jnp.float32) - jnp.concatenate(sums, axis=1)
    return jnp.dot(
        dinv_ref[section],
        residual,
        precision=lax.Precision.HIGHEST,
        preferred_element_type=jnp.float32,
    )


def middle_kernel(section, rhs_ref, dinv_ref, arrived_ref, solution_ref, solved_ref):
    result = solve_level(section, rhs_ref, dinv_ref, arrived_ref)
    solution_ref[...] = result
    solved_ref[...] = result.astype(jnp.bfloat16)


def last_kernel(rhs_ref, dinv_ref, arrived_ref, *refs):
    earlier, out_ref, result_ref, sems = refs[:-3], refs[-3], refs[-2], refs[-1]
    section = len(earlier)
    copies = [
        pltpu.make_async_copy(ref, out_ref.at[level], sems.at[level])
        for level, ref in enumerate(earlier)
    ]
    for copy in copies:
        copy.start()
    result_ref[...] = solve_level(section, rhs_ref, dinv_ref, arrived_ref)
    copies.append(pltpu.make_async_copy(result_ref, out_ref.at[section], sems.at[section]))
    copies[-1].start()
    for copy in copies:
        copy.wait()


def solve_middle(section, rhs, dinv, arrived):
    _, block_rows, width = rhs.shape
    return pl.pallas_call(
        functools.partial(middle_kernel, section),
        out_shape=(
            jax.ShapeDtypeStruct((block_rows, width), jnp.float32),
            jax.ShapeDtypeStruct((block_rows, width), jnp.bfloat16),
        ),
        in_specs=[VMEM] * 3,
        out_specs=(VMEM, VMEM),
        name="solve_middle",
    )(rhs, dinv, arrived)


def solve_last(rhs, dinv, arrived, earlier):
    levels, block_rows, width = rhs.shape
    return pl.pallas_call(
        last_kernel,
        out_shape=jax.ShapeDtypeStruct((levels, block_rows, width), jnp.float32),
        in_specs=[VMEM] * (3 + len(earlier)),
        out_specs=pl.BlockSpec(memory_space=pl.ANY),
        scratch_shapes=[
            pltpu.VMEM((block_rows, width), jnp.float32),
            pltpu.SemaphoreType.DMA((levels,)),
        ],
        name="solve_last",
    )(rhs, dinv, arrived, *earlier)


def on_device(rhs, dinv, lower, sources):
    levels = rhs.shape[0]
    pair_of = {}
    for section in range(levels):
        for target in range(section + 1, levels):
            pair_of[section, target] = len(pair_of)
    rhs, dinv, lower = rhs[:, 0, 0], dinv[:, 0, 0], lower[:, 0, 0]
    sources = sources.reshape(-1)
    solution = jnp.dot(
        dinv[0],
        rhs[0].astype(jnp.float32),
        precision=lax.Precision.HIGHEST,
        preferred_element_type=jnp.float32,
    )
    solved = solution.astype(jnp.bfloat16)
    solutions, gathered = [solution], []
    for section in range(1, levels):
        gathered.append(lax.all_gather(solved, "row", axis=0, tiled=False))
        pairs = tuple(pair_of[earlier, section] for earlier in range(section))
        coded = local_terms(pairs, sources, lower, gathered)
        arrived = lax.all_to_all(coded, "col", split_axis=0, concat_axis=0, tiled=True)
        if section + 1 < levels:
            solution, solved = solve_middle(section, rhs, dinv, arrived)
            solutions.append(solution)
        else:
            stacked = solve_last(rhs, dinv, arrived, solutions)
    return stacked[:, None, None]


def solution(mesh):
    in_specs = (
        P(None, "row", "col", None, None),
        P(None, "row", "col", None, None),
        P(None, "row", "col", None, None, None),
        P(None, "row", "col", None, None),
    )
    out_specs = P(None, "row", "col", None, None)
    return jax.shard_map(
        on_device, mesh=mesh, in_specs=in_specs, out_specs=out_specs, check_vma=False
    )
```

time: 184 us -> 203 us (1.10); the launches traced: 181 us -> 203 us
  blocking collectives: 93.7 us -> 177 us
  waiting for transfers between devices: 32.5 us -> 0 us
  Pallas kernels: 0 us -> 23 us
  starting transfers between devices: 15.9 us -> 0 us
  matrix products: 16.8 us -> 1.55 us
  local copies, waits for them, and re-layouts: 12.6 us -> 1.52 us
  other arithmetic: 9.61 us -> 0 us
    all_to_all x1 -> x3, blocking collectives: 29.9 us -> 115 us  [on_device(): lax.all_to_all(coded, 'col', split_axis=0, concat_axis=0, tiled=True)]
    all_to_all x2 -> x0, waiting for transfers between devices: 32.5 us -> none  [on_device(): lax.all_to_all(partial.astype(jnp.bfloat16), 'col', split_axis=0, concat_...]
    pallas_call x0 -> x6, Pallas kernels: none -> 23 us  [the longest x3 15.2 us: local_terms(): pl.pallas_call(functools.partial(terms_kernel, pairs), out_shape=jax.Shap...]
    all_to_all x2 -> x0, starting transfers between devices: 15.9 us -> none  [on_device(): lax.all_to_all(partial.astype(jnp.bfloat16), 'col', split_axis=0, concat_...]
    dot_general x10 -> x1, matrix products: 16.8 us -> 1.55 us  [on_device(): jnp.dot(dinv[0], rhs[0].astype(jnp.float32), precision=lax.Precision.HIGH...]
    gather x6 -> x0, local copies, waits for them, and re-layouts: 4.08 us -> none  [level_terms(): picked = jnp.take(gathered, clipped, axis=0)]
    reduce_sum x3 -> x0, other arithmetic: 2.92 us -> none  [on_device(): residual = residual - jnp.sum(arrived.astype(jnp.float32), axis=0)]
    unnamed x24 -> x1, local copies, waits for them, and re-layouts: 3.16 us -> 0.8 us
  transfers between devices with their start and end apart: 2 -> 0, of which waited for: 2 -> 0; matrix products, arithmetic and copies ran while one was open for 10% -> 0% of each run, Pallas kernels for 0% -> 0%
where the time goes in v2:
time: 203 us
  blocking collectives  177 us (87%)
  Pallas kernels  23 us (11%)
    all_to_all x3, blocking collectives, on_device(): lax.all_to_all(coded, 'col', split_axis=0, concat_axis=0, tiled=True)  115 us
    all_gather x3, blocking collectives, on_device(): gathered.append(lax.all_gather(solved, 'row', axis=0, tiled=False))  62.1 us
    pallas_call x3, Pallas kernels, local_terms(): pl.pallas_call(functools.partial(terms_kernel, pairs), out_shape=jax.Shap...  15.2 us
    pallas_call x2, Pallas kernels, solve_middle(): pl.pallas_call(functools.partial(middle_kernel, section), out_shape=(jax....  5.14 us

profile of v2, /device:TPU:1, one launch (start us, length us, event | category | flops | bytes accessed | tf_op | source)
XLA Modules:
  0.0 202.7 jit_solution(11120129326624488853)
XLA Ops:
  0.0 0.8 copy.6
  0.8 0.7 reshape.7.sources_ref
  1.5 1.5 fusion.5
  3.1 23.8 %all-gather = bf16[1024,256]{1,0:T(8,128)(2,1)} all-gather(bf16[64,256]{1,0:T(8,128)(2,1)S(1)} %get-tuple-element.13), channel_id=2, replica_groups=mesh['row'=16,'col'=32] {'row'}, dimensions={0}, use_global_device_ids=true | all-gather | bytes 557056 | tf_op jit(solution)/shard_map/all_gather | solution.py:161
  26.9 4.6 %local_terms.3 = s16[32,136,128]{2,1,0:T(8,128)(2,1)} custom-call(s32[384]{0:T(512)} %reshape.7.sources_ref, bf16[6,32,64,128]{3,2,1,0:T(8,128)(2,1)} %bitcast.23, bf16[16,64,256]{2,1,0:T(8,128)(2,1)} %bitcast.26), custom_call_target="tpu_custom_call" | custom-call | tf_op jit(solution)/shard_map/local_terms/pallas_call | solution.py:56
  31.5 42.3 %all_to_all.15.arrived_ref = s16[32,136,128]{2,1,0:T(8,128)(2,1)} all-to-all(s16[32,136,128]{2,1,0:T(8,128)(2,1)} %local_terms.3), channel_id=1, replica_groups=mesh['row'=16,'col'=32] {'col'}, dimensions={0} | all-to-all | bytes 2228224 | tf_op jit(solution)/shard_map/all_to_all | solution.py:164
  73.8 2.6 %solve_middle.2 = (f32[64,256]{1,0:T(8,128)}, bf16[64,256]{1,0:T(8,128)(2,1)}) custom-call(bf16[4,64,256]{2,1,0:T(8,128)(2,1)} %bitcast.32, f32[4,64,64]{2,1,0:T(8,128)} %bitcast.35, s16[32,136,128]{2,1,0:T(8,128)(2,1)} %all_to_all.15.arrived_ref), custom_call_target="tpu_custom_call" | custom-call | tf_op jit(solution)/shard_map/solve_middle/pallas_call | solution.py:117
  76.3 19.0 %all-gather.1 = bf16[1024,256]{1,0:T(8,128)(2,1)} all-gather(bf16[64,256]{1,0:T(8,128)(2,1)} %get-tuple-element.9), channel_id=3, replica_groups=mesh['row'=16,'col'=32] {'row'}, dimensions={0}, use_global_device_ids=true | all-gather | bytes 557056 | tf_op jit(solution)/shard_map/all_gather | solution.py:161
  95.3 5.1 %local_terms.4 = s16[32,136,128]{2,1,0:T(8,128)(2,1)} custom-call(s32[384]{0:T(512)} %reshape.7.sources_ref, bf16[6,32,64,128]{3,2,1,0:T(8,128)(2,1)} %bitcast.24, bf16[16,64,256]{2,1,0:T(8,128)(2,1)} %bitcast.27, bf16[16,64,256]{2,1,0:T(8,128)(2,1)} %bitcast.29), custom_call_target="tpu_custom_call" | custom-call | tf_op jit(solution)/shard_map/local_terms/pallas_call | solution.py:56
  100.4 36.1 %all_to_all.16.arrived_ref = s16[32,136,128]{2,1,0:T(8,128)(2,1)} all-to-all(s16[32,136,128]{2,1,0:T(8,128)(2,1)} %local_terms.4), channel_id=1, replica_groups=mesh['row'=16,'col'=32] {'col'}, dimensions={0} | all-to-all | bytes 2228224 | tf_op jit(solution)/shard_map/all_to_all | solution.py:164
  136.5 2.6 %solve_middle.3 = (f32[64,256]{1,0:T(8,128)}, bf16[64,256]{1,0:T(8,128)(2,1)}) custom-call(bf16[4,64,256]{2,1,0:T(8,128)(2,1)} %bitcast.33, f32[4,64,64]{2,1,0:T(8,128)} %bitcast.36, s16[32,136,128]{2,1,0:T(8,128)(2,1)} %all_to_all.16.arrived_ref), custom_call_target="tpu_custom_call" | custom-call | tf_op jit(solution)/shard_map/solve_middle/pallas_call | solution.py:117
  139.1 19.3 %all-gather.2 = bf16[1024,256]{1,0:T(8,128)(2,1)} all-gather(bf16[64,256]{1,0:T(8,128)(2,1)} %get-tuple-element.10), channel_id=4, replica_groups=mesh['row'=16,'col'=32] {'row'}, dimensions={0}, use_global_device_ids=true | all-gather | bytes 557056 | tf_op jit(solution)/shard_map/all_gather | solution.py:161
  158.4 5.5 %local_terms.5 = s16[32,136,128]{2,1,0:T(8,128)(2,1)} custom-call(s32[384]{0:T(512)} %reshape.7.sources_ref, bf16[6,32,64,128]{3,2,1,0:T(8,128)(2,1)} %bitcast.25, bf16[16,64,256]{2,1,0:T(8,128)(2,1)} %bitcast.28, bf16[16,64,256]{2,1,0:T(8,128)(2,1)} %bitcast.30, bf16[16,64,256]{2,1,0:T(8,128)(2,1)} %bitcast.31), custom_call_target="tpu_custom_call" | custom-call | tf_op jit(solution)/shard_map/local_terms/pallas_call | solution.py:56
  163.9 36.1 %all_to_all.17.arrived_ref = s16[32,136,128]{2,1,0:T(8,128)(2,1)} all-to-all(s16[32,136,128]{2,1,0:T(8,128)(2,1)} %local_terms.5), channel_id=1, replica_groups=mesh['row'=16,'col'=32] {'col'}, dimensions={0} | all-to-all | bytes 2228224 | tf_op jit(solution)/shard_map/all_to_all | solution.py:164
  200.1 2.6 %solve_last.1 = f32[4,64,256]{2,1,0:T(8,128)} custom-call(bf16[4,64,256]{2,1,0:T(8,128)(2,1)} %bitcast.34, f32[4,64,64]{2,1,0:T(8,128)} %bitcast.37, s16[32,136,128]{2,1,0:T(8,128)(2,1)} %all_to_all.17.arrived_ref, f32[64,256]{1,0:T(8,128)} %get-tuple-element.14.refs_0_, f32[64,256]{1,0:T(8,128)} %get-tuple-element.11.refs_1_, ...), custom_call_target="tpu_custom_call" | custom-call | tf_op jit(solution)/shard_map/solve_last/pallas_call | solution.py:131

commit v3 on v2

--- a/solution.py
+++ b/solution.py
@@ -9,22 +9,47 @@
 
 LANES = 128
 PAD = 8
+KERNEL_VMEM = 8 << 20
+CHUNKS = 4
 VMEM = pl.BlockSpec(memory_space=pltpu.VMEM)
 
 
+def in_vmem(array):
+    return pltpu.with_memory_space_constraint(array, pltpu.VMEM)
+
+
+def in_hbm(array):
+    return pltpu.with_memory_space_constraint(array, pltpu.HBM)
+
+
 def terms_kernel(pairs, sources_ref, lower_ref, *refs):
-    gathered, out_ref = refs[:-1], refs[-1]
+    gathered, (out_ref, factors_ref, sems) = refs[:-3], refs[-3:]
     _, targets, block_rows, depth = lower_ref.shape
+    chunk = targets // CHUNKS
+    copies = [
+        [
+            pltpu.make_async_copy(
+                lower_ref.at[pair, pl.ds(step * chunk, chunk)],
+                factors_ref.at[place, pl.ds(step * chunk, chunk)],
+                sems.at[step, place],
+            )
+            for place, pair in enumerate(pairs)
+        ]
+        for step in range(CHUNKS)
+    ]
+    for step in range(CHUNKS):
+        for copy in copies[step]:
+            copy.start()
     per = depth // block_rows
     halves = gathered[0].shape[2] // LANES
     tail = halves * block_rows
 
     def one(target, carry):
         factors, picked = [], []
-        for block, pair in zip(gathered, pairs):
-            factors.append(lower_ref[pair, target])
+        for place, (block, pair) in enumerate(zip(gathered, pairs)):
+            factors.append(factors_ref[place, target])
             for entry in range(per):
-                source = sources_ref[(pair * targets + target) * per + entry]
+                source = sources_ref[pair, entry, target]
                 rows = block[jnp.maximum(source, 0)]
                 picked.append(jnp.where(source >= 0, rows, jnp.zeros_like(rows)))
         term = jnp.dot(
@@ -46,20 +71,29 @@
         out_ref[target, tail : tail + PAD, :] = powers.astype(jnp.int32).astype(jnp.int16)
         return carry
 
-    lax.fori_loop(0, targets, one, 0, unroll=8)
+    for step in range(CHUNKS):
+        for copy in copies[step]:
+            copy.wait()
+        lax.fori_loop(step * chunk, (step + 1) * chunk, one, 0, unroll=True)
 
 
 def local_terms(pairs, sources, lower, gathered):
-    _, targets, block_rows, _ = lower.shape
+    _, targets, block_rows, depth = lower.shape
     halves = gathered[0].shape[2] // LANES
     rows = halves * block_rows + PAD
     return pl.pallas_call(
         functools.partial(terms_kernel, pairs),
-        out_shape=jax.ShapeDtypeStruct((targets, rows, LANES), jnp.int16),
-        in_specs=[pl.BlockSpec(memory_space=pltpu.SMEM)] + [VMEM] * (1 + len(gathered)),
+        out_shape=pltpu.VMEM((targets, rows, LANES), jnp.int16),
+        in_specs=[pl.BlockSpec(memory_space=pltpu.SMEM), pl.BlockSpec(memory_space=pl.ANY)]
+        + [VMEM] * len(gathered),
         out_specs=VMEM,
+        scratch_shapes=[
+            pltpu.VMEM((len(pairs), targets, block_rows, depth), lower.dtype),
+            pltpu.SemaphoreType.DMA((CHUNKS, len(pairs))),
+        ],
+        compiler_params=pltpu.CompilerParams(vmem_limit_bytes=KERNEL_VMEM),
         name="local_terms",
-    )(sources, lower, *gathered)
+    )(in_hbm(sources), in_hbm(lower), *map(in_vmem, gathered))
 
 
 def solve_level(section, rhs_ref, dinv_ref, arrived_ref):
@@ -117,13 +151,14 @@
     return pl.pallas_call(
         functools.partial(middle_kernel, section),
         out_shape=(
-            jax.ShapeDtypeStruct((block_rows, width), jnp.float32),
-            jax.ShapeDtypeStruct((block_rows, width), jnp.bfloat16),
+            pltpu.VMEM((block_rows, width), jnp.float32),
+            pltpu.VMEM((block_rows, width), jnp.bfloat16),
         ),
         in_specs=[VMEM] * 3,
         out_specs=(VMEM, VMEM),
+        compiler_params=pltpu.CompilerParams(vmem_limit_bytes=KERNEL_VMEM),
         name="solve_middle",
-    )(rhs, dinv, arrived)
+    )(*map(in_vmem, (rhs, dinv, arrived)))
 
 
 def solve_last(rhs, dinv, arrived, earlier):
@@ -137,8 +172,9 @@
             pltpu.VMEM((block_rows, width), jnp.float32),
             pltpu.SemaphoreType.DMA((levels,)),
         ],
+        compiler_params=pltpu.CompilerParams(vmem_limit_bytes=KERNEL_VMEM),
         name="solve_last",
-    )(rhs, dinv, arrived, *earlier)
+    )(*map(in_vmem, (rhs, dinv, arrived, *earlier)))
 
 
 def on_device(rhs, dinv, lower, sources):
@@ -148,7 +184,7 @@
         for target in range(section + 1, levels):
             pair_of[section, target] = len(pair_of)
     rhs, dinv, lower = rhs[:, 0, 0], dinv[:, 0, 0], lower[:, 0, 0]
-    sources = sources.reshape(-1)
+    sources = jnp.swapaxes(sources[:, 0, 0], 1, 2)
     solution = jnp.dot(
         dinv[0],
         rhs[0].astype(jnp.float32),

time: 203 us -> 183 us (0.901)
  Pallas kernels: 23 us -> 13.3 us
  blocking collectives: 177 us -> 169 us
    pallas_call x5, Pallas kernels: 20.4 us -> 12.1 us  [the longest x3 11 us: local_terms(): pl.pallas_call(functools.partial(terms_kernel, pairs), out_shape=pltpu.VM...]
    all_gather x3, blocking collectives: 62.1 us -> 57.6 us  [on_device(): gathered.append(lax.all_gather(solved, 'row', axis=0, tiled=False))]
    all_to_all x3, blocking collectives: 115 us -> 111 us  [on_device(): lax.all_to_all(coded, 'col', split_axis=0, concat_axis=0, tiled=True)]
where the time goes in v3:
time: 183 us
  blocking collectives  169 us (92%)
  Pallas kernels  13.3 us (7%)
    all_to_all x3, blocking collectives, on_device(): lax.all_to_all(coded, 'col', split_axis=0, concat_axis=0, tiled=True)  111 us
    all_gather x3, blocking collectives, on_device(): gathered.append(lax.all_gather(solved, 'row', axis=0, tiled=False))  57.6 us
    pallas_call x3, Pallas kernels, local_terms(): pl.pallas_call(functools.partial(terms_kernel, pairs), out_shape=pltpu.VM...  11 us

profile of v3, /device:TPU:1, one launch (start us, length us, event | category | flops | bytes accessed | tf_op | source)
XLA Modules:
  0.0 182.8 jit_solution(314105976476722525)
XLA Ops:
  0.0 0.9 fusion.5
  0.9 22.4 %all-gather = bf16[1024,256]{1,0:T(8,128)(2,1)S(1)} all-gather(bf16[64,256]{1,0:T(8,128)(2,1)S(1)} %get-tuple-element.13), channel_id=2, replica_groups=mesh['row'=16,'col'=32] {'row'}, dimensions={0}, use_global_device_ids=true | all-gather | bytes 557056 | tf_op jit(solution)/shard_map/all_gather | solution.py:197
  23.4 3.3 %local_terms.3 = s16[32,136,128]{2,1,0:T(8,128)(2,1)S(1)} custom-call(s32[6,2,32]{2,1,0:T(2,128)} %bitcast.37, bf16[6,32,64,128]{3,2,1,0:T(8,128)(2,1)} %bitcast.34, bf16[16,64,256]{2,1,0:T(8,128)(2,1)S(1)} %bitcast.22), custom_call_target="tpu_custom_call" | custom-call | tf_op jit(solution)/shard_map/local_terms/pallas_call | solution.py:84
  26.7 0.0 copy-start
  26.7 0.0 copy-start.1
  26.7 42.1 %all_to_all.15.arrived_ref = s16[32,136,128]{2,1,0:T(8,128)(2,1)S(1)} all-to-all(s16[32,136,128]{2,1,0:T(8,128)(2,1)S(1)} %local_terms.3), channel_id=1, replica_groups=mesh['row'=16,'col'=32] {'col'}, dimensions={0} | all-to-all | bytes 2228224 | tf_op jit(solution)/shard_map/all_to_all | solution.py:200
  68.8 0.0 copy-done
  68.8 0.0 copy-done.1
  68.8 0.5 solve_middle.2
  69.3 17.4 %all-gather.1 = bf16[1024,256]{1,0:T(8,128)(2,1)S(1)} all-gather(bf16[64,256]{1,0:T(8,128)(2,1)S(1)} %get-tuple-element.9), channel_id=3, replica_groups=mesh['row'=16,'col'=32] {'row'}, dimensions={0}, use_global_device_ids=true | all-gather | bytes 557056 | tf_op jit(solution)/shard_map/all_gather | solution.py:197
  86.7 3.6 %local_terms.4 = s16[32,136,128]{2,1,0:T(8,128)(2,1)S(1)} custom-call(s32[6,2,32]{2,1,0:T(2,128)} %bitcast.38, bf16[6,32,64,128]{3,2,1,0:T(8,128)(2,1)} %bitcast.35, bf16[16,64,256]{2,1,0:T(8,128)(2,1)S(1)} %bitcast.23, bf16[16,64,256]{2,1,0:T(8,128)(2,1)S(1)} %bitcast.25), custom_call_target="tpu_custom_call" | custom-call | tf_op jit(solution)/shard_map/local_terms/pallas_call | solution.py:84
  90.4 34.4 %all_to_all.16.arrived_ref = s16[32,136,128]{2,1,0:T(8,128)(2,1)S(1)} all-to-all(s16[32,136,128]{2,1,0:T(8,128)(2,1)S(1)} %local_terms.4), channel_id=1, replica_groups=mesh['row'=16,'col'=32] {'col'}, dimensions={0} | all-to-all | bytes 2228224 | tf_op jit(solution)/shard_map/all_to_all | solution.py:200
  124.8 0.5 solve_middle.3
  125.3 17.8 %all-gather.2 = bf16[1024,256]{1,0:T(8,128)(2,1)S(1)} all-gather(bf16[64,256]{1,0:T(8,128)(2,1)S(1)} %get-tuple-element.10), channel_id=4, replica_groups=mesh['row'=16,'col'=32] {'row'}, dimensions={0}, use_global_device_ids=true | all-gather | bytes 557056 | tf_op jit(solution)/shard_map/all_gather | solution.py:197
  143.1 4.1 %local_terms.5 = s16[32,136,128]{2,1,0:T(8,128)(2,1)S(1)} custom-call(s32[6,2,32]{2,1,0:T(2,128)} %bitcast.39, bf16[6,32,64,128]{3,2,1,0:T(8,128)(2,1)} %bitcast.36, bf16[16,64,256]{2,1,0:T(8,128)(2,1)S(1)} %bitcast.24, bf16[16,64,256]{2,1,0:T(8,128)(2,1)S(1)} %bitcast.26, bf16[16,64,256]{2,1,0:T(8,128)(2,1)S(1)} %bitcast.27), custom_call_target="tpu_custom_call" | custom-call | tf_op jit(solution)/shard_map/local_terms/pallas_call | solution.py:84
  147.2 34.4 %all_to_all.17.arrived_ref = s16[32,136,128]{2,1,0:T(8,128)(2,1)S(1)} all-to-all(s16[32,136,128]{2,1,0:T(8,128)(2,1)S(1)} %local_terms.5), channel_id=1, replica_groups=mesh['row'=16,'col'=32] {'col'}, dimensions={0} | all-to-all | bytes 2228224 | tf_op jit(solution)/shard_map/all_to_all | solution.py:200
  181.6 1.2 solve_last.1
Async XLA Ops:
  26.7 42.1 %copy-start = (bf16[4,1,1,64,256]{4,3,2,1,0:T(8,128)(2,1)S(1)}, bf16[4,1,1,64,256]{4,3,2,1,0:T(8,128)(2,1)}, u32[]{:S(2)}) copy-start(bf16[4,1,1,64,256]{4,3,2,1,0:T(8,128)(2,1)} %param.4) | copy-start | bytes 393220
  26.7 42.1 %copy-start.1 = (f32[4,1,1,64,64]{4,3,2,1,0:T(8,128)S(1)}, f32[4,1,1,64,64]{4,3,2,1,0:T(8,128)}, u32[]{:S(2)}) copy-start(f32[4,1,1,64,64]{4,3,2,1,0:T(8,128)} %param.5) | copy-start | bytes 196612

commit v4 on v3

v4 whole, which is shorter than its diff:
```python
import functools

import jax
import jax.numpy as jnp
from jax import lax
from jax.experimental import pallas as pl
from jax.experimental.pallas import tpu as pltpu
from jax.sharding import PartitionSpec as P

LANES = 128
PAD = 8
KERNEL_VMEM = 8 << 20
CHUNKS = 4
VMEM = pl.BlockSpec(memory_space=pltpu.VMEM)


def in_vmem(array):
    return pltpu.with_memory_space_constraint(array, pltpu.VMEM)


def in_hbm(array):
    return pltpu.with_memory_space_constraint(array, pltpu.HBM)


def terms_kernel(pairs, sources_ref, lower_ref, *refs):
    gathered, (out_ref, factors_ref, sems) = refs[:-3], refs[-3:]
    _, targets, block_rows, depth = lower_ref.shape
    chunk = targets // CHUNKS
    copies = [
        [
            pltpu.make_async_copy(
                lower_ref.at[pair, pl.ds(step * chunk, chunk)],
                factors_ref.at[place, pl.ds(step * chunk, chunk)],
                sems.at[step, place],
            )
            for place, pair in enumerate(pairs)
        ]
        for step in range(CHUNKS)
    ]
    for step in range(CHUNKS):
        for copy in copies[step]:
            copy.start()
    per = depth // block_rows

    def one(target, carry):
        factors, picked = [], []
        for place, (block, pair) in enumerate(zip(gathered, pairs)):
            factors.append(factors_ref[place, target])
            for entry in range(per):
                source = sources_ref[pair, entry, target]
                rows = block[jnp.maximum(source, 0)]
                picked.append(jnp.where(source >= 0, rows, jnp.zeros_like(rows)))
        term = jnp.dot(
            jnp.concatenate(factors, axis=1),
            jnp.concatenate(picked, axis=0),
            preferred_element_type=jnp.float32,
        )
        largest = jnp.max(jnp.abs(term), axis=0, keepdims=True)
        power = jnp.ceil(jnp.log2(jnp.maximum(largest * 1.001, 1e-30)))
        coded = jnp.floor(term * jnp.exp2(15.0 - power) + 0.5).astype(jnp.int32)
        out_ref[target, 0:block_rows, :] = coded.astype(jnp.int16)
        powers = jnp.broadcast_to(power, (PAD, LANES)).astype(jnp.int32)
        out_ref[target, block_rows : block_rows + PAD, :] = powers.astype(jnp.int16)
        return carry

    for step in range(CHUNKS):
        for copy in copies[step]:
            copy.wait()
        lax.fori_loop(step * chunk, (step + 1) * chunk, one, 0, unroll=True)


def local_terms(pairs, sources, lower, gathered):
    _, targets, block_rows, depth = lower.shape
    rows = block_rows + PAD
    return pl.pallas_call(
        functools.partial(terms_kernel, pairs),
        out_shape=pltpu.VMEM((targets, rows, LANES), jnp.int16),
        in_specs=[pl.BlockSpec(memory_space=pltpu.SMEM), pl.BlockSpec(memory_space=pl.ANY)]
        + [VMEM] * len(gathered),
        out_specs=VMEM,
        scratch_shapes=[
            pltpu.VMEM((len(pairs), targets, block_rows, depth), lower.dtype),
            pltpu.SemaphoreType.DMA((CHUNKS, len(pairs))),
        ],
        compiler_params=pltpu.CompilerParams(vmem_limit_bytes=KERNEL_VMEM),
        name="local_terms",
    )(in_hbm(sources), in_hbm(lower), *map(in_vmem, gathered))


def solve_level(section, chain, rhs_ref, dinv_ref, arrived_ref):
    peers = arrived_ref.shape[0]
    block_rows = rhs_ref.shape[1]

    def add(peer, total):
        powers = arrived_ref[peer, block_rows : block_rows + PAD, :].astype(jnp.int32)
        scale = jnp.exp2(powers.astype(jnp.float32) - 15.0)[0:1, :]
        coded = arrived_ref[peer, 0:block_rows, :].astype(jnp.int32).astype(jnp.float32)
        return total + coded * scale

    total = lax.fori_loop(0, peers, add, jnp.zeros((block_rows, LANES), jnp.float32), unroll=8)
    columns = rhs_ref[section, :, chain * LANES : (chain + 1) * LANES]
    return jnp.dot(
        dinv_ref[section],
        columns.astype(jnp.float32) - total,
        precision=lax.Precision.HIGHEST,
        preferred_element_type=jnp.float32,
    )


def middle_kernel(section, chain, rhs_ref, dinv_ref, arrived_ref, solution_ref, solved_ref):
    result = solve_level(section, chain, rhs_ref, dinv_ref, arrived_ref)
    solution_ref[...] = result
    solved_ref[...] = result.astype(jnp.bfloat16)


def last_kernel(chain, places, rhs_ref, dinv_ref, arrived_ref, *refs):
    earlier, out_ref, result_ref, sems = refs[:-3], refs[-3], refs[-2], refs[-1]
    section = out_ref.shape[0] - 1
    copies = []
    for index, (place, ref) in enumerate(zip(places, earlier)):
        level, start = place
        target = out_ref.at[level, :, pl.ds(start, ref.shape[1])]
        copies.append(pltpu.make_async_copy(ref, target, sems.at[index]))
    for copy in copies:
        copy.start()
    result_ref[...] = solve_level(section, chain, rhs_ref, dinv_ref, arrived_ref)
    target = out_ref.at[section, :, pl.ds(chain * LANES, LANES)]
    copies.append(pltpu.make_async_copy(result_ref, target, sems.at[len(places)]))
    copies[-1].start()
    for copy in copies:
        copy.wait()


def solve_middle(section, chain, rhs, dinv, arrived):
    block_rows = rhs.shape[1]
    return pl.pallas_call(
        functools.partial(middle_kernel, section, chain),
        out_shape=(
            pltpu.VMEM((block_rows, LANES), jnp.float32),
            pltpu.VMEM((block_rows, LANES), jnp.bfloat16),
        ),
        in_specs=[VMEM] * 3,
        out_specs=(VMEM, VMEM),
        compiler_params=pltpu.CompilerParams(vmem_limit_bytes=KERNEL_VMEM),
        name="solve_middle",
    )(*map(in_vmem, (rhs, dinv, arrived)))


def solve_last(chain, rhs, dinv, arrived, solutions):
    levels, block_rows, width = rhs.shape
    places, earlier = [(0, 0)], [solutions[0][0]]
    for other, results in enumerate(solutions):
        for level, result in enumerate(results[1:], 1):
            places.append((level, other * LANES))
            earlier.append(result)
    return pl.pallas_call(
        functools.partial(last_kernel, chain, tuple(places)),
        out_shape=jax.ShapeDtypeStruct((levels, block_rows, width), jnp.float32),
        in_specs=[VMEM] * (3 + len(earlier)),
        out_specs=pl.BlockSpec(memory_space=pl.ANY),
        scratch_shapes=[
            pltpu.VMEM((block_rows, LANES), jnp.float32),
            pltpu.SemaphoreType.DMA((len(earlier) + 1,)),
        ],
        compiler_params=pltpu.CompilerParams(vmem_limit_bytes=KERNEL_VMEM),
        name="solve_last",
    )(*map(in_vmem, (rhs, dinv, arrived, *earlier)))


def on_device(rhs, dinv, lower, sources):
    levels, _, _, _, width = rhs.shape
    pair_of = {}
    for section in range(levels):
        for target in range(section + 1, levels):
            pair_of[section, target] = len(pair_of)
    rhs, dinv, lower = rhs[:, 0, 0], dinv[:, 0, 0], lower[:, 0, 0]
    sources = jnp.swapaxes(sources[:, 0, 0], 1, 2)
    chains = range(width // LANES)
    first = jnp.dot(
        dinv[0],
        rhs[0].astype(jnp.float32),
        precision=lax.Precision.HIGHEST,
        preferred_element_type=jnp.float32,
    )
    solutions = [[first] for chain in chains]
    solved = [first[:, chain * LANES : (chain + 1) * LANES].astype(jnp.bfloat16) for chain in chains]
    gathered = [[] for chain in chains]
    pending = None
    for section in range(1, levels):
        pairs = tuple(pair_of[earlier, section] for earlier in range(section))
        for chain in chains:
            gathered[chain].append(lax.all_gather(solved[chain], "row", axis=0, tiled=False))
            coded = local_terms(pairs, sources, lower, gathered[chain])
            following = (chain + 1) % len(chains)
            if pending is None:
                coded, solved[following] = lax.optimization_barrier((coded, solved[following]))
            else:
                coded, pending = lax.optimization_barrier((coded, pending))
                before = (chain - 1) % len(chains)
                level = section if before < chain else section - 1
                solution, solved[before] = solve_middle(level, before, rhs, dinv, pending)
                solutions[before].append(solution)
            pending = lax.all_to_all(coded, "col", split_axis=0, concat_axis=0, tiled=True)
    stacked = solve_last(len(chains) - 1, rhs, dinv, pending, solutions)
    return stacked[:, None, None]


def solution(mesh):
    in_specs = (
        P(None, "row", "col", None, None),
        P(None, "row", "col", None, None),
        P(None, "row", "col", None, None, None),
        P(None, "row", "col", None, None),
    )
    out_specs = P(None, "row", "col", None, None)
    return jax.shard_map(
        on_device, mesh=mesh, in_specs=in_specs, out_specs=out_specs, check_vma=False
    )
```

time: 183 us -> 207 us (1.13); the launches traced: 183 us -> 203 us
  blocking collectives: 169 us -> 102 us
  starting transfers between devices: 0 us -> 58.7 us
  waiting for transfers between devices: 0 us -> 14.9 us
  Pallas kernels: 13.3 us -> 26.7 us
    all_to_all x3 -> x0, blocking collectives: 111 us -> none  [on_device(): lax.all_to_all(coded, 'col', split_axis=0, concat_axis=0, tiled=True)]
    all_to_all x0 -> x6, starting transfers between devices: none -> 58.7 us  [on_device(): lax.all_to_all(coded, 'col', split_axis=0, concat_axis=0, tiled=True)]
    all_gather x3 -> x6, blocking collectives: 57.6 us -> 102 us  [on_device(): lax.all_gather(solved[chain], 'row', axis=0, tiled=False)]
    all_to_all x0 -> x6, waiting for transfers between devices: none -> 14.9 us  [on_device(): lax.all_to_all(coded, 'col', split_axis=0, concat_axis=0, tiled=True)]
    pallas_call x3 -> x6, Pallas kernels: 11 us -> 23.5 us  [local_terms(): pl.pallas_call(functools.partial(terms_kernel, pairs), out_shape=pltpu.VM...]
  transfers between devices with their start and end apart: 0 -> 6, of which waited for: 0 -> 1; matrix products, arithmetic and copies ran while one was open for 0% -> 0% of each run, Pallas kernels for 0% -> 11%
where the time goes in v4:
time: 207 us; the launch traced here: 203 us
  blocking collectives  102 us (49%)
  starting transfers between devices  58.7 us (28%)
  Pallas kernels  26.7 us (13%)
  waiting for transfers between devices  14.9 us (7%)
    all_gather x6, blocking collectives, on_device(): lax.all_gather(solved[chain], 'row', axis=0, tiled=False)  102 us
    all_to_all x6, starting transfers between devices, on_device(): lax.all_to_all(coded, 'col', split_axis=0, concat_axis=0, tiled=True)  58.7 us
    pallas_call x6, Pallas kernels, local_terms(): pl.pallas_call(functools.partial(terms_kernel, pairs), out_shape=pltpu.VM...  23.5 us
    all_to_all x6, waiting for transfers between devices, on_device(): lax.all_to_all(coded, 'col', split_axis=0, concat_axis=0, tiled=True)  14.9 us
  transfers between devices with their start and end apart: 6, of which 1 were waited for; matrix products, arithmetic and copies ran while one was open for 0% of the time, Pallas kernels for 11%

profile of v4, /device:TPU:1, one launch (start us, length us, event | category | flops | bytes accessed | tf_op | source)
XLA Modules:
  0.0 203.5 jit_solution(15003956777923232765)
XLA Ops:
  0.0 0.9 fusion.6
  1.0 21.6 %all-gather = bf16[1024,128]{1,0:T(8,128)(2,1)S(1)} all-gather(bf16[64,128]{1,0:T(8,128)(2,1)S(1)} %get-tuple-element.48), channel_id=2, replica_groups=mesh['row'=16,'col'=32] {'row'}, dimensions={0}, use_global_device_ids=true | all-gather | bytes 278528 | tf_op jit(solution)/shard_map/all_gather | solution.py:192
  22.5 3.6 %local_terms.6 = s16[32,72,128]{2,1,0:T(8,128)(2,1)} custom-call(s32[6,2,32]{2,1,0:T(2,128)} %bitcast.55, bf16[6,32,64,128]{3,2,1,0:T(8,128)(2,1)} %bitcast.49, bf16[16,64,128]{2,1,0:T(8,128)(2,1)S(1)} %bitcast.40), custom_call_target="tpu_custom_call" | custom-call | tf_op jit(solution)/shard_map/local_terms/pallas_call | solution.py:75
  26.2 0.0 copy-start
  26.2 0.0 copy-start.1
  26.2 11.1 %all-to-all-start = ((s16[32,72,128]{2,1,0:T(8,128)(2,1)}), s16[32,72,128]{2,1,0:T(8,128)(2,1)S(1)}, u32[]{:S(2)}, u32[]{:S(2)}) async-start(s16[32,72,128]{2,1,0:T(8,128)(2,1)} %local_terms.6), calls=%async_computation | async-start | bytes 1179648 | tf_op jit(solution)/shard_map/all_to_all | solution.py:203
  37.3 15.9 %all-gather.1 = bf16[1024,128]{1,0:T(8,128)(2,1)S(1)} all-gather(bf16[64,128]{1,0:T(8,128)(2,1)S(1)} %get-tuple-element.26), channel_id=3, replica_groups=mesh['row'=16,'col'=32] {'row'}, dimensions={0}, use_global_device_ids=true | all-gather | bytes 278528 | tf_op jit(solution)/shard_map/all_gather | solution.py:192
  53.2 3.6 %local_terms.7 = s16[32,72,128]{2,1,0:T(8,128)(2,1)} custom-call(s32[6,2,32]{2,1,0:T(2,128)} %bitcast.56, bf16[6,32,64,128]{3,2,1,0:T(8,128)(2,1)} %bitcast.50, bf16[16,64,128]{2,1,0:T(8,128)(2,1)S(1)} %bitcast.37), custom_call_target="tpu_custom_call" | custom-call | tf_op jit(solution)/shard_map/local_terms/pallas_call | solution.py:75
  56.8 0.0 all-to-all-done.arrived_ref
  56.8 9.5 %all-to-all-start.1 = ((s16[32,72,128]{2,1,0:T(8,128)(2,1)}), s16[32,72,128]{2,1,0:T(8,128)(2,1)S(1)}, u32[]{:S(2)}, u32[]{:S(2)}) async-start(s16[32,72,128]{2,1,0:T(8,128)(2,1)} %local_terms.7), calls=%async_computation.1 | async-start | bytes 1179648 | tf_op jit(solution)/shard_map/all_to_all | solution.py:203
  66.3 0.3 solve_middle.5
  66.7 16.3 %all-gather.2 = bf16[1024,128]{1,0:T(8,128)(2,1)S(1)} all-gather(bf16[64,128]{1,0:T(8,128)(2,1)S(1)} %get-tuple-element.29), channel_id=4, replica_groups=mesh['row'=16,'col'=32] {'row'}, dimensions={0}, use_global_device_ids=true | all-gather | bytes 278528 | tf_op jit(solution)/shard_map/all_gather | solution.py:192
  83.0 4.0 %local_terms.8 = s16[32,72,128]{2,1,0:T(8,128)(2,1)} custom-call(s32[6,2,32]{2,1,0:T(2,128)} %bitcast.57, bf16[6,32,64,128]{3,2,1,0:T(8,128)(2,1)} %bitcast.51, bf16[16,64,128]{2,1,0:T(8,128)(2,1)S(1)} %bitcast.41, bf16[16,64,128]{2,1,0:T(8,128)(2,1)S(1)} %bitcast.45), custom_call_target="tpu_custom_call" | custom-call | tf_op jit(solution)/shard_map/local_terms/pallas_call | solution.py:75
  87.0 0.0 all-to-all-done.1.arrived_ref
  87.0 9.5 %all-to-all-start.2 = ((s16[32,72,128]{2,1,0:T(8,128)(2,1)}), s16[32,72,128]{2,1,0:T(8,128)(2,1)S(1)}, u32[]{:S(2)}, u32[]{:S(2)}) async-start(s16[32,72,128]{2,1,0:T(8,128)(2,1)} %local_terms.8), calls=%async_computation.2 | async-start | bytes 1179648 | tf_op jit(solution)/shard_map/all_to_all | solution.py:203
  96.5 0.3 solve_middle.6
  96.8 15.9 %all-gather.3 = bf16[1024,128]{1,0:T(8,128)(2,1)S(1)} all-gather(bf16[64,128]{1,0:T(8,128)(2,1)S(1)} %get-tuple-element.32), channel_id=5, replica_groups=mesh['row'=16,'col'=32] {'row'}, dimensions={0}, use_global_device_ids=true | all-gather | bytes 278528 | tf_op jit(solution)/shard_map/all_gather | solution.py:192
  112.8 3.9 %local_terms.9 = s16[32,72,128]{2,1,0:T(8,128)(2,1)} custom-call(s32[6,2,32]{2,1,0:T(2,128)} %bitcast.58, bf16[6,32,64,128]{3,2,1,0:T(8,128)(2,1)} %bitcast.52, bf16[16,64,128]{2,1,0:T(8,128)(2,1)S(1)} %bitcast.38, bf16[16,64,128]{2,1,0:T(8,128)(2,1)S(1)} %bitcast.43), custom_call_target="tpu_custom_call" | custom-call | tf_op jit(solution)/shard_map/local_terms/pallas_call | solution.py:75
  116.7 0.0 all-to-all-done.2.arrived_ref
  116.7 9.5 %all-to-all-start.3 = ((s16[32,72,128]{2,1,0:T(8,128)(2,1)}), s16[32,72,128]{2,1,0:T(8,128)(2,1)S(1)}, u32[]{:S(2)}, u32[]{:S(2)}) async-start(s16[32,72,128]{2,1,0:T(8,128)(2,1)} %local_terms.9), calls=%async_computation.3 | async-start | bytes 1179648 | tf_op jit(solution)/shard_map/all_to_all | solution.py:203
  126.3 0.3 solve_middle.7
  126.6 16.3 %all-gather.4 = bf16[1024,128]{1,0:T(8,128)(2,1)S(1)} all-gather(bf16[64,128]{1,0:T(8,128)(2,1)S(1)} %get-tuple-element.35), channel_id=6, replica_groups=mesh['row'=16,'col'=32] {'row'}, dimensions={0}, use_global_device_ids=true | all-gather | bytes 278528 | tf_op jit(solution)/shard_map/all_gather | solution.py:192
  142.9 4.2 %local_terms.10 = s16[32,72,128]{2,1,0:T(8,128)(2,1)} custom-call(s32[6,2,32]{2,1,0:T(2,128)} %bitcast.59, bf16[6,32,64,128]{3,2,1,0:T(8,128)(2,1)} %bitcast.53, bf16[16,64,128]{2,1,0:T(8,128)(2,1)S(1)} %bitcast.42, bf16[16,64,128]{2,1,0:T(8,128)(2,1)S(1)} %bitcast.46, bf16[16,64,128]{2,1,0:T(8,128)(2,1)S(1)} %bitcast.47), custom_call_target="tpu_custom_call" | custom-call | tf_op jit(solution)/shard_map/local_terms/pallas_call | solution.py:75
  147.1 9.5 %all-to-all-start.4 = ((s16[32,72,128]{2,1,0:T(8,128)(2,1)}), s16[32,72,128]{2,1,0:T(8,128)(2,1)S(1)}, u32[]{:S(2)}, u32[]{:S(2)}) async-start(s16[32,72,128]{2,1,0:T(8,128)(2,1)} %local_terms.10), calls=%async_computation.4 | async-start | bytes 1179648 | tf_op jit(solution)/shard_map/all_to_all | solution.py:203
  156.6 0.3 solve_middle.8
  157.0 15.9 %all-gather.5 = bf16[1024,128]{1,0:T(8,128)(2,1)S(1)} all-gather(bf16[64,128]{1,0:T(8,128)(2,1)S(1)} %get-tuple-element.38), channel_id=7, replica_groups=mesh['row'=16,'col'=32] {'row'}, dimensions={0}, use_global_device_ids=true | all-gather | bytes 278528 | tf_op jit(solution)/shard_map/all_gather | solution.py:192
  172.9 4.2 %local_terms.11 = s16[32,72,128]{2,1,0:T(8,128)(2,1)} custom-call(s32[6,2,32]{2,1,0:T(2,128)} %bitcast.60, bf16[6,32,64,128]{3,2,1,0:T(8,128)(2,1)} %bitcast.54, bf16[16,64,128]{2,1,0:T(8,128)(2,1)S(1)} %bitcast.39, bf16[16,64,128]{2,1,0:T(8,128)(2,1)S(1)} %bitcast.44, bf16[16,64,128]{2,1,0:T(8,128)(2,1)S(1)} %bitcast.48), custom_call_target="tpu_custom_call" | custom-call | tf_op jit(solution)/shard_map/local_terms/pallas_call | solution.py:75
  177.1 0.0 all-to-all-done.4.arrived_ref
  177.1 9.5 %all-to-all-start.5 = ((s16[32,72,128]{2,1,0:T(8,128)(2,1)}), s16[32,72,128]{2,1,0:T(8,128)(2,1)S(1)}, u32[]{:S(2)}, u32[]{:S(2)}) async-start(s16[32,72,128]{2,1,0:T(8,128)(2,1)} %local_terms.11), calls=%async_computation.5 | async-start | bytes 1179648 | tf_op jit(solution)/shard_map/all_to_all | solution.py:203
  186.6 0.9 solve_middle.9
  187.6 14.9 %all-to-all-done.5.arrived_ref = s16[32,72,128]{2,1,0:T(8,128)(2,1)S(1)} async-done(((s16[32,72,128]{2,1,0:T(8,128)(2,1)}), s16[32,72,128]{2,1,0:T(8,128)(2,1)S(1)}, u32[]{:S(2)}, u32[]{:S(2)}) %all-to-all-start.5) | async-done | bytes 589856 | tf_op jit(solution)/shard_map/all_to_all | solution.py:203
  202.5 1.0 solve_last.1
  (4 shorter events, 0.0 us)
Async XLA Ops:
  26.2 40.2 %copy-start = (bf16[4,1,1,64,256]{4,3,2,1,0:T(8,128)(2,1)S(1)}, bf16[4,1,1,64,256]{4,3,2,1,0:T(8,128)(2,1)}, u32[]{:S(2)}) copy-start(bf16[4,1,1,64,256]{4,3,2,1,0:T(8,128)(2,1)} %param.4) | copy-start | bytes 393220
  26.2 40.2 %copy-start.1 = (f32[4,1,1,64,64]{4,3,2,1,0:T(8,128)S(1)}, f32[4,1,1,64,64]{4,3,2,1,0:T(8,128)}, u32[]{:S(2)}) copy-start(f32[4,1,1,64,64]{4,3,2,1,0:T(8,128)} %param.5) | copy-start | bytes 196612
  26.2 30.6 %all-to-all-start = ((s16[32,72,128]{2,1,0:T(8,128)(2,1)}), s16[32,72,128]{2,1,0:T(8,128)(2,1)S(1)}, u32[]{:S(2)}, u32[]{:S(2)}) async-start(s16[32,72,128]{2,1,0:T(8,128)(2,1)} %local_terms.6), calls=%async_computation | async-start | bytes 1179648 | tf_op jit(solution)/shard_map/all_to_all | solution.py:203
  56.8 30.2 %all-to-all-start.1 = ((s16[32,72,128]{2,1,0:T(8,128)(2,1)}), s16[32,72,128]{2,1,0:T(8,128)(2,1)S(1)}, u32[]{:S(2)}, u32[]{:S(2)}) async-start(s16[32,72,128]{2,1,0:T(8,128)(2,1)} %local_terms.7), calls=%async_computation.1 | async-start | bytes 1179648 | tf_op jit(solution)/shard_map/all_to_all | solution.py:203
  87.0 29.7 %all-to-all-start.2 = ((s16[32,72,128]{2,1,0:T(8,128)(2,1)}), s16[32,72,128]{2,1,0:T(8,128)(2,1)S(1)}, u32[]{:S(2)}, u32[]{:S(2)}) async-start(s16[32,72,128]{2,1,0:T(8,128)(2,1)} %local_terms.8), calls=%async_computation.2 | async-start | bytes 1179648 | tf_op jit(solution)/shard_map/all_to_all | solution.py:203
  116.7 30.4 %all-to-all-start.3 = ((s16[32,72,128]{2,1,0:T(8,128)(2,1)}), s16[32,72,128]{2,1,0:T(8,128)(2,1)S(1)}, u32[]{:S(2)}, u32[]{:S(2)}) async-start(s16[32,72,128]{2,1,0:T(8,128)(2,1)} %local_terms.9), calls=%async_computation.3 | async-start | bytes 1179648 | tf_op jit(solution)/shard_map/all_to_all | solution.py:203
  147.1 30.0 %all-to-all-start.4 = ((s16[32,72,128]{2,1,0:T(8,128)(2,1)}), s16[32,72,128]{2,1,0:T(8,128)(2,1)S(1)}, u32[]{:S(2)}, u32[]{:S(2)}) async-start(s16[32,72,128]{2,1,0:T(8,128)(2,1)} %local_terms.10), calls=%async_computation.4 | async-start | bytes 1179648 | tf_op jit(solution)/shard_map/all_to_all | solution.py:203
  177.1 25.4 %all-to-all-start.5 = ((s16[32,72,128]{2,1,0:T(8,128)(2,1)}), s16[32,72,128]{2,1,0:T(8,128)(2,1)S(1)}, u32[]{:S(2)}, u32[]{:S(2)}) async-start(s16[32,72,128]{2,1,0:T(8,128)(2,1)} %local_terms.11), calls=%async_computation.5 | async-start | bytes 1179648 | tf_op jit(solution)/shard_map/all_to_all | solution.py:203

commit v5 on v1

v5 whole, which is shorter than its diff:
```python
import functools

import jax
import jax.numpy as jnp
from jax import lax
from jax.experimental import pallas as pl
from jax.experimental.pallas import tpu as pltpu
from jax.sharding import Mesh, PartitionSpec as P

LANES = 128
PAD = 8
SIDES = 2
KERNEL_VMEM = 12 << 20
CHUNKS = 4
VMEM = pl.BlockSpec(memory_space=pltpu.VMEM)
SMEM = pl.BlockSpec(memory_space=pltpu.SMEM)
ANY = pl.BlockSpec(memory_space=pl.ANY)
PARAMS = pltpu.CompilerParams(vmem_limit_bytes=KERNEL_VMEM)


def in_vmem(array):
    return pltpu.with_memory_space_constraint(array, pltpu.VMEM)


def in_hbm(array):
    return pltpu.with_memory_space_constraint(array, pltpu.HBM)


def encode(parts, out_ref, index):
    powers = []
    for side, part in enumerate(parts):
        rows = part.shape[0]
        largest = jnp.max(jnp.abs(part), axis=0, keepdims=True)
        power = jnp.ceil(jnp.log2(jnp.maximum(largest * 1.001, 1e-30)))
        coded = jnp.floor(part * jnp.exp2(15.0 - power) + 0.5).astype(jnp.int32)
        out_ref[index, side * rows : (side + 1) * rows, :] = coded.astype(jnp.int16)
        powers.append(jnp.broadcast_to(power, (PAD // len(parts), LANES)))
    powers = jnp.concatenate(powers, axis=0).astype(jnp.int32)
    out_ref[index, len(parts) * rows : len(parts) * rows + PAD, :] = powers.astype(jnp.int16)


def decode(block):
    rows = (block.shape[0] - PAD) // SIDES
    powers = block[SIDES * rows :, :].astype(jnp.int32).astype(jnp.float32)
    scales = jnp.exp2(powers - 15.0)
    parts = []
    for side in range(SIDES):
        coded = block[side * rows : (side + 1) * rows, :].astype(jnp.int32).astype(jnp.float32)
        first = side * (PAD // SIDES)
        parts.append(coded * scales[first : first + 1, :])
    return parts


def add_peers(peers, load):
    total = None
    for peer in range(peers):
        parts = decode(load(peer))
        total = parts if total is None else [a + b for a, b in zip(total, parts)]
    return total


def first_kernel(rhs_ref, dinv_ref, solution_ref, payload_ref):
    solution = jnp.dot(
        dinv_ref[0],
        rhs_ref[0].astype(jnp.float32),
        precision=lax.Precision.HIGHEST,
        preferred_element_type=jnp.float32,
    )
    solution_ref[...] = solution
    for half in range(SIDES):
        columns = slice(half * LANES, (half + 1) * LANES)
        payload_ref[half, 0] = solution[:, columns].astype(jnp.bfloat16)
        for level in range(1, rhs_ref.shape[0]):
            payload_ref[half, level] = rhs_ref[level, :, columns]


def spread_kernel(swapped_ref, copies_ref):
    core = lax.axis_index("core")
    for side, row in enumerate((core, 1 - core)):
        block = swapped_ref[row, 0]
        for peer in range(copies_ref.shape[0]):
            copies_ref[peer, side] = block


def terms_kernel(pairs, *refs):
    sources, lowers, gathered = refs[:SIDES], refs[SIDES : 2 * SIDES], refs[2 * SIDES : -3]
    out_ref, factors_ref, sems = refs[-3:]
    core = lax.axis_index("core")
    _, targets, block_rows, depth = lowers[0].shape
    per = depth // block_rows
    chunk = targets // CHUNKS
    copies = [
        [
            pltpu.make_async_copy(
                lowers[side].at[pair, pl.ds(step * chunk, chunk)],
                factors_ref.at[side, place, pl.ds(step * chunk, chunk)],
                sems.at[step, side, place],
            )
            for side in range(SIDES)
            for place, pair in enumerate(pairs)
        ]
        for step in range(CHUNKS)
    ]
    for step in range(CHUNKS):
        for copy in copies[step]:
            copy.start()

    def one(target, carry):
        parts = []
        for side in range(SIDES):
            factors, picked = [], []
            for place, (block, pair) in enumerate(zip(gathered, pairs)):
                factors.append(factors_ref[side, place, target])
                for entry in range(per):
                    source = sources[side][pair, entry, target]
                    rows = block[jnp.bitwise_xor(jnp.maximum(source, 0), core)]
                    picked.append(jnp.where(source >= 0, rows, jnp.zeros_like(rows)))
            parts.append(
                jnp.dot(
                    jnp.concatenate(factors, axis=1),
                    jnp.concatenate(picked, axis=0),
                    preferred_element_type=jnp.float32,
                )
            )
        encode(parts, out_ref, target)
        return carry

    for step in range(CHUNKS):
        for copy in copies[step]:
            copy.wait()
        lax.fori_loop(step * chunk, (step + 1) * chunk, one, 0, unroll=True)


def middle_kernel(arrived_ref, out_ref):
    peers, targets = arrived_ref.shape[:2]
    for target in range(targets):
        encode(add_peers(peers, lambda peer: arrived_ref[peer, target]), out_ref, target)


def solve_parts(level, swapped_ref, dinv_refs, arrived_ref):
    core = lax.axis_index("core")
    total = add_peers(arrived_ref.shape[0], lambda peer: arrived_ref[peer])
    parts = []
    for row, dinv_ref, part in zip((core, 1 - core), dinv_refs, total):
        residual = swapped_ref[row, level].astype(jnp.float32) - part
        parts.append(
            jnp.dot(
                dinv_ref[level],
                residual,
                precision=lax.Precision.HIGHEST,
                preferred_element_type=jnp.float32,
            )
        )
    return parts


def solve_kernel(level, swapped_ref, own_ref, other_ref, arrived_ref, solution_ref, copies_ref):
    parts = solve_parts(level, swapped_ref, (own_ref, other_ref), arrived_ref)
    for side, part in enumerate(parts):
        solution_ref[side] = part
        for peer in range(copies_ref.shape[0]):
            copies_ref[peer, side] = part.astype(jnp.bfloat16)


def last_kernel(swapped_ref, own_ref, other_ref, arrived_ref, *refs):
    earlier, out_ref = refs[:-1], refs[-1]
    core = lax.axis_index("core")
    for place, ref in enumerate(earlier):
        out_ref[core, place] = ref[0]
        out_ref[1 - core, place] = ref[1]
    level = len(earlier) + 1
    parts = solve_parts(level, swapped_ref, (own_ref, other_ref), arrived_ref)
    out_ref[core, level - 1] = parts[0]
    out_ref[1 - core, level - 1] = parts[1]


def join_kernel(first_ref, halves_ref, out_ref, sems):
    copies = [pltpu.make_async_copy(first_ref, out_ref.at[0], sems.at[0])]
    for half in range(SIDES):
        target = out_ref.at[pl.ds(1, halves_ref.shape[1]), :, pl.ds(half * LANES, LANES)]
        copies.append(pltpu.make_async_copy(halves_ref.at[half], target, sems.at[1 + half]))
    for copy in copies:
        copy.start()
    for copy in copies:
        copy.wait()


def on_device(rhs, dinv, lower, sources):
    levels, _, _, block_rows, width = rhs.shape
    x_size, y_size, z_size = (lax.axis_size(name) for name in ("x", "y", "z"))
    pair_of = {}
    for section in range(levels):
        for target in range(section + 1, levels):
            pair_of[section, target] = len(pair_of)
    rhs, dinv, lower = rhs[:, 0, 0], dinv[:, 0, 0], lower[:, 0, 0]
    sources = jnp.swapaxes(sources[:, 0, 0], 1, 2)
    targets, depth = lower.shape[1], lower.shape[3]
    coded_rows = SIDES * block_rows + PAD
    copies_shape = pltpu.VMEM((y_size, SIDES, block_rows, LANES), jnp.bfloat16)

    first, payload = pl.pallas_call(
        first_kernel,
        out_shape=(
            pltpu.VMEM((block_rows, width), jnp.float32),
            pltpu.VMEM((SIDES, levels, block_rows, LANES), jnp.bfloat16),
        ),
        in_specs=[VMEM] * 2,
        out_specs=(VMEM, VMEM),
        compiler_params=PARAMS,
        name="first",
    )(rhs, dinv)
    swapped = lax.all_to_all(payload, "core", split_axis=0, concat_axis=0, tiled=True)
    copies = pl.pallas_call(
        spread_kernel,
        out_shape=copies_shape,
        in_specs=[VMEM],
        out_specs=VMEM,
        compiler_params=PARAMS,
        name="spread",
    )(in_vmem(swapped))

    swap = [(0, 1), (1, 0)]
    copies, lower_sent, dinv_sent, sources_sent = lax.optimization_barrier(
        (copies, lower, dinv, sources)
    )
    lowers = (lower, lax.ppermute(lower_sent, "core", swap))
    dinvs = (dinv, lax.ppermute(dinv_sent, "core", swap))
    tables = (sources, lax.ppermute(sources_sent, "core", swap))

    gathered, solutions = [], []
    for level in range(1, levels):
        blocks = lax.all_to_all(copies, "y", split_axis=0, concat_axis=0, tiled=True)
        gathered.append(in_vmem(blocks.reshape(y_size * SIDES, block_rows, LANES)))
        pairs = tuple(pair_of[earlier, level] for earlier in range(level))
        coded = pl.pallas_call(
            functools.partial(terms_kernel, pairs),
            out_shape=pltpu.VMEM((targets, coded_rows, LANES), jnp.int16),
            in_specs=[SMEM] * SIDES + [ANY] * SIDES + [VMEM] * len(gathered),
            out_specs=VMEM,
            scratch_shapes=[
                pltpu.VMEM((SIDES, len(pairs), targets, block_rows, depth), lower.dtype),
                pltpu.SemaphoreType.DMA((CHUNKS, SIDES, len(pairs))),
            ],
            compiler_params=PARAMS,
            name="local_terms",
        )(*map(in_hbm, tables), *map(in_hbm, lowers), *gathered)
        coded = coded.reshape(x_size, z_size, coded_rows, LANES)
        arrived = lax.all_to_all(coded, "x", split_axis=0, concat_axis=0, tiled=True)
        coded = pl.pallas_call(
            middle_kernel,
            out_shape=pltpu.VMEM((z_size, coded_rows, LANES), jnp.int16),
            in_specs=[VMEM],
            out_specs=VMEM,
            compiler_params=PARAMS,
            name="sum_x",
        )(in_vmem(arrived))
        arrived = lax.all_to_all(coded, "z", split_axis=0, concat_axis=0, tiled=True)
        operands = [in_vmem(array) for array in (swapped, *dinvs, arrived)]
        if level + 1 < levels:
            solution, copies = pl.pallas_call(
                functools.partial(solve_kernel, level),
                out_shape=(pltpu.VMEM((SIDES, block_rows, LANES), jnp.float32), copies_shape),
                in_specs=[VMEM] * 4,
                out_specs=(VMEM, VMEM),
                compiler_params=PARAMS,
                name="solve",
            )(*operands)
            solutions.append(solution)
        else:
            parts = pl.pallas_call(
                last_kernel,
                out_shape=pltpu.VMEM((SIDES, levels - 1, block_rows, LANES), jnp.float32),
                in_specs=[VMEM] * (4 + len(solutions)),
                out_specs=VMEM,
                compiler_params=PARAMS,
                name="solve_last",
            )(*operands, *map(in_vmem, solutions))
    halves = lax.all_to_all(parts, "core", split_axis=0, concat_axis=0, tiled=True)
    joined = pl.pallas_call(
        join_kernel,
        out_shape=jax.ShapeDtypeStruct((levels, block_rows, width), jnp.float32),
        in_specs=[VMEM] * 2,
        out_specs=ANY,
        scratch_shapes=[pltpu.SemaphoreType.DMA((1 + SIDES,))],
        compiler_params=PARAMS,
        name="join",
    )(in_vmem(first), in_vmem(halves))
    return joined[:, None, None]


def solution(mesh):
    split = Mesh(mesh.devices.reshape(8, 2, 4, 8), ("y", "core", "x", "z"))
    row, col = ("y", "core"), ("x", "z")
    in_specs = (
        P(None, row, col, None, None),
        P(None, row, col, None, None),
        P(None, row, col, None, None, None),
        P(None, row, col, None, None),
    )
    out_specs = P(None, row, col, None, None)
    return jax.shard_map(
        on_device, mesh=split, in_specs=in_specs, out_specs=out_specs, check_vma=False
    )
```

time: 184 us -> 174 us (0.946)
  blocking collectives: 93.7 us -> 117 us
  matrix products: 16.8 us -> 0 us
  Pallas kernels: 0 us -> 16.8 us
  waiting for transfers between devices: 32.5 us -> 15.7 us
  local copies, waits for them, and re-layouts: 12.6 us -> 1.82 us
  other arithmetic: 9.61 us -> 0 us
  starting transfers between devices: 15.9 us -> 21 us
    all_to_all x1 -> x9, blocking collectives: 29.9 us -> 117 us  [the longest x3 43.7 us: on_device(): lax.all_to_all(coded, 'x', split_axis=0, concat_axis=0, tiled=True)]
    all_gather x3 -> x0, blocking collectives: 63.8 us -> none  [on_device(): gathered.append(lax.all_gather(solved[None], 'row', axis=0, tiled=True))]
    all_to_all x2, waiting for transfers between devices: 32.5 us -> 13.7 us  [the longest x1 9.21 us: on_device(): lax.all_to_all(copies, 'y', split_axis=0, concat_axis=0, tiled=True)]
    pallas_call x0 -> x12, Pallas kernels: none -> 16.8 us  [the longest x3 12.3 us: on_device(): pl.pallas_call(functools.partial(terms_kernel, pairs), out_shape=pltpu.VM...]
    dot_general x10 -> x0, matrix products: 16.8 us -> none  [the longest x6 15.3 us: level_terms(): jnp.einsum('qik,qkn->qin', blocks, picked, preferred_element_type=jnp.flo...]
    ppermute x0 -> x3, starting transfers between devices: none -> 8.24 us  [the longest x1 3.92 us: on_device(): dinvs = (dinv, lax.ppermute(dinv_sent, 'core', swap))]
    gather x6 -> x0, local copies, waits for them, and re-layouts: 4.08 us -> none  [level_terms(): picked = jnp.take(gathered, clipped, axis=0)]
    all_to_all x2, starting transfers between devices: 15.9 us -> 12.7 us  [the longest x1 9.31 us: on_device(): lax.all_to_all(coded, 'z', split_axis=0, concat_axis=0, tiled=True)]
  transfers between devices with their start and end apart: 2 -> 5, of which waited for: 2 -> 4; matrix products, arithmetic and copies ran while one was open for 10% -> 0% of each run, Pallas kernels for 0% -> 0%
where the time goes in v5:
time: 174 us; the launch traced here: 173 us
  blocking collectives  117 us (67%)
  starting transfers between devices  21 us (12%)
  Pallas kernels  16.8 us (10%)
  waiting for transfers between devices  15.7 us (9%)
  local copies, waits for them, and re-layouts  1.82 us (1%)
    all_to_all x3, blocking collectives, on_device(): lax.all_to_all(coded, 'x', split_axis=0, concat_axis=0, tiled=True)  43.7 us
    all_to_all x2, blocking collectives, on_device(): lax.all_to_all(coded, 'z', split_axis=0, concat_axis=0, tiled=True)  26.2 us
    all_to_all x2, blocking collectives, on_device(): lax.all_to_all(copies, 'y', split_axis=0, concat_axis=0, tiled=True)  26 us
    pallas_call x3, Pallas kernels, on_device(): pl.pallas_call(functools.partial(terms_kernel, pairs), out_shape=pltpu.VM...  12.3 us
    all_to_all x1, blocking collectives, on_device(): lax.all_to_all(parts, 'core', split_axis=0, concat_axis=0, tiled=True)  11 us
    all_to_all x1, blocking collectives, on_device(): lax.all_to_all(payload, 'core', split_axis=0, concat_axis=0, tiled=True)  10.4 us
    all_to_all x1, starting transfers between devices, on_device(): lax.all_to_all(coded, 'z', split_axis=0, concat_axis=0, tiled=True)  9.31 us
    all_to_all x1, waiting for transfers between devices, on_device(): lax.all_to_all(copies, 'y', split_axis=0, concat_axis=0, tiled=True)  9.21 us
  transfers between devices with their start and end apart: 5, of which 4 were waited for; matrix products, arithmetic and copies ran while one was open for 0% of the time, Pallas kernels for 0%

profile of v5, /device:TPU:1, one launch (start us, length us, event | category | flops | bytes accessed | tf_op | source)
XLA Modules:
  0.0 172.8 jit_solution(4706653359431438052)
XLA Ops:
  0.0 0.9 copy-done
  0.9 0.9 copy-done.2
  1.8 0.2 first.1
  2.0 10.4 %all_to_all.55.swapped_ref = bf16[2,4,64,128]{3,2,1,0:T(8,128)(2,1)S(1)} all-to-all(bf16[2,4,64,128]{3,2,1,0:T(8,128)(2,1)S(1)} %get-tuple-element.16), channel_id=1, replica_groups=mesh['y'=8,'core'=2,'x'=4,'z'=8] {'core'}, dimensions={0} | all-to-all | bytes 262144 | tf_op jit(solution)/shard_map/all_to_all | solution.py:212
  12.4 0.7 spread.1
  13.1 2.3 %collective-permute-start.2 = (bf16[6,32,64,128]{3,2,1,0:T(8,128)(2,1)}, bf16[6,32,64,128]{3,2,1,0:T(8,128)(2,1)}, u32[]{:S(2)}, u32[]{:S(2)}) collective-permute-start(bf16[6,32,64,128]{3,2,1,0:T(8,128)(2,1)} %bitcast.30), channel_id=1, source_target_pairs={{0,32},{32,0},{1,33},{33,1},{2,34},{34,2},{3,35},{35,3},{4,36},{36... | collective-permute-start | bytes 9437192 | tf_op jit(solution)/shard_map/ppermute | solution.py:226
  15.4 3.4 %all-to-all-start.1 = ((bf16[8,2,64,128]{3,2,1,0:T(8,128)(2,1)}), bf16[8,2,64,128]{3,2,1,0:T(8,128)(2,1)S(1)}, u32[]{:S(2)}, u32[]{:S(2)}) async-start(bf16[8,2,64,128]{3,2,1,0:T(8,128)(2,1)} %spread.1), calls=%async_computation.1 | async-start | bytes 524288 | tf_op jit(solution)/shard_map/all_to_all | solution.py:232
  18.8 2.1 %collective-permute-start.1 = (s32[6,2,32]{2,1,0:T(2,128)S(1)}, s32[6,2,32]{2,1,0:T(2,128)S(1)}, u32[]{:S(2)}, u32[]{:S(2)}) collective-permute-start(s32[6,2,32]{2,1,0:T(2,128)S(1)} %bitcast.37), channel_id=1, source_target_pairs={{0,32},{32,0},{1,33},{33,1},{2,34},{34,2},{3,35},{35,3},{4,36},{36... | collective-permute-start | bytes 4616 | tf_op jit(solution)/shard_map/ppermute | solution.py:228
  20.9 1.0 collective-permute-done.1.refs_1_
  21.9 9.2 %all-to-all-done.1 = bf16[8,2,64,128]{3,2,1,0:T(8,128)(2,1)S(1)} async-done(((bf16[8,2,64,128]{3,2,1,0:T(8,128)(2,1)}), bf16[8,2,64,128]{3,2,1,0:T(8,128)(2,1)S(1)}, u32[]{:S(2)}, u32[]{:S(2)}) %all-to-all-start.1) | async-done | bytes 262176 | tf_op jit(solution)/shard_map/all_to_all | solution.py:232
  31.1 3.3 %local_terms.3 = s16[32,136,128]{2,1,0:T(8,128)(2,1)S(1)} custom-call(s32[6,2,32]{2,1,0:T(2,128)} %bitcast.34, s32[6,2,32]{2,1,0:T(2,128)} %copy-done.4, bf16[6,32,64,128]{3,2,1,0:T(8,128)(2,1)} %bitcast.31, bf16[6,32,64,128]{3,2,1,0:T(8,128)(2,1)} %collective-permute-done.2.refs_3_, bf16[16,64,128]{2,1,0:T(8,128)(2,1)S(1)} %bitcast.18), custom_call_target="tpu_custom_call" | custom-call | tf_op jit(solution)/shard_map/local_terms/pallas_call | solution.py:235
  34.4 17.6 %all_to_all.56.arrived_ref = s16[4,8,136,128]{3,2,1,0:T(8,128)(2,1)S(1)} all-to-all(s16[4,8,136,128]{3,2,1,0:T(8,128)(2,1)S(1)} %bitcast.16), channel_id=1, replica_groups=mesh['y'=8,'core'=2,'x'=4,'z'=8] {'x'}, dimensions={0} | all-to-all | bytes 2228224 | tf_op jit(solution)/shard_map/all_to_all | solution.py:248
  52.0 1.2 sum_x.3
  53.1 9.3 %all-to-all-start.3 = ((s16[8,136,128]{2,1,0:T(8,128)(2,1)}), s16[8,136,128]{2,1,0:T(8,128)(2,1)S(1)}, u32[]{:S(2)}, u32[]{:S(2)}) async-start(s16[8,136,128]{2,1,0:T(8,128)(2,1)} %sum_x.3), calls=%async_computation.3 | async-start | bytes 557056 | tf_op jit(solution)/shard_map/all_to_all | solution.py:257
  62.5 3.9 %collective-permute-start = (f32[4,64,64]{2,1,0:T(8,128)S(1)}, f32[4,64,64]{2,1,0:T(8,128)S(1)}, u32[]{:S(2)}, u32[]{:S(2)}) collective-permute-start(f32[4,64,64]{2,1,0:T(8,128)S(1)} %bitcast.24), channel_id=1, source_target_pairs={{0,32},{32,0},{1,33},{33,1},{2,34},{34,2},{3,35},{35,3},{4,36},{36... | collective-permute-start | bytes 196616 | tf_op jit(solution)/shard_map/ppermute | solution.py:227
  66.4 1.0 collective-permute-done.other_ref
  67.3 4.5 %all-to-all-done.3.arrived_ref = s16[8,136,128]{2,1,0:T(8,128)(2,1)S(1)} async-done(((s16[8,136,128]{2,1,0:T(8,128)(2,1)}), s16[8,136,128]{2,1,0:T(8,128)(2,1)S(1)}, u32[]{:S(2)}, u32[]{:S(2)}) %all-to-all-start.3) | async-done | bytes 278560 | tf_op jit(solution)/shard_map/all_to_all | solution.py:257
  71.9 0.3 solve.2
  72.2 11.9 %all_to_all.57 = bf16[8,2,64,128]{3,2,1,0:T(8,128)(2,1)S(1)} all-to-all(bf16[8,2,64,128]{3,2,1,0:T(8,128)(2,1)S(1)} %get-tuple-element.21), channel_id=1, replica_groups=mesh['y'=8,'core'=2,'x'=4,'z'=8] {'y'}, dimensions={0} | all-to-all | bytes 524288 | tf_op jit(solution)/shard_map/all_to_all | solution.py:232
  84.1 4.1 %local_terms.4 = s16[32,136,128]{2,1,0:T(8,128)(2,1)S(1)} custom-call(s32[6,2,32]{2,1,0:T(2,128)} %bitcast.35, s32[6,2,32]{2,1,0:T(2,128)} %copy-done.4, bf16[6,32,64,128]{3,2,1,0:T(8,128)(2,1)} %bitcast.32, bf16[6,32,64,128]{3,2,1,0:T(8,128)(2,1)} %collective-permute-done.2.refs_3_, bf16[16,64,128]{2,1,0:T(8,128)(2,1)S(1)} %bitcast.19, ...), custom_call_target="tpu_custom_call" | custom-call | tf_op jit(solution)/shard_map/local_terms/pallas_call | solution.py:235
  88.2 13.5 %all_to_all.58.arrived_ref = s16[4,8,136,128]{3,2,1,0:T(8,128)(2,1)S(1)} all-to-all(s16[4,8,136,128]{3,2,1,0:T(8,128)(2,1)S(1)} %bitcast.17), channel_id=1, replica_groups=mesh['y'=8,'core'=2,'x'=4,'z'=8] {'x'}, dimensions={0} | all-to-all | bytes 2228224 | tf_op jit(solution)/shard_map/all_to_all | solution.py:248
  101.7 0.4 sum_x.4
  102.1 14.1 %all_to_all.59.arrived_ref = s16[8,136,128]{2,1,0:T(8,128)(2,1)S(1)} all-to-all(s16[8,136,128]{2,1,0:T(8,128)(2,1)S(1)} %sum_x.4), channel_id=1, replica_groups=mesh['y'=8,'core'=2,'x'=4,'z'=8] {'z'}, dimensions={0} | all-to-all | bytes 557056 | tf_op jit(solution)/shard_map/all_to_all | solution.py:257
  116.3 0.3 solve.3
  116.6 14.1 %all_to_all.60 = bf16[8,2,64,128]{3,2,1,0:T(8,128)(2,1)S(1)} all-to-all(bf16[8,2,64,128]{3,2,1,0:T(8,128)(2,1)S(1)} %get-tuple-element.22), channel_id=1, replica_groups=mesh['y'=8,'core'=2,'x'=4,'z'=8] {'y'}, dimensions={0} | all-to-all | bytes 524288 | tf_op jit(solution)/shard_map/all_to_all | solution.py:232
  130.7 4.9 %local_terms.5 = s16[32,136,128]{2,1,0:T(8,128)(2,1)S(1)} custom-call(s32[6,2,32]{2,1,0:T(2,128)} %bitcast.36, s32[6,2,32]{2,1,0:T(2,128)} %copy-done.4, bf16[6,32,64,128]{3,2,1,0:T(8,128)(2,1)} %bitcast.33, bf16[6,32,64,128]{3,2,1,0:T(8,128)(2,1)} %collective-permute-done.2.refs_3_, bf16[16,64,128]{2,1,0:T(8,128)(2,1)S(1)} %bitcast.20, ...), custom_call_target="tpu_custom_call" | custom-call | tf_op jit(solution)/shard_map/local_terms/pallas_call | solution.py:235
  135.6 12.7 %all_to_all.61.arrived_ref = s16[4,8,136,128]{3,2,1,0:T(8,128)(2,1)S(1)} all-to-all(s16[4,8,136,128]{3,2,1,0:T(8,128)(2,1)S(1)} %bitcast.15), channel_id=1, replica_groups=mesh['y'=8,'core'=2,'x'=4,'z'=8] {'x'}, dimensions={0} | all-to-all | bytes 2228224 | tf_op jit(solution)/shard_map/all_to_all | solution.py:248
  148.2 0.4 sum_x.5
  148.7 12.0 %all_to_all.62.arrived_ref = s16[8,136,128]{2,1,0:T(8,128)(2,1)S(1)} all-to-all(s16[8,136,128]{2,1,0:T(8,128)(2,1)S(1)} %sum_x.5), channel_id=1, replica_groups=mesh['y'=8,'core'=2,'x'=4,'z'=8] {'z'}, dimensions={0} | all-to-all | bytes 557056 | tf_op jit(solution)/shard_map/all_to_all | solution.py:257
  160.7 0.3 solve_last.1
  161.0 11.0 %all_to_all.63.halves_ref = f32[2,3,64,128]{3,2,1,0:T(8,128)S(1)} all-to-all(f32[2,3,64,128]{3,2,1,0:T(8,128)S(1)} %solve_last.1), channel_id=1, replica_groups=mesh['y'=8,'core'=2,'x'=4,'z'=8] {'core'}, dimensions={0} | all-to-all | bytes 393216 | tf_op jit(solution)/shard_map/all_to_all | solution.py:278
  172.0 0.7 join.1
  (9 shorter events, 0.0 us)
Async XLA Ops:
  0.0 0.9 copy-start
  0.9 0.9 copy-start.2
  1.8 17.0 %copy-start.3 = (s32[6,1,1,32,2]{3,4,2,1,0:T(2,128)S(1)}, s32[6,1,1,32,2]{3,4,2,1,0:T(2,128)}, u32[]{:S(2)}) copy-start(s32[6,1,1,32,2]{3,4,2,1,0:T(2,128)} %param.7) | copy-start | bytes 4612
  13.1 18.0 %collective-permute-start.2 = (bf16[6,32,64,128]{3,2,1,0:T(8,128)(2,1)}, bf16[6,32,64,128]{3,2,1,0:T(8,128)(2,1)}, u32[]{:S(2)}, u32[]{:S(2)}) collective-permute-start(bf16[6,32,64,128]{3,2,1,0:T(8,128)(2,1)} %bitcast.30), channel_id=1, source_target_pairs={{0,32},{32,0},{1,33},{33,1},{2,34},{34,2},{3,35},{35,3},{4,36},{36... | collective-permute-start | bytes 9437192 | tf_op jit(solution)/shard_map/ppermute | solution.py:226
  15.4 15.7 %all-to-all-start.1 = ((bf16[8,2,64,128]{3,2,1,0:T(8,128)(2,1)}), bf16[8,2,64,128]{3,2,1,0:T(8,128)(2,1)S(1)}, u32[]{:S(2)}, u32[]{:S(2)}) async-start(bf16[8,2,64,128]{3,2,1,0:T(8,128)(2,1)} %spread.1), calls=%async_computation.1 | async-start | bytes 524288 | tf_op jit(solution)/shard_map/all_to_all | solution.py:232
  18.8 3.1 %collective-permute-start.1 = (s32[6,2,32]{2,1,0:T(2,128)S(1)}, s32[6,2,32]{2,1,0:T(2,128)S(1)}, u32[]{:S(2)}, u32[]{:S(2)}) collective-permute-start(s32[6,2,32]{2,1,0:T(2,128)S(1)} %bitcast.37), channel_id=1, source_target_pairs={{0,32},{32,0},{1,33},{33,1},{2,34},{34,2},{3,35},{35,3},{4,36},{36... | collective-permute-start | bytes 4616 | tf_op jit(solution)/shard_map/ppermute | solution.py:228
  21.9 9.2 %copy-start.4 = (s32[6,2,32]{2,1,0:T(2,128)}, s32[6,2,32]{2,1,0:T(2,128)S(1)}, u32[]{:S(2)}) copy-start(s32[6,2,32]{2,1,0:T(2,128)S(1)} %collective-permute-done.1.refs_1_) | copy-start | bytes 4612
  52.0 10.5 %copy-start.1 = (f32[4,1,1,64,64]{4,3,2,1,0:T(8,128)S(1)}, f32[4,1,1,64,64]{4,3,2,1,0:T(8,128)}, u32[]{:S(2)}) copy-start(f32[4,1,1,64,64]{4,3,2,1,0:T(8,128)} %param.5) | copy-start | bytes 196612
  53.1 18.7 %all-to-all-start.3 = ((s16[8,136,128]{2,1,0:T(8,128)(2,1)}), s16[8,136,128]{2,1,0:T(8,128)(2,1)S(1)}, u32[]{:S(2)}, u32[]{:S(2)}) async-start(s16[8,136,128]{2,1,0:T(8,128)(2,1)} %sum_x.3), calls=%async_computation.3 | async-start | bytes 557056 | tf_op jit(solution)/shard_map/all_to_all | solution.py:257
  62.5 4.9 %collective-permute-start = (f32[4,64,64]{2,1,0:T(8,128)S(1)}, f32[4,64,64]{2,1,0:T(8,128)S(1)}, u32[]{:S(2)}, u32[]{:S(2)}) collective-permute-start(f32[4,64,64]{2,1,0:T(8,128)S(1)} %bitcast.24), channel_id=1, source_target_pairs={{0,32},{32,0},{1,33},{33,1},{2,34},{34,2},{3,35},{35,3},{4,36},{36... | collective-permute-start | bytes 196616 | tf_op jit(solution)/shard_map/ppermute | solution.py:227

commit v6 on v5

v6 whole, which is shorter than its diff:
```python
import functools

import jax
import jax.numpy as jnp
from jax import lax
from jax.experimental import pallas as pl
from jax.experimental.pallas import tpu as pltpu
from jax.sharding import Mesh, PartitionSpec as P

LANES = 128
PAD = 8
SIDES = 2
KERNEL_VMEM = 12 << 20
VMEM = pl.BlockSpec(memory_space=pltpu.VMEM)
SMEM = pl.BlockSpec(memory_space=pltpu.SMEM)
ANY = pl.BlockSpec(memory_space=pl.ANY)
PARAMS = pltpu.CompilerParams(vmem_limit_bytes=KERNEL_VMEM)


def in_vmem(array):
    return pltpu.with_memory_space_constraint(array, pltpu.VMEM)


def in_hbm(array):
    return pltpu.with_memory_space_constraint(array, pltpu.HBM)


def encode(parts, out_ref, index):
    powers = []
    for side, part in enumerate(parts):
        rows = part.shape[0]
        largest = jnp.max(jnp.abs(part), axis=0, keepdims=True)
        power = jnp.ceil(jnp.log2(jnp.maximum(largest * 1.001, 1e-30)))
        coded = jnp.floor(part * jnp.exp2(15.0 - power) + 0.5).astype(jnp.int32)
        out_ref[index, side * rows : (side + 1) * rows, :] = coded.astype(jnp.int16)
        powers.append(jnp.broadcast_to(power, (PAD // len(parts), LANES)))
    powers = jnp.concatenate(powers, axis=0).astype(jnp.int32)
    out_ref[index, len(parts) * rows : len(parts) * rows + PAD, :] = powers.astype(jnp.int16)


def decode(block):
    rows = (block.shape[0] - PAD) // SIDES
    powers = block[SIDES * rows :, :].astype(jnp.int32).astype(jnp.float32)
    scales = jnp.exp2(powers - 15.0)
    parts = []
    for side in range(SIDES):
        coded = block[side * rows : (side + 1) * rows, :].astype(jnp.int32).astype(jnp.float32)
        first = side * (PAD // SIDES)
        parts.append(coded * scales[first : first + 1, :])
    return parts


def add_peers(peers, load):
    total = None
    for peer in range(peers):
        parts = decode(load(peer))
        total = parts if total is None else [a + b for a, b in zip(total, parts)]
    return total


def first_kernel(rhs_hbm, dinv_hbm, sources_ref, solution_ref, mine_ref, sent_ref, rhs_ref, dinv_ref, sems):
    copies = [
        pltpu.make_async_copy(rhs_hbm, rhs_ref, sems.at[0]),
        pltpu.make_async_copy(dinv_hbm, dinv_ref, sems.at[1]),
    ]
    for copy in copies:
        copy.start()
    levels, block_rows, _ = rhs_ref.shape
    base = levels * block_rows
    sent_ref[base:, :] = jnp.zeros((sent_ref.shape[0] - base, LANES), jnp.float32)
    tables = base + (levels - 1) * block_rows
    pairs, per, targets = sources_ref.shape
    for pair in range(pairs):
        rows = slice(tables + pair * per, tables + (pair + 1) * per)
        sent_ref[rows, 0:targets] = sources_ref[pair].astype(jnp.float32)
    for copy in copies:
        copy.wait()
    solution = jnp.dot(
        dinv_ref[0],
        rhs_ref[0].astype(jnp.float32),
        precision=lax.Precision.HIGHEST,
        preferred_element_type=jnp.float32,
    )
    solution_ref[...] = solution
    left_is_mine = lax.axis_index("core") == 0
    for level in range(levels):
        block = rhs_ref[level].astype(jnp.float32) if level else solution
        left, right = block[:, :LANES], block[:, LANES:]
        mine_ref[level] = jnp.where(left_is_mine, left, right).astype(jnp.bfloat16)
        rows = slice(level * block_rows, (level + 1) * block_rows)
        sent_ref[rows, :] = jnp.where(left_is_mine, right, left)
        if level:
            rows = slice(base + (level - 1) * block_rows, base + level * block_rows)
            sent_ref[rows, 0:block_rows] = dinv_ref[level]


def spread_kernel(mine_ref, swapped_ref, copies_ref, table_ref):
    block_rows = mine_ref.shape[1]
    other = swapped_ref.at[1 - lax.axis_index("core")]
    blocks = mine_ref[0], other[0:block_rows, :].astype(jnp.bfloat16)
    for side, block in enumerate(blocks):
        for peer in range(copies_ref.shape[0]):
            copies_ref[peer, side] = block
    rows = table_ref.shape[0]
    table_ref[...] = other[other.shape[0] - rows :, :].astype(jnp.int32)


def terms_kernel(pairs, own_table, other_table, *refs):
    lowers, gathered, out_ref = refs[:SIDES], refs[SIDES:-1], refs[-1]
    core = lax.axis_index("core")
    _, targets, block_rows, depth = lowers[0].shape
    per = depth // block_rows

    def one(target, carry):
        parts = []
        for side in range(SIDES):
            factors, picked = [], []
            for block, pair in zip(gathered, pairs):
                factors.append(lowers[side][pair, target])
                for entry in range(per):
                    if side == 0:
                        source = own_table[pair, entry, target]
                    else:
                        source = other_table[pair * per + entry, target]
                    rows = block[jnp.bitwise_xor(jnp.maximum(source, 0), core)]
                    picked.append(jnp.where(source >= 0, rows, jnp.zeros_like(rows)))
            parts.append(
                jnp.dot(
                    jnp.concatenate(factors, axis=1),
                    jnp.concatenate(picked, axis=0),
                    preferred_element_type=jnp.float32,
                )
            )
        encode(parts, out_ref, target)
        return carry

    lax.fori_loop(0, targets, one, 0, unroll=8)


def middle_kernel(arrived_ref, out_ref):
    peers, targets = arrived_ref.shape[:2]
    for target in range(targets):
        encode(add_peers(peers, lambda peer: arrived_ref[peer, target]), out_ref, target)


def solve_parts(level, mine_ref, swapped_ref, dinv_ref, arrived_ref):
    levels, block_rows, _ = mine_ref.shape
    other = swapped_ref.at[1 - lax.axis_index("core")]
    base = (levels + level - 1) * block_rows
    blocks = mine_ref[level].astype(jnp.float32), other[level * block_rows : (level + 1) * block_rows, :]
    factors = dinv_ref[level], other[base : base + block_rows, 0:block_rows]
    total = add_peers(arrived_ref.shape[0], lambda peer: arrived_ref[peer])
    return [
        jnp.dot(
            factor,
            block - part,
            precision=lax.Precision.HIGHEST,
            preferred_element_type=jnp.float32,
        )
        for factor, block, part in zip(factors, blocks, total)
    ]


def solve_kernel(level, mine_ref, swapped_ref, dinv_ref, arrived_ref, solution_ref, copies_ref):
    parts = solve_parts(level, mine_ref, swapped_ref, dinv_ref, arrived_ref)
    for side, part in enumerate(parts):
        solution_ref[side] = part
        for peer in range(copies_ref.shape[0]):
            copies_ref[peer, side] = part.astype(jnp.bfloat16)


def last_kernel(mine_ref, swapped_ref, dinv_ref, arrived_ref, *refs):
    earlier, outs = refs[:-SIDES], refs[-SIDES:]
    for place, ref in enumerate(earlier):
        for side, out_ref in enumerate(outs):
            out_ref[place] = ref[side]
    level = len(earlier) + 1
    parts = solve_parts(level, mine_ref, swapped_ref, dinv_ref, arrived_ref)
    for part, out_ref in zip(parts, outs):
        out_ref[level - 1] = part


def join_kernel(first_ref, mine_ref, swapped_ref, out_ref, sems):
    core = lax.axis_index("core")
    later = pl.ds(1, mine_ref.shape[0])
    copies = [pltpu.make_async_copy(first_ref, out_ref.at[0], sems.at[0])]
    for index, (half, ref) in enumerate(((core, mine_ref), (1 - core, swapped_ref.at[1 - core]))):
        columns = pl.ds(pl.multiple_of(half * LANES, LANES), LANES)
        copies.append(pltpu.make_async_copy(ref, out_ref.at[later, :, columns], sems.at[1 + index]))
    for copy in copies:
        copy.start()
    for copy in copies:
        copy.wait()


def on_device(rhs, dinv, lower, sources):
    levels, _, _, block_rows, width = rhs.shape
    x_size, y_size, z_size = (lax.axis_size(name) for name in ("x", "y", "z"))
    pair_of = {}
    for section in range(levels):
        for target in range(section + 1, levels):
            pair_of[section, target] = len(pair_of)
    rhs, dinv, lower = rhs[:, 0, 0], dinv[:, 0, 0], lower[:, 0, 0]
    sources = jnp.swapaxes(sources[:, 0, 0], 1, 2)
    targets = lower.shape[1]
    coded_rows = SIDES * block_rows + PAD
    copies_shape = pltpu.VMEM((y_size, SIDES, block_rows, LANES), jnp.bfloat16)

    table_rows = -(-sources.shape[0] * sources.shape[1] // PAD) * PAD
    sent_rows = (2 * levels - 1) * block_rows + table_rows
    first, mine, sent = pl.pallas_call(
        first_kernel,
        out_shape=(
            pltpu.VMEM((block_rows, width), jnp.float32),
            pltpu.VMEM((levels, block_rows, LANES), jnp.bfloat16),
            pltpu.VMEM((sent_rows, LANES), jnp.float32),
        ),
        in_specs=[ANY, ANY, VMEM],
        out_specs=(VMEM,) * 3,
        scratch_shapes=[
            pltpu.VMEM(rhs.shape, rhs.dtype),
            pltpu.VMEM(dinv.shape, dinv.dtype),
            pltpu.SemaphoreType.DMA((2,)),
        ],
        compiler_params=PARAMS,
        name="first",
    )(in_hbm(rhs), in_hbm(dinv), in_hbm(sources))
    swapped = in_vmem(lax.all_gather(sent, "core", axis=0, tiled=False))
    mine = in_vmem(mine)
    copies, table = pl.pallas_call(
        spread_kernel,
        out_shape=(copies_shape, pltpu.VMEM((table_rows, LANES), jnp.int32)),
        in_specs=[VMEM] * 2,
        out_specs=(VMEM, VMEM),
        compiler_params=PARAMS,
        name="spread",
    )(mine, swapped)
    copies, lower_sent = lax.optimization_barrier((copies, lower))
    lowers = (lower, lax.ppermute(lower_sent, "core", [(0, 1), (1, 0)]))

    gathered, solutions = [], []
    for level in range(1, levels):
        blocks = lax.all_to_all(copies, "y", split_axis=0, concat_axis=0, tiled=True)
        gathered.append(in_vmem(blocks.reshape(y_size * SIDES, block_rows, LANES)))
        pairs = tuple(pair_of[earlier, level] for earlier in range(level))
        coded = pl.pallas_call(
            functools.partial(terms_kernel, pairs),
            out_shape=pltpu.VMEM((targets, coded_rows, LANES), jnp.int16),
            in_specs=[SMEM] * 2 + [VMEM] * (SIDES + len(gathered)),
            out_specs=VMEM,
            compiler_params=PARAMS,
            name="local_terms",
        )(in_hbm(sources), table, *map(in_vmem, lowers), *gathered)
        coded = coded.reshape(x_size, z_size, coded_rows, LANES)
        arrived = lax.all_to_all(coded, "x", split_axis=0, concat_axis=0, tiled=True)
        coded = pl.pallas_call(
            middle_kernel,
            out_shape=pltpu.VMEM((z_size, coded_rows, LANES), jnp.int16),
            in_specs=[VMEM],
            out_specs=VMEM,
            compiler_params=PARAMS,
            name="sum_x",
        )(in_vmem(arrived))
        arrived = lax.all_to_all(coded, "z", split_axis=0, concat_axis=0, tiled=True)
        operands = [mine, swapped] + [in_vmem(array) for array in (dinv, arrived)]
        if level + 1 < levels:
            solution, copies = pl.pallas_call(
                functools.partial(solve_kernel, level),
                out_shape=(pltpu.VMEM((SIDES, block_rows, LANES), jnp.float32), copies_shape),
                in_specs=[VMEM] * 4,
                out_specs=(VMEM, VMEM),
                compiler_params=PARAMS,
                name="solve",
            )(*operands)
            solutions.append(solution)
        else:
            parts = pl.pallas_call(
                last_kernel,
                out_shape=(pltpu.VMEM((levels - 1, block_rows, LANES), jnp.float32),) * SIDES,
                in_specs=[VMEM] * (4 + len(solutions)),
                out_specs=(VMEM,) * SIDES,
                compiler_params=PARAMS,
                name="solve_last",
            )(*operands, *map(in_vmem, solutions))
    halves = lax.all_gather(parts[1], "core", axis=0, tiled=False)
    joined = pl.pallas_call(
        join_kernel,
        out_shape=jax.ShapeDtypeStruct((levels, block_rows, width), jnp.float32),
        in_specs=[VMEM] * 3,
        out_specs=ANY,
        scratch_shapes=[pltpu.SemaphoreType.DMA((1 + SIDES,))],
        compiler_params=PARAMS,
        name="join",
    )(in_vmem(first), in_vmem(parts[0]), in_vmem(halves))
    return joined[:, None, None]


def solution(mesh):
    split = Mesh(mesh.devices.reshape(8, 2, 4, 8), ("y", "core", "x", "z"))
    row, col = ("y", "core"), ("x", "z")
    in_specs = (
        P(None, row, col, None, None),
        P(None, row, col, None, None),
        P(None, row, col, None, None, None),
        P(None, row, col, None, None),
    )
    out_specs = P(None, row, col, None, None)
    return jax.shard_map(
        on_device, mesh=split, in_specs=in_specs, out_specs=out_specs, check_vma=False
    )
```

time: 174 us -> 167 us (0.960)
  blocking collectives: 117 us -> 148 us
  starting transfers between devices: 21 us -> 2.28 us
  waiting for transfers between devices: 15.7 us -> 0.01 us
  Pallas kernels: 16.8 us -> 13.5 us
    all_to_all x2 -> x0, blocking collectives: 21.4 us -> none  [the longest x1 11 us: on_device(): lax.all_to_all(parts, 'core', split_axis=0, concat_axis=0, tiled=True)]
    all_to_all x2 -> x3, blocking collectives: 26.2 us -> 46.3 us  [on_device(): lax.all_to_all(coded, 'z', split_axis=0, concat_axis=0, tiled=True)]
    all_gather x0 -> x2, blocking collectives: none -> 17.7 us  [the longest x1 9.06 us: on_device(): halves = lax.all_gather(parts[1], 'core', axis=0, tiled=False)]
    all_to_all x2 -> x3, blocking collectives: 26 us -> 40.7 us  [on_device(): lax.all_to_all(copies, 'y', split_axis=0, concat_axis=0, tiled=True)]
    all_to_all x2 -> x0, waiting for transfers between devices: 13.7 us -> none  [the longest x1 9.21 us: on_device(): lax.all_to_all(copies, 'y', split_axis=0, concat_axis=0, tiled=True)]
    all_to_all x2 -> x0, starting transfers between devices: 12.7 us -> none  [the longest x1 9.31 us: on_device(): lax.all_to_all(coded, 'z', split_axis=0, concat_axis=0, tiled=True)]
    ppermute x3 -> x1, starting transfers between devices: 8.24 us -> 2.28 us  [on_device(): lowers = (lower, lax.ppermute(lower_sent, 'core', [(0, 1), (1, 0)]))]
    pallas_call x3, Pallas kernels: 12.3 us -> 8.71 us  [on_device(): pl.pallas_call(functools.partial(terms_kernel, pairs), out_shape=pltpu.VM...]
  transfers between devices with their start and end apart: 5 -> 1, of which waited for: 4 -> 0; matrix products, arithmetic and copies ran while one was open for 0% -> 0% of each run, Pallas kernels for 0% -> 0%
where the time goes in v6:
time: 167 us; the launch traced here: 166 us
  blocking collectives  148 us (89%)
  Pallas kernels  13.5 us (8%)
  starting transfers between devices  2.28 us (1%)
  local copies, waits for them, and re-layouts  1.9 us (1%)
    all_to_all x3, blocking collectives, on_device(): lax.all_to_all(coded, 'z', split_axis=0, concat_axis=0, tiled=True)  46.3 us
    all_to_all x3, blocking collectives, on_device(): lax.all_to_all(coded, 'x', split_axis=0, concat_axis=0, tiled=True)  43.6 us
    all_to_all x3, blocking collectives, on_device(): lax.all_to_all(copies, 'y', split_axis=0, concat_axis=0, tiled=True)  40.7 us
    all_gather x1, blocking collectives, on_device(): halves = lax.all_gather(parts[1], 'core', axis=0, tiled=False)  9.06 us
    pallas_call x3, Pallas kernels, on_device(): pl.pallas_call(functools.partial(terms_kernel, pairs), out_shape=pltpu.VM...  8.71 us
    all_gather x1, blocking collectives, on_device(): swapped = in_vmem(lax.all_gather(sent, 'core', axis=0, tiled=False))  8.65 us
  transfers between devices with their start and end apart: 1, of which 0 were waited for; matrix products, arithmetic and copies ran while one was open for 0% of the time, Pallas kernels for 0%

profile of v6, /device:TPU:1, one launch (start us, length us, event | category | flops | bytes accessed | tf_op | source)
XLA Modules:
  0.0 166.1 jit_solution(3513544499524453871)
XLA Ops:
  0.0 1.9 %first.1 = (f32[64,256]{1,0:T(8,128)S(1)}, bf16[4,64,128]{2,1,0:T(8,128)(2,1)S(1)}, f32[464,128]{1,0:T(8,128)S(1)}) custom-call(bf16[4,64,256]{2,1,0:T(8,128)(2,1)} %bitcast.39, f32[4,64,64]{2,1,0:T(8,128)} %bitcast.33, s32[6,2,32]{2,1,0:T(2,128)} %bitcast.40), custom_call_target="tpu_custom_call" | custom-call | tf_op jit(solution)/shard_map/first/pallas_call | solution.py:211
  1.9 8.7 %all-gather = f32[928,128]{1,0:T(8,128)S(1)} all-gather(f32[464,128]{1,0:T(8,128)S(1)} %get-tuple-element.20), channel_id=2, replica_groups=mesh['y'=8,'core'=2,'x'=4,'z'=8] {'core'}, dimensions={0}, use_global_device_ids=true | all-gather | bytes 712704 | tf_op jit(solution)/shard_map/all_gather | solution.py:228
  10.6 2.3 %collective-permute-start = (bf16[6,32,64,128]{3,2,1,0:T(8,128)(2,1)}, bf16[6,32,64,128]{3,2,1,0:T(8,128)(2,1)S(1)}, u32[]{:S(2)}, u32[]{:S(2)}) collective-permute-start(bf16[6,32,64,128]{3,2,1,0:T(8,128)(2,1)} %bitcast.17), channel_id=1, source_target_pairs={{0,32},{32,0},{1,33},{33,1},{2,34},{34,2},{3,35},{35,3},{4,36},{36... | collective-permute-start | bytes 9437192 | tf_op jit(solution)/shard_map/ppermute | solution.py:239
  12.9 14.8 %all_to_all.45 = bf16[8,2,64,128]{3,2,1,0:T(8,128)(2,1)S(1)} all-to-all(bf16[8,2,64,128]{3,2,1,0:T(8,128)(2,1)S(1)} %get-tuple-element.24), channel_id=1, replica_groups=mesh['y'=8,'core'=2,'x'=4,'z'=8] {'y'}, dimensions={0} | all-to-all | bytes 524288 | tf_op jit(solution)/shard_map/all_to_all | solution.py:243
  27.6 0.0 collective-permute-done.refs_1_
  27.6 0.0 copy-start
  27.6 1.9 %copy-done = bf16[6,1,1,32,64,128]{5,4,3,2,1,0:T(8,128)(2,1)S(1)} copy-done((bf16[6,1,1,32,64,128]{5,4,3,2,1,0:T(8,128)(2,1)S(1)}, bf16[6,1,1,32,64,128]{5,4,3,2,1,0:T(8,128)(2,1)}, u32[]{:S(2)}) %copy-start) | copy-done | bytes 3145752
  29.5 2.2 %local_terms.3 = s16[32,136,128]{2,1,0:T(8,128)(2,1)S(1)} custom-call(s32[6,2,32]{2,1,0:T(2,128)} %bitcast.41, s32[16,128]{1,0:T(8,128)S(1)} %get-tuple-element.21.other_table, bf16[6,32,64,128]{3,2,1,0:T(8,128)(2,1)S(1)} %bitcast.18, bf16[6,32,64,128]{3,2,1,0:T(8,128)(2,1)S(1)} %collective-permute-done.refs_1_, bf16[16,64,128]{2,1,0:T(8,128)(2,1)S(1)} %bitcast.28), custom_call_target="tpu_custom_call" | custom-call | tf_op jit(solution)/shard_map/local_terms/pallas_call | solution.py:246
  31.7 0.0 copy-start.2
  31.7 17.7 %all_to_all.46.arrived_ref = s16[4,8,136,128]{3,2,1,0:T(8,128)(2,1)S(1)} all-to-all(s16[4,8,136,128]{3,2,1,0:T(8,128)(2,1)S(1)} %bitcast.26), channel_id=1, replica_groups=mesh['y'=8,'core'=2,'x'=4,'z'=8] {'x'}, dimensions={0} | all-to-all | bytes 2228224 | tf_op jit(solution)/shard_map/all_to_all | solution.py:255
  49.4 0.0 copy-start.1
  49.4 0.4 sum_x.3
  49.9 19.2 %all_to_all.47.arrived_ref = s16[8,136,128]{2,1,0:T(8,128)(2,1)S(1)} all-to-all(s16[8,136,128]{2,1,0:T(8,128)(2,1)S(1)} %sum_x.3), channel_id=1, replica_groups=mesh['y'=8,'core'=2,'x'=4,'z'=8] {'z'}, dimensions={0} | all-to-all | bytes 557056 | tf_op jit(solution)/shard_map/all_to_all | solution.py:264
  69.1 0.0 copy-done.2
  69.1 0.3 solve.2
  69.4 11.8 %all_to_all.48 = bf16[8,2,64,128]{3,2,1,0:T(8,128)(2,1)S(1)} all-to-all(bf16[8,2,64,128]{3,2,1,0:T(8,128)(2,1)S(1)} %get-tuple-element.25), channel_id=1, replica_groups=mesh['y'=8,'core'=2,'x'=4,'z'=8] {'y'}, dimensions={0} | all-to-all | bytes 524288 | tf_op jit(solution)/shard_map/all_to_all | solution.py:243
  81.2 0.0 copy-done.1
  81.2 2.9 %local_terms.4 = s16[32,136,128]{2,1,0:T(8,128)(2,1)S(1)} custom-call(s32[6,2,32]{2,1,0:T(2,128)} %bitcast.42, s32[16,128]{1,0:T(8,128)S(1)} %get-tuple-element.21.other_table, bf16[6,32,64,128]{3,2,1,0:T(8,128)(2,1)S(1)} %bitcast.19, bf16[6,32,64,128]{3,2,1,0:T(8,128)(2,1)S(1)} %collective-permute-done.refs_1_, bf16[16,64,128]{2,1,0:T(8,128)(2,1)S(1)} %bitcast.29, ...), custom_call_target="tpu_custom_call" | custom-call | tf_op jit(solution)/shard_map/local_terms/pallas_call | solution.py:246
  84.0 13.2 %all_to_all.49.arrived_ref = s16[4,8,136,128]{3,2,1,0:T(8,128)(2,1)S(1)} all-to-all(s16[4,8,136,128]{3,2,1,0:T(8,128)(2,1)S(1)} %bitcast.27), channel_id=1, replica_groups=mesh['y'=8,'core'=2,'x'=4,'z'=8] {'x'}, dimensions={0} | all-to-all | bytes 2228224 | tf_op jit(solution)/shard_map/all_to_all | solution.py:255
  97.2 0.4 sum_x.4
  97.7 15.1 %all_to_all.50.arrived_ref = s16[8,136,128]{2,1,0:T(8,128)(2,1)S(1)} all-to-all(s16[8,136,128]{2,1,0:T(8,128)(2,1)S(1)} %sum_x.4), channel_id=1, replica_groups=mesh['y'=8,'core'=2,'x'=4,'z'=8] {'z'}, dimensions={0} | all-to-all | bytes 557056 | tf_op jit(solution)/shard_map/all_to_all | solution.py:264
  112.8 0.3 solve.3
  113.0 14.1 %all_to_all.51 = bf16[8,2,64,128]{3,2,1,0:T(8,128)(2,1)S(1)} all-to-all(bf16[8,2,64,128]{3,2,1,0:T(8,128)(2,1)S(1)} %get-tuple-element.26), channel_id=1, replica_groups=mesh['y'=8,'core'=2,'x'=4,'z'=8] {'y'}, dimensions={0} | all-to-all | bytes 524288 | tf_op jit(solution)/shard_map/all_to_all | solution.py:243
  127.1 3.7 %local_terms.5 = s16[32,136,128]{2,1,0:T(8,128)(2,1)S(1)} custom-call(s32[6,2,32]{2,1,0:T(2,128)} %bitcast.43, s32[16,128]{1,0:T(8,128)S(1)} %get-tuple-element.21.other_table, bf16[6,32,64,128]{3,2,1,0:T(8,128)(2,1)S(1)} %bitcast.20, bf16[6,32,64,128]{3,2,1,0:T(8,128)(2,1)S(1)} %collective-permute-done.refs_1_, bf16[16,64,128]{2,1,0:T(8,128)(2,1)S(1)} %bitcast.30, ...), custom_call_target="tpu_custom_call" | custom-call | tf_op jit(solution)/shard_map/local_terms/pallas_call | solution.py:246
  130.8 12.7 %all_to_all.52.arrived_ref = s16[4,8,136,128]{3,2,1,0:T(8,128)(2,1)S(1)} all-to-all(s16[4,8,136,128]{3,2,1,0:T(8,128)(2,1)S(1)} %bitcast.25), channel_id=1, replica_groups=mesh['y'=8,'core'=2,'x'=4,'z'=8] {'x'}, dimensions={0} | all-to-all | bytes 2228224 | tf_op jit(solution)/shard_map/all_to_all | solution.py:255
  143.5 0.4 sum_x.5
  144.0 12.0 %all_to_all.53.arrived_ref = s16[8,136,128]{2,1,0:T(8,128)(2,1)S(1)} all-to-all(s16[8,136,128]{2,1,0:T(8,128)(2,1)S(1)} %sum_x.5), channel_id=1, replica_groups=mesh['y'=8,'core'=2,'x'=4,'z'=8] {'z'}, dimensions={0} | all-to-all | bytes 557056 | tf_op jit(solution)/shard_map/all_to_all | solution.py:264
  156.0 0.3 solve_last.1
  156.3 9.1 %all-gather.1 = f32[6,64,128]{2,1,0:T(8,128)S(1)} all-gather(f32[3,64,128]{2,1,0:T(8,128)S(1)} %get-tuple-element.30), channel_id=3, replica_groups=mesh['y'=8,'core'=2,'x'=4,'z'=8] {'core'}, dimensions={0}, use_global_device_ids=true | all-gather | bytes 294912 | tf_op jit(solution)/shard_map/all_gather | solution.py:285
  165.3 0.7 join.1
  (1 shorter events, 0.0 us)
Async XLA Ops:
  10.6 17.1 %collective-permute-start = (bf16[6,32,64,128]{3,2,1,0:T(8,128)(2,1)}, bf16[6,32,64,128]{3,2,1,0:T(8,128)(2,1)S(1)}, u32[]{:S(2)}, u32[]{:S(2)}) collective-permute-start(bf16[6,32,64,128]{3,2,1,0:T(8,128)(2,1)} %bitcast.17), channel_id=1, source_target_pairs={{0,32},{32,0},{1,33},{33,1},{2,34},{34,2},{3,35},{35,3},{4,36},{36... | collective-permute-start | bytes 9437192 | tf_op jit(solution)/shard_map/ppermute | solution.py:239
  27.6 1.9 %copy-start = (bf16[6,1,1,32,64,128]{5,4,3,2,1,0:T(8,128)(2,1)S(1)}, bf16[6,1,1,32,64,128]{5,4,3,2,1,0:T(8,128)(2,1)}, u32[]{:S(2)}) copy-start(bf16[6,1,1,32,64,128]{5,4,3,2,1,0:T(8,128)(2,1)} %param.6) | copy-start | bytes 9437188
  31.7 37.4 %copy-start.2 = (f32[4,1,1,64,64]{4,3,2,1,0:T(8,128)S(1)}, f32[4,1,1,64,64]{4,3,2,1,0:T(8,128)}, u32[]{:S(2)}) copy-start(f32[4,1,1,64,64]{4,3,2,1,0:T(8,128)} %param.5) | copy-start | bytes 196612
  49.4 31.7 %copy-start.1 = (bf16[6,1,1,32,64,128]{5,4,3,2,1,0:T(8,128)(2,1)S(1)}, bf16[6,1,1,32,64,128]{5,4,3,2,1,0:T(8,128)(2,1)}, u32[]{:S(2)}) copy-start(bf16[6,1,1,32,64,128]{5,4,3,2,1,0:T(8,128)(2,1)} %param.6) | copy-start | bytes 9437188

commit v7 on v6

--- a/solution.py
+++ b/solution.py
@@ -58,12 +58,16 @@
     return total
 
 
-def first_kernel(rhs_hbm, dinv_hbm, sources_ref, solution_ref, mine_ref, sent_ref, rhs_ref, dinv_ref, sems):
+def first_kernel(rhs_hbm, dinv_hbm, lower_hbm, sources_ref, *refs):
+    solution_ref, mine_ref, sent_ref, factors_ref, rhs_ref, dinv_ref, sems = refs
     copies = [
         pltpu.make_async_copy(rhs_hbm, rhs_ref, sems.at[0]),
         pltpu.make_async_copy(dinv_hbm, dinv_ref, sems.at[1]),
     ]
-    for copy in copies:
+    early = pltpu.make_async_copy(
+        lower_hbm.at[pl.ds(0, factors_ref.shape[0])], factors_ref, sems.at[2]
+    )
+    for copy in (*copies, early):
         copy.start()
     levels, block_rows, _ = rhs_ref.shape
     base = levels * block_rows
@@ -92,6 +96,7 @@
         if level:
             rows = slice(base + (level - 1) * block_rows, base + level * block_rows)
             sent_ref[rows, 0:block_rows] = dinv_ref[level]
+    early.wait()
 
 
 def spread_kernel(mine_ref, swapped_ref, copies_ref, table_ref):
@@ -105,13 +110,17 @@
     table_ref[...] = other[other.shape[0] - rows :, :].astype(jnp.int32)
 
 
-def terms_kernel(pairs, own_table, other_table, *refs):
+def terms_kernel(pairs, z_sizes, own_table, other_table, *refs):
     lowers, gathered, out_ref = refs[:SIDES], refs[SIDES:-1], refs[-1]
     core = lax.axis_index("core")
     _, targets, block_rows, depth = lowers[0].shape
     per = depth // block_rows
+    za_size, zb_size = z_sizes
+    z_size = za_size * zb_size
 
     def one(target, carry):
+        z = lax.rem(target, z_size)
+        slot = target - z + lax.rem(z, zb_size) * za_size + lax.div(z, zb_size)
         parts = []
         for side in range(SIDES):
             factors, picked = [], []
@@ -131,7 +140,7 @@
                     preferred_element_type=jnp.float32,
                 )
             )
-        encode(parts, out_ref, target)
+        encode(parts, out_ref, slot)
         return carry
 
     lax.fori_loop(0, targets, one, 0, unroll=8)
@@ -195,7 +204,7 @@
 
 def on_device(rhs, dinv, lower, sources):
     levels, _, _, block_rows, width = rhs.shape
-    x_size, y_size, z_size = (lax.axis_size(name) for name in ("x", "y", "z"))
+    y_size, x_size, za_size, zb_size = (lax.axis_size(name) for name in ("y", "x", "za", "zb"))
     pair_of = {}
     for section in range(levels):
         for target in range(section + 1, levels):
@@ -208,23 +217,24 @@
 
     table_rows = -(-sources.shape[0] * sources.shape[1] // PAD) * PAD
     sent_rows = (2 * levels - 1) * block_rows + table_rows
-    first, mine, sent = pl.pallas_call(
+    first, mine, sent, early = pl.pallas_call(
         first_kernel,
         out_shape=(
             pltpu.VMEM((block_rows, width), jnp.float32),
             pltpu.VMEM((levels, block_rows, LANES), jnp.bfloat16),
             pltpu.VMEM((sent_rows, LANES), jnp.float32),
+            pltpu.VMEM((1,) + lower.shape[1:], lower.dtype),
         ),
-        in_specs=[ANY, ANY, VMEM],
-        out_specs=(VMEM,) * 3,
+        in_specs=[ANY, ANY, ANY, VMEM],
+        out_specs=(VMEM,) * 4,
         scratch_shapes=[
             pltpu.VMEM(rhs.shape, rhs.dtype),
             pltpu.VMEM(dinv.shape, dinv.dtype),
-            pltpu.SemaphoreType.DMA((2,)),
+            pltpu.SemaphoreType.DMA((3,)),
         ],
         compiler_params=PARAMS,
         name="first",
-    )(in_hbm(rhs), in_hbm(dinv), in_hbm(sources))
+    )(in_hbm(rhs), in_hbm(dinv), in_hbm(lower), in_hbm(sources))
     swapped = in_vmem(lax.all_gather(sent, "core", axis=0, tiled=False))
     mine = in_vmem(mine)
     copies, table = pl.pallas_call(
@@ -236,32 +246,33 @@
         name="spread",
     )(mine, swapped)
     copies, lower_sent = lax.optimization_barrier((copies, lower))
-    lowers = (lower, lax.ppermute(lower_sent, "core", [(0, 1), (1, 0)]))
+    other_lower = lax.ppermute(lower_sent, "core", [(0, 1), (1, 0)])
 
     gathered, solutions = [], []
     for level in range(1, levels):
         blocks = lax.all_to_all(copies, "y", split_axis=0, concat_axis=0, tiled=True)
         gathered.append(in_vmem(blocks.reshape(y_size * SIDES, block_rows, LANES)))
         pairs = tuple(pair_of[earlier, level] for earlier in range(level))
+        own = early if level == 1 else lower
         coded = pl.pallas_call(
-            functools.partial(terms_kernel, pairs),
+            functools.partial(terms_kernel, pairs, (za_size, zb_size)),
             out_shape=pltpu.VMEM((targets, coded_rows, LANES), jnp.int16),
             in_specs=[SMEM] * 2 + [VMEM] * (SIDES + len(gathered)),
             out_specs=VMEM,
             compiler_params=PARAMS,
             name="local_terms",
-        )(in_hbm(sources), table, *map(in_vmem, lowers), *gathered)
-        coded = coded.reshape(x_size, z_size, coded_rows, LANES)
-        arrived = lax.all_to_all(coded, "x", split_axis=0, concat_axis=0, tiled=True)
+        )(in_hbm(sources), table, in_vmem(own), in_vmem(other_lower), *gathered)
+        coded = coded.reshape(x_size * zb_size, za_size, coded_rows, LANES)
+        arrived = lax.all_to_all(coded, ("x", "zb"), split_axis=0, concat_axis=0, tiled=True)
         coded = pl.pallas_call(
             middle_kernel,
-            out_shape=pltpu.VMEM((z_size, coded_rows, LANES), jnp.int16),
+            out_shape=pltpu.VMEM((za_size, coded_rows, LANES), jnp.int16),
             in_specs=[VMEM],
             out_specs=VMEM,
             compiler_params=PARAMS,
-            name="sum_x",
+            name="sum_near",
         )(in_vmem(arrived))
-        arrived = lax.all_to_all(coded, "z", split_axis=0, concat_axis=0, tiled=True)
+        arrived = lax.all_to_all(coded, "za", split_axis=0, concat_axis=0, tiled=True)
         operands = [mine, swapped] + [in_vmem(array) for array in (dinv, arrived)]
         if level + 1 < levels:
             solution, copies = pl.pallas_call(
@@ -296,8 +307,8 @@
 
 
 def solution(mesh):
-    split = Mesh(mesh.devices.reshape(8, 2, 4, 8), ("y", "core", "x", "z"))
-    row, col = ("y", "core"), ("x", "z")
+    split = Mesh(mesh.devices.reshape(8, 2, 4, 4, 2), ("y", "core", "x", "za", "zb"))
+    row, col = ("y", "core"), ("x", "za", "zb")
     in_specs = (
         P(None, row, col, None, None),
         P(None, row, col, None, None),

time: 167 us -> 161 us (0.964)
  blocking collectives: 148 us -> 144 us
  local copies, waits for them, and re-layouts: 1.9 us -> 0.01 us
    all_to_all x6, blocking collectives: 89.9 us -> 84.2 us  [the longest x3 47.8 us: on_device(): lax.all_to_all(coded, ('x', 'zb'), split_axis=0, concat_axis=0, tiled=True)]
    all_gather x1, blocking collectives: 9.06 us -> 13.2 us  [on_device(): halves = lax.all_gather(parts[1], 'core', axis=0, tiled=False)]
    all_to_all x3, blocking collectives: 40.7 us -> 38.4 us  [on_device(): lax.all_to_all(copies, 'y', split_axis=0, concat_axis=0, tiled=True)]
    unnamed x6 -> x4, local copies, waits for them, and re-layouts: 1.9 us -> 0.01 us
where the time goes in v7:
time: 161 us
  blocking collectives  144 us (89%)
  Pallas kernels  13.8 us (9%)
  starting transfers between devices  2.28 us (1%)
    all_to_all x3, blocking collectives, on_device(): lax.all_to_all(coded, ('x', 'zb'), split_axis=0, concat_axis=0, tiled=True)  47.8 us
    all_to_all x3, blocking collectives, on_device(): lax.all_to_all(copies, 'y', split_axis=0, concat_axis=0, tiled=True)  38.4 us
    all_to_all x3, blocking collectives, on_device(): lax.all_to_all(coded, 'za', split_axis=0, concat_axis=0, tiled=True)  36.4 us
    all_gather x1, blocking collectives, on_device(): halves = lax.all_gather(parts[1], 'core', axis=0, tiled=False)  13.2 us
    pallas_call x3, Pallas kernels, on_device(): pl.pallas_call(functools.partial(terms_kernel, pairs, (za_size, zb_size))...  9.01 us
    all_gather x1, blocking collectives, on_device(): swapped = in_vmem(lax.all_gather(sent, 'core', axis=0, tiled=False))  8.65 us
  transfers between devices with their start and end apart: 1, of which 0 were waited for; matrix products, arithmetic and copies ran while one was open for 0% of the time, Pallas kernels for 0%

profile of v7, /device:TPU:1, one launch (start us, length us, event | category | flops | bytes accessed | tf_op | source)
XLA Modules:
  0.0 160.6 jit_solution(12072045149631382964)
XLA Ops:
  0.0 0.0 copy-start
  0.0 2.2 %first.1 = (f32[64,256]{1,0:T(8,128)S(1)}, bf16[4,64,128]{2,1,0:T(8,128)(2,1)S(1)}, f32[464,128]{1,0:T(8,128)S(1)}, bf16[1,32,64,128]{3,2,1,0:T(8,128)(2,1)S(1)}) custom-call(bf16[4,64,256]{2,1,0:T(8,128)(2,1)} %bitcast.39, f32[4,64,64]{2,1,0:T(8,128)} %bitcast.33, bf16[6,32,64,128]{3,2,1,0:T(8,128)(2,1)} %bitcast.17, s32[6,2,32]{2,1,0:T(2,128)} %bitcast.40), custom_call_target="tpu_custom_call" | custom-call | tf_op jit(solution)/shard_map/first/pallas_call | solution.py:220
  2.2 8.7 %all-gather = f32[928,128]{1,0:T(8,128)S(1)} all-gather(f32[464,128]{1,0:T(8,128)S(1)} %get-tuple-element.21), channel_id=2, replica_groups=mesh['y'=8,'core'=2,'x'=4,'za'=4,'zb'=2] {'core'}, dimensions={0}, use_global_device_ids=true | all-gather | bytes 712704 | tf_op jit(solution)/shard_map/all_gather | solution.py:238
  10.8 0.0 copy-done
  10.9 2.3 %collective-permute-start = (bf16[6,32,64,128]{3,2,1,0:T(8,128)(2,1)S(1)}, bf16[6,32,64,128]{3,2,1,0:T(8,128)(2,1)S(1)}, u32[]{:S(2)}, u32[]{:S(2)}) collective-permute-start(bf16[6,32,64,128]{3,2,1,0:T(8,128)(2,1)S(1)} %bitcast.18), channel_id=1, source_target_pairs={{0,32},{32,0},{1,33},{33,1},{2,34},{34,2},{3,35},{35,3},{4,36},{36... | collective-permute-start | bytes 9437192 | tf_op jit(solution)/shard_map/ppermute | solution.py:249
  13.1 14.8 %all_to_all.45 = bf16[8,2,64,128]{3,2,1,0:T(8,128)(2,1)S(1)} all-to-all(bf16[8,2,64,128]{3,2,1,0:T(8,128)(2,1)S(1)} %get-tuple-element.25), channel_id=1, replica_groups=mesh['y'=8,'core'=2,'x'=4,'za'=4,'zb'=2] {'y'}, dimensions={0} | all-to-all | bytes 524288 | tf_op jit(solution)/shard_map/all_to_all | solution.py:253
  27.9 0.0 collective-permute-done.refs_1_
  27.9 2.3 %local_terms.3 = s16[32,136,128]{2,1,0:T(8,128)(2,1)S(1)} custom-call(s32[6,2,32]{2,1,0:T(2,128)} %bitcast.41, s32[16,128]{1,0:T(8,128)S(1)} %get-tuple-element.22.other_table, bf16[1,32,64,128]{3,2,1,0:T(8,128)(2,1)S(1)} %get-tuple-element.26.refs_0_, bf16[6,32,64,128]{3,2,1,0:T(8,128)(2,1)S(1)} %collective-permute-done.refs_1_, ...), custom_call_target="tpu_custom_call" | custom-call | tf_op jit(solution)/shard_map/local_terms/pallas_call | solution.py:257
  30.2 20.1 %all_to_all.46.arrived_ref = s16[8,4,136,128]{3,2,1,0:T(8,128)(2,1)S(1)} all-to-all(s16[8,4,136,128]{3,2,1,0:T(8,128)(2,1)S(1)} %bitcast.27), channel_id=1, replica_groups=mesh['y'=8,'core'=2,'x'=4,'za'=4,'zb'=2] {'x','zb'}, dimensions={0} | all-to-all | bytes 2228224 | tf_op jit(solution)/shard_map/all_to_all | solution.py:266
  50.3 0.0 copy-start.1
  50.3 0.4 sum_near.3
  50.7 16.2 %all_to_all.47.arrived_ref = s16[4,136,128]{2,1,0:T(8,128)(2,1)S(1)} all-to-all(s16[4,136,128]{2,1,0:T(8,128)(2,1)S(1)} %sum_near.3), channel_id=1, replica_groups=mesh['y'=8,'core'=2,'x'=4,'za'=4,'zb'=2] {'za'}, dimensions={0} | all-to-all | bytes 278528 | tf_op jit(solution)/shard_map/all_to_all | solution.py:275
  66.9 0.0 copy-done.1
  66.9 0.2 solve.2
  67.2 11.8 %all_to_all.48 = bf16[8,2,64,128]{3,2,1,0:T(8,128)(2,1)S(1)} all-to-all(bf16[8,2,64,128]{3,2,1,0:T(8,128)(2,1)S(1)} %get-tuple-element.27), channel_id=1, replica_groups=mesh['y'=8,'core'=2,'x'=4,'za'=4,'zb'=2] {'y'}, dimensions={0} | all-to-all | bytes 524288 | tf_op jit(solution)/shard_map/all_to_all | solution.py:253
  79.0 2.9 %local_terms.4 = s16[32,136,128]{2,1,0:T(8,128)(2,1)S(1)} custom-call(s32[6,2,32]{2,1,0:T(2,128)} %bitcast.42, s32[16,128]{1,0:T(8,128)S(1)} %get-tuple-element.22.other_table, bf16[6,32,64,128]{3,2,1,0:T(8,128)(2,1)S(1)} %bitcast.19, bf16[6,32,64,128]{3,2,1,0:T(8,128)(2,1)S(1)} %collective-permute-done.refs_1_, bf16[16,64,128]{2,1,0:T(8,128)(2,1)S(1)} %bitcast.29, ...), custom_call_target="tpu_custom_call" | custom-call | tf_op jit(solution)/shard_map/local_terms/pallas_call | solution.py:257
  82.0 14.0 %all_to_all.49.arrived_ref = s16[8,4,136,128]{3,2,1,0:T(8,128)(2,1)S(1)} all-to-all(s16[8,4,136,128]{3,2,1,0:T(8,128)(2,1)S(1)} %bitcast.26), channel_id=1, replica_groups=mesh['y'=8,'core'=2,'x'=4,'za'=4,'zb'=2] {'x','zb'}, dimensions={0} | all-to-all | bytes 2228224 | tf_op jit(solution)/shard_map/all_to_all | solution.py:266
  96.0 0.4 sum_near.4
  96.4 10.1 %all_to_all.50.arrived_ref = s16[4,136,128]{2,1,0:T(8,128)(2,1)S(1)} all-to-all(s16[4,136,128]{2,1,0:T(8,128)(2,1)S(1)} %sum_near.4), channel_id=1, replica_groups=mesh['y'=8,'core'=2,'x'=4,'za'=4,'zb'=2] {'za'}, dimensions={0} | all-to-all | bytes 278528 | tf_op jit(solution)/shard_map/all_to_all | solution.py:275
  106.5 0.2 solve.3
  106.8 11.7 %all_to_all.51 = bf16[8,2,64,128]{3,2,1,0:T(8,128)(2,1)S(1)} all-to-all(bf16[8,2,64,128]{3,2,1,0:T(8,128)(2,1)S(1)} %get-tuple-element.28), channel_id=1, replica_groups=mesh['y'=8,'core'=2,'x'=4,'za'=4,'zb'=2] {'y'}, dimensions={0} | all-to-all | bytes 524288 | tf_op jit(solution)/shard_map/all_to_all | solution.py:253
  118.5 3.8 %local_terms.5 = s16[32,136,128]{2,1,0:T(8,128)(2,1)S(1)} custom-call(s32[6,2,32]{2,1,0:T(2,128)} %bitcast.43, s32[16,128]{1,0:T(8,128)S(1)} %get-tuple-element.22.other_table, bf16[6,32,64,128]{3,2,1,0:T(8,128)(2,1)S(1)} %bitcast.20, bf16[6,32,64,128]{3,2,1,0:T(8,128)(2,1)S(1)} %collective-permute-done.refs_1_, bf16[16,64,128]{2,1,0:T(8,128)(2,1)S(1)} %bitcast.30, ...), custom_call_target="tpu_custom_call" | custom-call | tf_op jit(solution)/shard_map/local_terms/pallas_call | solution.py:257
  122.3 13.7 %all_to_all.52.arrived_ref = s16[8,4,136,128]{3,2,1,0:T(8,128)(2,1)S(1)} all-to-all(s16[8,4,136,128]{3,2,1,0:T(8,128)(2,1)S(1)} %bitcast.25), channel_id=1, replica_groups=mesh['y'=8,'core'=2,'x'=4,'za'=4,'zb'=2] {'x','zb'}, dimensions={0} | all-to-all | bytes 2228224 | tf_op jit(solution)/shard_map/all_to_all | solution.py:266
  136.0 0.4 sum_near.5
  136.4 10.0 %all_to_all.53.arrived_ref = s16[4,136,128]{2,1,0:T(8,128)(2,1)S(1)} all-to-all(s16[4,136,128]{2,1,0:T(8,128)(2,1)S(1)} %sum_near.5), channel_id=1, replica_groups=mesh['y'=8,'core'=2,'x'=4,'za'=4,'zb'=2] {'za'}, dimensions={0} | all-to-all | bytes 278528 | tf_op jit(solution)/shard_map/all_to_all | solution.py:275
  146.5 0.2 solve_last.1
  146.7 13.2 %all-gather.1 = f32[6,64,128]{2,1,0:T(8,128)S(1)} all-gather(f32[3,64,128]{2,1,0:T(8,128)S(1)} %get-tuple-element.32), channel_id=3, replica_groups=mesh['y'=8,'core'=2,'x'=4,'za'=4,'zb'=2] {'core'}, dimensions={0}, use_global_device_ids=true | all-gather | bytes 294912 | tf_op jit(solution)/shard_map/all_gather | solution.py:296
  159.9 0.7 join.1
  (1 shorter events, 0.0 us)
Async XLA Ops:
  0.0 10.8 %copy-start = (bf16[6,1,1,32,64,128]{5,4,3,2,1,0:T(8,128)(2,1)S(1)}, bf16[6,1,1,32,64,128]{5,4,3,2,1,0:T(8,128)(2,1)}, u32[]{:S(2)}) copy-start(bf16[6,1,1,32,64,128]{5,4,3,2,1,0:T(8,128)(2,1)} %param.6) | copy-start | bytes 9437188
  10.9 17.1 %collective-permute-start = (bf16[6,32,64,128]{3,2,1,0:T(8,128)(2,1)S(1)}, bf16[6,32,64,128]{3,2,1,0:T(8,128)(2,1)S(1)}, u32[]{:S(2)}, u32[]{:S(2)}) collective-permute-start(bf16[6,32,64,128]{3,2,1,0:T(8,128)(2,1)S(1)} %bitcast.18), channel_id=1, source_target_pairs={{0,32},{32,0},{1,33},{33,1},{2,34},{34,2},{3,35},{35,3},{4,36},{36... | collective-permute-start | bytes 9437192 | tf_op jit(solution)/shard_map/ppermute | solution.py:249
  50.3 16.6 %copy-start.1 = (f32[4,1,1,64,64]{4,3,2,1,0:T(8,128)S(1)}, f32[4,1,1,64,64]{4,3,2,1,0:T(8,128)}, u32[]{:S(2)}) copy-start(f32[4,1,1,64,64]{4,3,2,1,0:T(8,128)} %param.5) | copy-start | bytes 196612

commit v8 on v7

--- a/solution.py
+++ b/solution.py
@@ -31,7 +31,7 @@
         rows = part.shape[0]
         largest = jnp.max(jnp.abs(part), axis=0, keepdims=True)
         power = jnp.ceil(jnp.log2(jnp.maximum(largest * 1.001, 1e-30)))
-        coded = jnp.floor(part * jnp.exp2(15.0 - power) + 0.5).astype(jnp.int32)
+        coded = jnp.round(part * jnp.exp2(15.0 - power)).astype(jnp.int32)
         out_ref[index, side * rows : (side + 1) * rows, :] = coded.astype(jnp.int16)
         powers.append(jnp.broadcast_to(power, (PAD // len(parts), LANES)))
     powers = jnp.concatenate(powers, axis=0).astype(jnp.int32)
@@ -99,24 +99,37 @@
     early.wait()
 
 
-def spread_kernel(mine_ref, swapped_ref, copies_ref, table_ref):
+def spread_kernel(mine_ref, swapped_ref, sources_ref, copies_ref, table_ref):
+    core = lax.axis_index("core")
     block_rows = mine_ref.shape[1]
-    other = swapped_ref.at[1 - lax.axis_index("core")]
+    other = swapped_ref.at[1 - core]
     blocks = mine_ref[0], other[0:block_rows, :].astype(jnp.bfloat16)
     for side, block in enumerate(blocks):
         for peer in range(copies_ref.shape[0]):
             copies_ref[peer, side] = block
-    rows = table_ref.shape[0]
-    table_ref[...] = other[other.shape[0] - rows :, :].astype(jnp.int32)
-
-
-def terms_kernel(pairs, z_sizes, own_table, other_table, *refs):
-    lowers, gathered, out_ref = refs[:SIDES], refs[SIDES:-1], refs[-1]
-    core = lax.axis_index("core")
+    none = SIDES * copies_ref.shape[0]
+
+    def places(sources):
+        return jnp.where(sources >= 0, jnp.bitwise_xor(sources, core), none)
+
+    pairs, per, targets = sources_ref.shape
+    rows = table_ref.shape[1]
+    table_ref[0] = jnp.zeros(table_ref.shape[1:], jnp.int32)
+    for pair in range(pairs):
+        table_ref[0, pair * per : (pair + 1) * per, 0:targets] = places(sources_ref[pair])
+    table_ref[1] = places(other[other.shape[0] - rows :, :].astype(jnp.int32))
+
+
+def terms_kernel(pairs, z_sizes, table_ref, *refs):
+    lowers, gathered, (out_ref, blocks_ref) = refs[:SIDES], refs[SIDES:-2], refs[-2:]
     _, targets, block_rows, depth = lowers[0].shape
     per = depth // block_rows
     za_size, zb_size = z_sizes
     z_size = za_size * zb_size
+    none = blocks_ref.shape[1] - 1
+    for place, block in enumerate(gathered):
+        blocks_ref[place, 0:none] = block[...]
+        blocks_ref[place, none] = jnp.zeros(blocks_ref.shape[2:], blocks_ref.dtype)
 
     def one(target, carry):
         z = lax.rem(target, z_size)
@@ -124,15 +137,10 @@
         parts = []
         for side in range(SIDES):
             factors, picked = [], []
-            for block, pair in zip(gathered, pairs):
+            for place, pair in enumerate(pairs):
                 factors.append(lowers[side][pair, target])
                 for entry in range(per):
-                    if side == 0:
-                        source = own_table[pair, entry, target]
-                    else:
-                        source = other_table[pair * per + entry, target]
-                    rows = block[jnp.bitwise_xor(jnp.maximum(source, 0), core)]
-                    picked.append(jnp.where(source >= 0, rows, jnp.zeros_like(rows)))
+                    picked.append(blocks_ref[place, table_ref[side, pair * per + entry, target]])
             parts.append(
                 jnp.dot(
                     jnp.concatenate(factors, axis=1),
@@ -143,7 +151,7 @@
         encode(parts, out_ref, slot)
         return carry
 
-    lax.fori_loop(0, targets, one, 0, unroll=8)
+    lax.fori_loop(0, targets, one, 0, unroll=True)
 
 
 def middle_kernel(arrived_ref, out_ref):
@@ -239,12 +247,12 @@
     mine = in_vmem(mine)
     copies, table = pl.pallas_call(
         spread_kernel,
-        out_shape=(copies_shape, pltpu.VMEM((table_rows, LANES), jnp.int32)),
-        in_specs=[VMEM] * 2,
+        out_shape=(copies_shape, pltpu.VMEM((SIDES, table_rows, LANES), jnp.int32)),
+        in_specs=[VMEM] * 3,
         out_specs=(VMEM, VMEM),
         compiler_params=PARAMS,
         name="spread",
-    )(mine, swapped)
+    )(mine, swapped, sources)
     copies, lower_sent = lax.optimization_barrier((copies, lower))
     other_lower = lax.ppermute(lower_sent, "core", [(0, 1), (1, 0)])
 
@@ -257,11 +265,14 @@
         coded = pl.pallas_call(
             functools.partial(terms_kernel, pairs, (za_size, zb_size)),
             out_shape=pltpu.VMEM((targets, coded_rows, LANES), jnp.int16),
-            in_specs=[SMEM] * 2 + [VMEM] * (SIDES + len(gathered)),
+            in_specs=[SMEM] + [VMEM] * (SIDES + len(gathered)),
             out_specs=VMEM,
+            scratch_shapes=[
+                pltpu.VMEM((level, y_size * SIDES + 1, block_rows, LANES), jnp.bfloat16)
+            ],
             compiler_params=PARAMS,
             name="local_terms",
-        )(in_hbm(sources), table, in_vmem(own), in_vmem(other_lower), *gathered)
+        )(table, in_vmem(own), in_vmem(other_lower), *gathered)
         coded = coded.reshape(x_size * zb_size, za_size, coded_rows, LANES)
         arrived = lax.all_to_all(coded, ("x", "zb"), split_axis=0, concat_axis=0, tiled=True)
         coded = pl.pallas_call(

time: 161 us -> 158 us (0.981)
  Pallas kernels: 13.8 us -> 10.4 us
    pallas_call x3, Pallas kernels: 9.01 us -> 5.68 us  [on_device(): pl.pallas_call(functools.partial(terms_kernel, pairs, (za_size, zb_size))...]
where the time goes in v8:
time: 158 us; the launch traced here: 157 us
  blocking collectives  144 us (91%)
  Pallas kernels  10.4 us (7%)
  starting transfers between devices  2.28 us (1%)
    all_to_all x3, blocking collectives, on_device(): lax.all_to_all(coded, ('x', 'zb'), split_axis=0, concat_axis=0, tiled=True)  47.9 us
    all_to_all x3, blocking collectives, on_device(): lax.all_to_all(copies, 'y', split_axis=0, concat_axis=0, tiled=True)  38.4 us
    all_to_all x3, blocking collectives, on_device(): lax.all_to_all(coded, 'za', split_axis=0, concat_axis=0, tiled=True)  36.4 us
    all_gather x1, blocking collectives, on_device(): halves = lax.all_gather(parts[1], 'core', axis=0, tiled=False)  13.1 us
    all_gather x1, blocking collectives, on_device(): swapped = in_vmem(lax.all_gather(sent, 'core', axis=0, tiled=False))  8.65 us
    pallas_call x3, Pallas kernels, on_device(): pl.pallas_call(functools.partial(terms_kernel, pairs, (za_size, zb_size))...  5.68 us
  transfers between devices with their start and end apart: 1, of which 0 were waited for; matrix products, arithmetic and copies ran while one was open for 0% of the time, Pallas kernels for 0%

profile of v8, /device:TPU:1, one launch (start us, length us, event | category | flops | bytes accessed | tf_op | source)
XLA Modules:
  0.0 157.2 jit_solution(11406719624549664196)
XLA Ops:
  0.0 0.0 copy-start.2
  0.0 0.0 copy-start
  0.0 2.2 %first.1 = (f32[64,256]{1,0:T(8,128)S(1)}, bf16[4,64,128]{2,1,0:T(8,128)(2,1)S(1)}, f32[464,128]{1,0:T(8,128)S(1)}, bf16[1,32,64,128]{3,2,1,0:T(8,128)(2,1)S(1)}) custom-call(bf16[4,64,256]{2,1,0:T(8,128)(2,1)} %bitcast.41, f32[4,64,64]{2,1,0:T(8,128)} %bitcast.33, bf16[6,32,64,128]{3,2,1,0:T(8,128)(2,1)} %bitcast.17, s32[6,2,32]{2,1,0:T(2,128)} %bitcast.39), custom_call_target="tpu_custom_call" | custom-call | tf_op jit(solution)/shard_map/first/pallas_call | solution.py:228
  2.2 8.7 %all-gather = f32[928,128]{1,0:T(8,128)S(1)} all-gather(f32[464,128]{1,0:T(8,128)S(1)} %get-tuple-element.21), channel_id=2, replica_groups=mesh['y'=8,'core'=2,'x'=4,'za'=4,'zb'=2] {'core'}, dimensions={0}, use_global_device_ids=true | all-gather | bytes 712704 | tf_op jit(solution)/shard_map/all_gather | solution.py:246
  10.8 0.0 copy-done.2
  10.9 0.0 copy-done
  10.9 2.3 %collective-permute-start = (bf16[6,32,64,128]{3,2,1,0:T(8,128)(2,1)S(1)}, bf16[6,32,64,128]{3,2,1,0:T(8,128)(2,1)S(1)}, u32[]{:S(2)}, u32[]{:S(2)}) collective-permute-start(bf16[6,32,64,128]{3,2,1,0:T(8,128)(2,1)S(1)} %bitcast.18), channel_id=1, source_target_pairs={{0,32},{32,0},{1,33},{33,1},{2,34},{34,2},{3,35},{35,3},{4,36},{36... | collective-permute-start | bytes 9437192 | tf_op jit(solution)/shard_map/ppermute | solution.py:257
  13.2 14.8 %all_to_all.45 = bf16[8,2,64,128]{3,2,1,0:T(8,128)(2,1)S(1)} all-to-all(bf16[8,2,64,128]{3,2,1,0:T(8,128)(2,1)S(1)} %get-tuple-element.25), channel_id=1, replica_groups=mesh['y'=8,'core'=2,'x'=4,'za'=4,'zb'=2] {'y'}, dimensions={0} | all-to-all | bytes 524288 | tf_op jit(solution)/shard_map/all_to_all | solution.py:261
  27.9 0.0 collective-permute-done.refs_1_
  28.0 1.6 local_terms.3
  29.5 20.1 %all_to_all.46.arrived_ref = s16[8,4,136,128]{3,2,1,0:T(8,128)(2,1)S(1)} all-to-all(s16[8,4,136,128]{3,2,1,0:T(8,128)(2,1)S(1)} %bitcast.25), channel_id=1, replica_groups=mesh['y'=8,'core'=2,'x'=4,'za'=4,'zb'=2] {'x','zb'}, dimensions={0} | all-to-all | bytes 2228224 | tf_op jit(solution)/shard_map/all_to_all | solution.py:277
  49.6 0.0 copy-start.1
  49.6 0.4 sum_near.3
  50.0 16.2 %all_to_all.47.arrived_ref = s16[4,136,128]{2,1,0:T(8,128)(2,1)S(1)} all-to-all(s16[4,136,128]{2,1,0:T(8,128)(2,1)S(1)} %sum_near.3), channel_id=1, replica_groups=mesh['y'=8,'core'=2,'x'=4,'za'=4,'zb'=2] {'za'}, dimensions={0} | all-to-all | bytes 278528 | tf_op jit(solution)/shard_map/all_to_all | solution.py:286
  66.2 0.0 copy-done.1
  66.2 0.2 solve.2
  66.5 11.8 %all_to_all.48 = bf16[8,2,64,128]{3,2,1,0:T(8,128)(2,1)S(1)} all-to-all(bf16[8,2,64,128]{3,2,1,0:T(8,128)(2,1)S(1)} %get-tuple-element.27), channel_id=1, replica_groups=mesh['y'=8,'core'=2,'x'=4,'za'=4,'zb'=2] {'y'}, dimensions={0} | all-to-all | bytes 524288 | tf_op jit(solution)/shard_map/all_to_all | solution.py:261
  78.3 1.9 %local_terms.4 = s16[32,136,128]{2,1,0:T(8,128)(2,1)S(1)} custom-call(s32[2,16,128]{2,1,0:T(8,128)S(1)} %get-tuple-element.22.table_ref, bf16[6,32,64,128]{3,2,1,0:T(8,128)(2,1)S(1)} %bitcast.19, bf16[6,32,64,128]{3,2,1,0:T(8,128)(2,1)S(1)} %collective-permute-done.refs_1_, bf16[16,64,128]{2,1,0:T(8,128)(2,1)S(1)} %bitcast.29, bf16[16,64,128]{2,1,0:T(8,128)(2,1)S(1)} %bitcast.31), custom_call_target="tpu_custom_call" | custom-call | tf_op jit(solution)/shard_map/local_terms/pallas_call | solution.py:265
  80.2 14.0 %all_to_all.49.arrived_ref = s16[8,4,136,128]{3,2,1,0:T(8,128)(2,1)S(1)} all-to-all(s16[8,4,136,128]{3,2,1,0:T(8,128)(2,1)S(1)} %bitcast.27), channel_id=1, replica_groups=mesh['y'=8,'core'=2,'x'=4,'za'=4,'zb'=2] {'x','zb'}, dimensions={0} | all-to-all | bytes 2228224 | tf_op jit(solution)/shard_map/all_to_all | solution.py:277
  94.2 0.4 sum_near.4
  94.5 10.1 %all_to_all.50.arrived_ref = s16[4,136,128]{2,1,0:T(8,128)(2,1)S(1)} all-to-all(s16[4,136,128]{2,1,0:T(8,128)(2,1)S(1)} %sum_near.4), channel_id=1, replica_groups=mesh['y'=8,'core'=2,'x'=4,'za'=4,'zb'=2] {'za'}, dimensions={0} | all-to-all | bytes 278528 | tf_op jit(solution)/shard_map/all_to_all | solution.py:286
  104.7 0.2 solve.3
  104.9 11.7 %all_to_all.51 = bf16[8,2,64,128]{3,2,1,0:T(8,128)(2,1)S(1)} all-to-all(bf16[8,2,64,128]{3,2,1,0:T(8,128)(2,1)S(1)} %get-tuple-element.28), channel_id=1, replica_groups=mesh['y'=8,'core'=2,'x'=4,'za'=4,'zb'=2] {'y'}, dimensions={0} | all-to-all | bytes 524288 | tf_op jit(solution)/shard_map/all_to_all | solution.py:261
  116.7 2.3 %local_terms.5 = s16[32,136,128]{2,1,0:T(8,128)(2,1)S(1)} custom-call(s32[2,16,128]{2,1,0:T(8,128)S(1)} %get-tuple-element.22.table_ref, bf16[6,32,64,128]{3,2,1,0:T(8,128)(2,1)S(1)} %bitcast.20, bf16[6,32,64,128]{3,2,1,0:T(8,128)(2,1)S(1)} %collective-permute-done.refs_1_, bf16[16,64,128]{2,1,0:T(8,128)(2,1)S(1)} %bitcast.30, ...), custom_call_target="tpu_custom_call" | custom-call | tf_op jit(solution)/shard_map/local_terms/pallas_call | solution.py:265
  119.0 13.8 %all_to_all.52.arrived_ref = s16[8,4,136,128]{3,2,1,0:T(8,128)(2,1)S(1)} all-to-all(s16[8,4,136,128]{3,2,1,0:T(8,128)(2,1)S(1)} %bitcast.26), channel_id=1, replica_groups=mesh['y'=8,'core'=2,'x'=4,'za'=4,'zb'=2] {'x','zb'}, dimensions={0} | all-to-all | bytes 2228224 | tf_op jit(solution)/shard_map/all_to_all | solution.py:277
  132.8 0.4 sum_near.5
  133.1 10.0 %all_to_all.53.arrived_ref = s16[4,136,128]{2,1,0:T(8,128)(2,1)S(1)} all-to-all(s16[4,136,128]{2,1,0:T(8,128)(2,1)S(1)} %sum_near.5), channel_id=1, replica_groups=mesh['y'=8,'core'=2,'x'=4,'za'=4,'zb'=2] {'za'}, dimensions={0} | all-to-all | bytes 278528 | tf_op jit(solution)/shard_map/all_to_all | solution.py:286
  143.2 0.2 solve_last.1
  143.4 13.1 %all-gather.1 = f32[6,64,128]{2,1,0:T(8,128)S(1)} all-gather(f32[3,64,128]{2,1,0:T(8,128)S(1)} %get-tuple-element.32), channel_id=3, replica_groups=mesh['y'=8,'core'=2,'x'=4,'za'=4,'zb'=2] {'core'}, dimensions={0}, use_global_device_ids=true | all-gather | bytes 294912 | tf_op jit(solution)/shard_map/all_gather | solution.py:307
  156.5 0.7 join.1
  (1 shorter events, 0.0 us)
Async XLA Ops:
  0.0 10.8 %copy-start.2 = (s32[6,1,1,32,2]{3,4,2,1,0:T(2,128)S(1)}, s32[6,1,1,32,2]{3,4,2,1,0:T(2,128)}, u32[]{:S(2)}) copy-start(s32[6,1,1,32,2]{3,4,2,1,0:T(2,128)} %param.7) | copy-start | bytes 4612
  0.0 10.9 %copy-start = (bf16[6,1,1,32,64,128]{5,4,3,2,1,0:T(8,128)(2,1)S(1)}, bf16[6,1,1,32,64,128]{5,4,3,2,1,0:T(8,128)(2,1)}, u32[]{:S(2)}) copy-start(bf16[6,1,1,32,64,128]{5,4,3,2,1,0:T(8,128)(2,1)} %param.6) | copy-start | bytes 9437188
  10.9 17.1 %collective-permute-start = (bf16[6,32,64,128]{3,2,1,0:T(8,128)(2,1)S(1)}, bf16[6,32,64,128]{3,2,1,0:T(8,128)(2,1)S(1)}, u32[]{:S(2)}, u32[]{:S(2)}) collective-permute-start(bf16[6,32,64,128]{3,2,1,0:T(8,128)(2,1)S(1)} %bitcast.18), channel_id=1, source_target_pairs={{0,32},{32,0},{1,33},{33,1},{2,34},{34,2},{3,35},{35,3},{4,36},{36... | collective-permute-start | bytes 9437192 | tf_op jit(solution)/shard_map/ppermute | solution.py:257
  49.6 16.6 %copy-start.1 = (f32[4,1,1,64,64]{4,3,2,1,0:T(8,128)S(1)}, f32[4,1,1,64,64]{4,3,2,1,0:T(8,128)}, u32[]{:S(2)}) copy-start(f32[4,1,1,64,64]{4,3,2,1,0:T(8,128)} %param.5) | copy-start | bytes 196612

commit v9 on v8

--- a/solution.py
+++ b/solution.py
@@ -15,6 +15,30 @@
 SMEM = pl.BlockSpec(memory_space=pltpu.SMEM)
 ANY = pl.BlockSpec(memory_space=pl.ANY)
 PARAMS = pltpu.CompilerParams(vmem_limit_bytes=KERNEL_VMEM)
+
+
+MESH_AXES = ("y", "core", "x", "z")
+NEAR_Z = 2
+
+
+def exchange_groups(sizes):
+    y_size, cores, x_size, z_size = sizes
+    far = z_size // NEAR_Z
+    near_first = [[(x, f * NEAR_Z + n) for x in range(x_size) for n in range(NEAR_Z)] for f in range(far)]
+    far_last = [[(x, f * NEAR_Z + n) for f in range(far)] for x in range(x_size) for n in range(NEAR_Z)]
+    z_first = [[(x, z) for z in range(z_size)] for x in range(x_size)]
+    x_last = [[(x, z) for x in range(x_size)] for z in range(z_size)]
+    stages = []
+    for plans in ((near_first, z_first), (far_last, x_last)):
+        stages.append(
+            [
+                [((y * cores + core) * x_size + x) * z_size + z for x, z in group]
+                for y in range(y_size)
+                for core in range(cores)
+                for group in plans[core]
+            ]
+        )
+    return stages
 
 
 def in_vmem(array):
@@ -120,12 +144,13 @@
     table_ref[1] = places(other[other.shape[0] - rows :, :].astype(jnp.int32))
 
 
-def terms_kernel(pairs, z_sizes, table_ref, *refs):
+def terms_kernel(pairs, x_size, table_ref, *refs):
     lowers, gathered, (out_ref, blocks_ref) = refs[:SIDES], refs[SIDES:-2], refs[-2:]
     _, targets, block_rows, depth = lowers[0].shape
     per = depth // block_rows
-    za_size, zb_size = z_sizes
-    z_size = za_size * zb_size
+    z_size = targets // x_size
+    far = z_size // NEAR_Z
+    near_first = lax.axis_index("core") == 0
     none = blocks_ref.shape[1] - 1
     for place, block in enumerate(gathered):
         blocks_ref[place, 0:none] = block[...]
@@ -133,7 +158,8 @@
 
     def one(target, carry):
         z = lax.rem(target, z_size)
-        slot = target - z + lax.rem(z, zb_size) * za_size + lax.div(z, zb_size)
+        near_slot = target - z + lax.rem(z, NEAR_Z) * far + lax.div(z, NEAR_Z)
+        slot = jnp.where(near_first, near_slot, z * x_size + lax.div(target, z_size))
         parts = []
         for side in range(SIDES):
             factors, picked = [], []
@@ -212,7 +238,16 @@
 
 def on_device(rhs, dinv, lower, sources):
     levels, _, _, block_rows, width = rhs.shape
-    y_size, x_size, za_size, zb_size = (lax.axis_size(name) for name in ("y", "x", "za", "zb"))
+    sizes = tuple(lax.axis_size(name) for name in MESH_AXES)
+    y_size, _, x_size, _ = sizes
+    first_groups, second_groups = exchange_groups(sizes)
+    first_peers, second_peers = len(first_groups[0]), len(second_groups[0])
+
+    def exchange(array, groups):
+        return lax.all_to_all(
+            array, MESH_AXES, split_axis=0, concat_axis=0, axis_index_groups=groups, tiled=True
+        )
+
     pair_of = {}
     for section in range(levels):
         for target in range(section + 1, levels):
@@ -263,7 +298,7 @@
         pairs = tuple(pair_of[earlier, level] for earlier in range(level))
         own = early if level == 1 else lower
         coded = pl.pallas_call(
-            functools.partial(terms_kernel, pairs, (za_size, zb_size)),
+            functools.partial(terms_kernel, pairs, x_size),
             out_shape=pltpu.VMEM((targets, coded_rows, LANES), jnp.int16),
             in_specs=[SMEM] + [VMEM] * (SIDES + len(gathered)),
             out_specs=VMEM,
@@ -273,17 +308,17 @@
             compiler_params=PARAMS,
             name="local_terms",
         )(table, in_vmem(own), in_vmem(other_lower), *gathered)
-        coded = coded.reshape(x_size * zb_size, za_size, coded_rows, LANES)
-        arrived = lax.all_to_all(coded, ("x", "zb"), split_axis=0, concat_axis=0, tiled=True)
+        coded = coded.reshape(first_peers, second_peers, coded_rows, LANES)
+        arrived = exchange(coded, first_groups)
         coded = pl.pallas_call(
             middle_kernel,
-            out_shape=pltpu.VMEM((za_size, coded_rows, LANES), jnp.int16),
+            out_shape=pltpu.VMEM((second_peers, coded_rows, LANES), jnp.int16),
             in_specs=[VMEM],
             out_specs=VMEM,
             compiler_params=PARAMS,
-            name="sum_near",
+            name="sum_first",
         )(in_vmem(arrived))
-        arrived = lax.all_to_all(coded, "za", split_axis=0, concat_axis=0, tiled=True)
+        arrived = exchange(coded, second_groups)
         operands = [mine, swapped] + [in_vmem(array) for array in (dinv, arrived)]
         if level + 1 < levels:
             solution, copies = pl.pallas_call(
@@ -318,8 +353,8 @@
 
 
 def solution(mesh):
-    split = Mesh(mesh.devices.reshape(8, 2, 4, 4, 2), ("y", "core", "x", "za", "zb"))
-    row, col = ("y", "core"), ("x", "za", "zb")
+    split = Mesh(mesh.devices.reshape(8, 2, 4, 8), MESH_AXES)
+    row, col = MESH_AXES[:2], MESH_AXES[2:]
     in_specs = (
         P(None, row, col, None, None),
         P(None, row, col, None, None),

time: 158 us -> 175 us (1.11)
  blocking collectives: 144 us -> 162 us
    all_to_all x6, blocking collectives: 84.3 us -> 106 us  [exchange(): lax.all_to_all(array, MESH_AXES, split_axis=0, concat_axis=0, axis_index_...]
    all_gather x1, blocking collectives: 13.1 us -> 8.69 us  [on_device(): halves = lax.all_gather(parts[1], 'core', axis=0, tiled=False)]
where the time goes in v9:
time: 175 us
  blocking collectives  162 us (93%)
  Pallas kernels  10.4 us (6%)
  starting transfers between devices  2.28 us (1%)
    all_to_all x6, blocking collectives, exchange(): lax.all_to_all(array, MESH_AXES, split_axis=0, concat_axis=0, axis_index_...  106 us
    all_to_all x3, blocking collectives, on_device(): lax.all_to_all(copies, 'y', split_axis=0, concat_axis=0, tiled=True)  38.3 us
    all_gather x1, blocking collectives, on_device(): halves = lax.all_gather(parts[1], 'core', axis=0, tiled=False)  8.69 us
    all_gather x1, blocking collectives, on_device(): swapped = in_vmem(lax.all_gather(sent, 'core', axis=0, tiled=False))  8.65 us
    pallas_call x3, Pallas kernels, on_device(): pl.pallas_call(functools.partial(terms_kernel, pairs, x_size), out_shape=...  5.67 us
  transfers between devices with their start and end apart: 1, of which 0 were waited for; matrix products, arithmetic and copies ran while one was open for 0% of the time, Pallas kernels for 0%

profile of v9, /device:TPU:1, one launch (start us, length us, event | category | flops | bytes accessed | tf_op | source)
XLA Modules:
  0.0 174.6 jit_solution(11876003998799418983)
XLA Ops:
  0.0 0.0 copy-start.2
  0.0 0.0 copy-start
  0.0 2.2 %first.1 = (f32[64,256]{1,0:T(8,128)S(1)}, bf16[4,64,128]{2,1,0:T(8,128)(2,1)S(1)}, f32[464,128]{1,0:T(8,128)S(1)}, bf16[1,32,64,128]{3,2,1,0:T(8,128)(2,1)S(1)}) custom-call(bf16[4,64,256]{2,1,0:T(8,128)(2,1)} %bitcast.41, f32[4,64,64]{2,1,0:T(8,128)} %bitcast.33, bf16[6,32,64,128]{3,2,1,0:T(8,128)(2,1)} %bitcast.17, s32[6,2,32]{2,1,0:T(2,128)} %bitcast.39), custom_call_target="tpu_custom_call" | custom-call | tf_op jit(solution)/shard_map/first/pallas_call | solution.py:263
  2.2 8.7 %all-gather = f32[928,128]{1,0:T(8,128)S(1)} all-gather(f32[464,128]{1,0:T(8,128)S(1)} %get-tuple-element.21), channel_id=2, replica_groups=mesh['y'=8,'core'=2,'x'=4,'z'=8] {'core'}, dimensions={0}, use_global_device_ids=true | all-gather | bytes 712704 | tf_op jit(solution)/shard_map/all_gather | solution.py:281
  10.8 0.0 copy-done.2
  10.9 0.0 copy-done
  10.9 2.3 %collective-permute-start = (bf16[6,32,64,128]{3,2,1,0:T(8,128)(2,1)S(1)}, bf16[6,32,64,128]{3,2,1,0:T(8,128)(2,1)S(1)}, u32[]{:S(2)}, u32[]{:S(2)}) collective-permute-start(bf16[6,32,64,128]{3,2,1,0:T(8,128)(2,1)S(1)} %bitcast.18), channel_id=1, source_target_pairs={{0,32},{32,0},{1,33},{33,1},{2,34},{34,2},{3,35},{35,3},{4,36},{36... | collective-permute-start | bytes 9437192 | tf_op jit(solution)/shard_map/ppermute | solution.py:292
  13.2 14.8 %all_to_all.45 = bf16[8,2,64,128]{3,2,1,0:T(8,128)(2,1)S(1)} all-to-all(bf16[8,2,64,128]{3,2,1,0:T(8,128)(2,1)S(1)} %get-tuple-element.25), channel_id=1, replica_groups=mesh['y'=8,'core'=2,'x'=4,'z'=8] {'y'}, dimensions={0} | all-to-all | bytes 524288 | tf_op jit(solution)/shard_map/all_to_all | solution.py:296
  27.9 0.0 collective-permute-done.refs_1_
  28.0 1.6 local_terms.3
  29.5 32.3 %all_to_all.46.arrived_ref = s16[8,4,136,128]{3,2,1,0:T(8,128)(2,1)S(1)} all-to-all(s16[8,4,136,128]{3,2,1,0:T(8,128)(2,1)S(1)} %bitcast.25), channel_id=1, replica_groups={{0,1,8,9,16,17,24,25},{2,3,10,11,18,19,26,27},{4,5,12,13,20,21,28,29},{..., dimensions={0} | all-to-all | bytes 2228224 | tf_op jit(solution)/shard_map/all_to_all | solution.py:247
  61.8 0.0 copy-start.1
  61.8 0.4 sum_first.3
  62.2 9.2 %all_to_all.47.arrived_ref = s16[4,136,128]{2,1,0:T(8,128)(2,1)S(1)} all-to-all(s16[4,136,128]{2,1,0:T(8,128)(2,1)S(1)} %sum_first.3), channel_id=1, replica_groups={{0,2,4,6},{1,3,5,7},{8,10,12,14},{9,11,13,15},{16,18,20,22},{17,19,21,2..., dimensions={0} | all-to-all | bytes 278528 | tf_op jit(solution)/shard_map/all_to_all | solution.py:247
  71.3 0.0 copy-done.1
  71.3 0.2 solve.2
  71.6 11.7 %all_to_all.48 = bf16[8,2,64,128]{3,2,1,0:T(8,128)(2,1)S(1)} all-to-all(bf16[8,2,64,128]{3,2,1,0:T(8,128)(2,1)S(1)} %get-tuple-element.27), channel_id=1, replica_groups=mesh['y'=8,'core'=2,'x'=4,'z'=8] {'y'}, dimensions={0} | all-to-all | bytes 524288 | tf_op jit(solution)/shard_map/all_to_all | solution.py:296
  83.3 1.8 %local_terms.4 = s16[32,136,128]{2,1,0:T(8,128)(2,1)S(1)} custom-call(s32[2,16,128]{2,1,0:T(8,128)S(1)} %get-tuple-element.22.table_ref, bf16[6,32,64,128]{3,2,1,0:T(8,128)(2,1)S(1)} %bitcast.19, bf16[6,32,64,128]{3,2,1,0:T(8,128)(2,1)S(1)} %collective-permute-done.refs_1_, bf16[16,64,128]{2,1,0:T(8,128)(2,1)S(1)} %bitcast.29, bf16[16,64,128]{2,1,0:T(8,128)(2,1)S(1)} %bitcast.31), custom_call_target="tpu_custom_call" | custom-call | tf_op jit(solution)/shard_map/local_terms/pallas_call | solution.py:300
  85.2 25.7 %all_to_all.49.arrived_ref = s16[8,4,136,128]{3,2,1,0:T(8,128)(2,1)S(1)} all-to-all(s16[8,4,136,128]{3,2,1,0:T(8,128)(2,1)S(1)} %bitcast.27), channel_id=1, replica_groups={{0,1,8,9,16,17,24,25},{2,3,10,11,18,19,26,27},{4,5,12,13,20,21,28,29},{..., dimensions={0} | all-to-all | bytes 2228224 | tf_op jit(solution)/shard_map/all_to_all | solution.py:247
  110.9 0.4 sum_first.4
  111.3 7.3 %all_to_all.50.arrived_ref = s16[4,136,128]{2,1,0:T(8,128)(2,1)S(1)} all-to-all(s16[4,136,128]{2,1,0:T(8,128)(2,1)S(1)} %sum_first.4), channel_id=1, replica_groups={{0,2,4,6},{1,3,5,7},{8,10,12,14},{9,11,13,15},{16,18,20,22},{17,19,21,2..., dimensions={0} | all-to-all | bytes 278528 | tf_op jit(solution)/shard_map/all_to_all | solution.py:247
  118.5 0.2 solve.3
  118.8 11.7 %all_to_all.51 = bf16[8,2,64,128]{3,2,1,0:T(8,128)(2,1)S(1)} all-to-all(bf16[8,2,64,128]{3,2,1,0:T(8,128)(2,1)S(1)} %get-tuple-element.28), channel_id=1, replica_groups=mesh['y'=8,'core'=2,'x'=4,'z'=8] {'y'}, dimensions={0} | all-to-all | bytes 524288 | tf_op jit(solution)/shard_map/all_to_all | solution.py:296
  130.5 2.3 %local_terms.5 = s16[32,136,128]{2,1,0:T(8,128)(2,1)S(1)} custom-call(s32[2,16,128]{2,1,0:T(8,128)S(1)} %get-tuple-element.22.table_ref, bf16[6,32,64,128]{3,2,1,0:T(8,128)(2,1)S(1)} %bitcast.20, bf16[6,32,64,128]{3,2,1,0:T(8,128)(2,1)S(1)} %collective-permute-done.refs_1_, bf16[16,64,128]{2,1,0:T(8,128)(2,1)S(1)} %bitcast.30, ...), custom_call_target="tpu_custom_call" | custom-call | tf_op jit(solution)/shard_map/local_terms/pallas_call | solution.py:300
  132.8 24.6 %all_to_all.52.arrived_ref = s16[8,4,136,128]{3,2,1,0:T(8,128)(2,1)S(1)} all-to-all(s16[8,4,136,128]{3,2,1,0:T(8,128)(2,1)S(1)} %bitcast.26), channel_id=1, replica_groups={{0,1,8,9,16,17,24,25},{2,3,10,11,18,19,26,27},{4,5,12,13,20,21,28,29},{..., dimensions={0} | all-to-all | bytes 2228224 | tf_op jit(solution)/shard_map/all_to_all | solution.py:247
  157.4 0.4 sum_first.5
  157.7 7.3 %all_to_all.53.arrived_ref = s16[4,136,128]{2,1,0:T(8,128)(2,1)S(1)} all-to-all(s16[4,136,128]{2,1,0:T(8,128)(2,1)S(1)} %sum_first.5), channel_id=1, replica_groups={{0,2,4,6},{1,3,5,7},{8,10,12,14},{9,11,13,15},{16,18,20,22},{17,19,21,2..., dimensions={0} | all-to-all | bytes 278528 | tf_op jit(solution)/shard_map/all_to_all | solution.py:247
  165.0 0.2 solve_last.1
  165.2 8.7 %all-gather.1 = f32[6,64,128]{2,1,0:T(8,128)S(1)} all-gather(f32[3,64,128]{2,1,0:T(8,128)S(1)} %get-tuple-element.32), channel_id=3, replica_groups=mesh['y'=8,'core'=2,'x'=4,'z'=8] {'core'}, dimensions={0}, use_global_device_ids=true | all-gather | bytes 294912 | tf_op jit(solution)/shard_map/all_gather | solution.py:342
  173.9 0.7 join.1
  (1 shorter events, 0.0 us)
Async XLA Ops:
  0.0 10.8 %copy-start.2 = (s32[6,1,1,32,2]{3,4,2,1,0:T(2,128)S(1)}, s32[6,1,1,32,2]{3,4,2,1,0:T(2,128)}, u32[]{:S(2)}) copy-start(s32[6,1,1,32,2]{3,4,2,1,0:T(2,128)} %param.7) | copy-start | bytes 4612
  0.0 10.9 %copy-start = (bf16[6,1,1,32,64,128]{5,4,3,2,1,0:T(8,128)(2,1)S(1)}, bf16[6,1,1,32,64,128]{5,4,3,2,1,0:T(8,128)(2,1)}, u32[]{:S(2)}) copy-start(bf16[6,1,1,32,64,128]{5,4,3,2,1,0:T(8,128)(2,1)} %param.6) | copy-start | bytes 9437188
  10.9 17.1 %collective-permute-start = (bf16[6,32,64,128]{3,2,1,0:T(8,128)(2,1)S(1)}, bf16[6,32,64,128]{3,2,1,0:T(8,128)(2,1)S(1)}, u32[]{:S(2)}, u32[]{:S(2)}) collective-permute-start(bf16[6,32,64,128]{3,2,1,0:T(8,128)(2,1)S(1)} %bitcast.18), channel_id=1, source_target_pairs={{0,32},{32,0},{1,33},{33,1},{2,34},{34,2},{3,35},{35,3},{4,36},{36... | collective-permute-start | bytes 9437192 | tf_op jit(solution)/shard_map/ppermute | solution.py:292
  61.8 9.6 %copy-start.1 = (f32[4,1,1,64,64]{4,3,2,1,0:T(8,128)S(1)}, f32[4,1,1,64,64]{4,3,2,1,0:T(8,128)}, u32[]{:S(2)}) copy-start(f32[4,1,1,64,64]{4,3,2,1,0:T(8,128)} %param.5) | copy-start | bytes 196612

commit v10 on v9

--- a/solution.py
+++ b/solution.py
@@ -24,21 +24,20 @@
 def exchange_groups(sizes):
     y_size, cores, x_size, z_size = sizes
     far = z_size // NEAR_Z
-    near_first = [[(x, f * NEAR_Z + n) for x in range(x_size) for n in range(NEAR_Z)] for f in range(far)]
-    far_last = [[(x, f * NEAR_Z + n) for f in range(far)] for x in range(x_size) for n in range(NEAR_Z)]
-    z_first = [[(x, z) for z in range(z_size)] for x in range(x_size)]
-    x_last = [[(x, z) for x in range(x_size)] for z in range(z_size)]
-    stages = []
-    for plans in ((near_first, z_first), (far_last, x_last)):
-        stages.append(
-            [
-                [((y * cores + core) * x_size + x) * z_size + z for x, z in group]
-                for y in range(y_size)
-                for core in range(cores)
-                for group in plans[core]
-            ]
-        )
-    return stages
+    first, second = [], []
+    for y in range(y_size):
+        for core in range(cores):
+
+            def device(x, f, n):
+                z = (f * NEAR_Z + n + core) % z_size
+                return ((y * cores + core) * x_size + x) * z_size + z
+
+            for f in range(far):
+                first.append([device(x, f, n) for x in range(x_size) for n in range(NEAR_Z)])
+            for x in range(x_size):
+                for n in range(NEAR_Z):
+                    second.append([device(x, f, n) for f in range(far)])
+    return first, second
 
 
 def in_vmem(array):
@@ -150,16 +149,16 @@
     per = depth // block_rows
     z_size = targets // x_size
     far = z_size // NEAR_Z
-    near_first = lax.axis_index("core") == 0
+    core = lax.axis_index("core")
     none = blocks_ref.shape[1] - 1
     for place, block in enumerate(gathered):
         blocks_ref[place, 0:none] = block[...]
         blocks_ref[place, none] = jnp.zeros(blocks_ref.shape[2:], blocks_ref.dtype)
 
     def one(target, carry):
-        z = lax.rem(target, z_size)
-        near_slot = target - z + lax.rem(z, NEAR_Z) * far + lax.div(z, NEAR_Z)
-        slot = jnp.where(near_first, near_slot, z * x_size + lax.div(target, z_size))
+        x = lax.div(target, z_size)
+        z = lax.rem(target + z_size - core, z_size)
+        slot = x * z_size + lax.rem(z, NEAR_Z) * far + lax.div(z, NEAR_Z)
         parts = []
         for side in range(SIDES):
             factors, picked = [], []

time: 175 us -> 163 us (0.931)
  blocking collectives: 162 us -> 149 us
    all_to_all x6, blocking collectives: 106 us -> 94.5 us  [exchange(): lax.all_to_all(array, MESH_AXES, split_axis=0, concat_axis=0, axis_index_...]
    all_gather x1, blocking collectives: 8.69 us -> 6.43 us  [on_device(): halves = lax.all_gather(parts[1], 'core', axis=0, tiled=False)]
where the time goes in v10:
time: 163 us; the launch traced here: 162 us
  blocking collectives  149 us (91%)
  Pallas kernels  10.4 us (6%)
  starting transfers between devices  2.28 us (1%)
    all_to_all x6, blocking collectives, exchange(): lax.all_to_all(array, MESH_AXES, split_axis=0, concat_axis=0, axis_index_...  94.5 us
    all_to_all x3, blocking collectives, on_device(): lax.all_to_all(copies, 'y', split_axis=0, concat_axis=0, tiled=True)  39.7 us
    all_gather x1, blocking collectives, on_device(): swapped = in_vmem(lax.all_gather(sent, 'core', axis=0, tiled=False))  8.65 us
    all_gather x1, blocking collectives, on_device(): halves = lax.all_gather(parts[1], 'core', axis=0, tiled=False)  6.43 us
    pallas_call x3, Pallas kernels, on_device(): pl.pallas_call(functools.partial(terms_kernel, pairs, x_size), out_shape=...  5.66 us
  transfers between devices with their start and end apart: 1, of which 0 were waited for; matrix products, arithmetic and copies ran while one was open for 0% of the time, Pallas kernels for 0%

profile of v10, /device:TPU:1, one launch (start us, length us, event | category | flops | bytes accessed | tf_op | source)
XLA Modules:
  0.0 162.1 jit_solution(14578465255206626305)
XLA Ops:
  0.0 0.0 copy-start.2
  0.0 0.0 copy-start
  0.0 2.2 %first.1 = (f32[64,256]{1,0:T(8,128)S(1)}, bf16[4,64,128]{2,1,0:T(8,128)(2,1)S(1)}, f32[464,128]{1,0:T(8,128)S(1)}, bf16[1,32,64,128]{3,2,1,0:T(8,128)(2,1)S(1)}) custom-call(bf16[4,64,256]{2,1,0:T(8,128)(2,1)} %bitcast.41, f32[4,64,64]{2,1,0:T(8,128)} %bitcast.33, bf16[6,32,64,128]{3,2,1,0:T(8,128)(2,1)} %bitcast.17, s32[6,2,32]{2,1,0:T(2,128)} %bitcast.39), custom_call_target="tpu_custom_call" | custom-call | tf_op jit(solution)/shard_map/first/pallas_call | solution.py:262
  2.2 8.7 %all-gather = f32[928,128]{1,0:T(8,128)S(1)} all-gather(f32[464,128]{1,0:T(8,128)S(1)} %get-tuple-element.21), channel_id=2, replica_groups=mesh['y'=8,'core'=2,'x'=4,'z'=8] {'core'}, dimensions={0}, use_global_device_ids=true | all-gather | bytes 712704 | tf_op jit(solution)/shard_map/all_gather | solution.py:280
  10.8 0.0 copy-done.2
  10.9 0.0 copy-done
  10.9 2.3 %collective-permute-start = (bf16[6,32,64,128]{3,2,1,0:T(8,128)(2,1)S(1)}, bf16[6,32,64,128]{3,2,1,0:T(8,128)(2,1)S(1)}, u32[]{:S(2)}, u32[]{:S(2)}) collective-permute-start(bf16[6,32,64,128]{3,2,1,0:T(8,128)(2,1)S(1)} %bitcast.18), channel_id=1, source_target_pairs={{0,32},{32,0},{1,33},{33,1},{2,34},{34,2},{3,35},{35,3},{4,36},{36... | collective-permute-start | bytes 9437192 | tf_op jit(solution)/shard_map/ppermute | solution.py:291
  13.2 14.8 %all_to_all.45 = bf16[8,2,64,128]{3,2,1,0:T(8,128)(2,1)S(1)} all-to-all(bf16[8,2,64,128]{3,2,1,0:T(8,128)(2,1)S(1)} %get-tuple-element.25), channel_id=1, replica_groups=mesh['y'=8,'core'=2,'x'=4,'z'=8] {'y'}, dimensions={0} | all-to-all | bytes 524288 | tf_op jit(solution)/shard_map/all_to_all | solution.py:295
  27.9 0.0 collective-permute-done.refs_1_
  28.0 1.6 %local_terms.3 = s16[32,136,128]{2,1,0:T(8,128)(2,1)S(1)} custom-call(s32[2,16,128]{2,1,0:T(8,128)S(1)} %get-tuple-element.22.table_ref, bf16[1,32,64,128]{3,2,1,0:T(8,128)(2,1)S(1)} %get-tuple-element.26.refs_0_, bf16[6,32,64,128]{3,2,1,0:T(8,128)(2,1)S(1)} %collective-permute-done.refs_1_, bf16[16,64,128]{2,1,0:T(8,128)(2,1)S(1)} %bitcast.28), custom_call_target="tpu_custom_call" | custom-call | tf_op jit(solution)/shard_map/local_terms/pallas_call | solution.py:299
  29.6 22.0 %all_to_all.46.arrived_ref = s16[8,4,136,128]{3,2,1,0:T(8,128)(2,1)S(1)} all-to-all(s16[8,4,136,128]{3,2,1,0:T(8,128)(2,1)S(1)} %bitcast.25), channel_id=1, replica_groups={{0,1,8,9,16,17,24,25},{2,3,10,11,18,19,26,27},{4,5,12,13,20,21,28,29},{..., dimensions={0} | all-to-all | bytes 2228224 | tf_op jit(solution)/shard_map/all_to_all | solution.py:246
  51.6 0.0 copy-start.1
  51.6 0.4 sum_first.3
  52.0 14.5 %all_to_all.47.arrived_ref = s16[4,136,128]{2,1,0:T(8,128)(2,1)S(1)} all-to-all(s16[4,136,128]{2,1,0:T(8,128)(2,1)S(1)} %sum_first.3), channel_id=1, replica_groups={{0,2,4,6},{1,3,5,7},{8,10,12,14},{9,11,13,15},{16,18,20,22},{17,19,21,2..., dimensions={0} | all-to-all | bytes 278528 | tf_op jit(solution)/shard_map/all_to_all | solution.py:246
  66.5 0.0 copy-done.1
  66.5 0.2 solve.2
  66.7 11.8 %all_to_all.48 = bf16[8,2,64,128]{3,2,1,0:T(8,128)(2,1)S(1)} all-to-all(bf16[8,2,64,128]{3,2,1,0:T(8,128)(2,1)S(1)} %get-tuple-element.27), channel_id=1, replica_groups=mesh['y'=8,'core'=2,'x'=4,'z'=8] {'y'}, dimensions={0} | all-to-all | bytes 524288 | tf_op jit(solution)/shard_map/all_to_all | solution.py:295
  78.6 1.8 %local_terms.4 = s16[32,136,128]{2,1,0:T(8,128)(2,1)S(1)} custom-call(s32[2,16,128]{2,1,0:T(8,128)S(1)} %get-tuple-element.22.table_ref, bf16[6,32,64,128]{3,2,1,0:T(8,128)(2,1)S(1)} %bitcast.19, bf16[6,32,64,128]{3,2,1,0:T(8,128)(2,1)S(1)} %collective-permute-done.refs_1_, bf16[16,64,128]{2,1,0:T(8,128)(2,1)S(1)} %bitcast.29, bf16[16,64,128]{2,1,0:T(8,128)(2,1)S(1)} %bitcast.31), custom_call_target="tpu_custom_call" | custom-call | tf_op jit(solution)/shard_map/local_terms/pallas_call | solution.py:299
  80.4 18.7 %all_to_all.49.arrived_ref = s16[8,4,136,128]{3,2,1,0:T(8,128)(2,1)S(1)} all-to-all(s16[8,4,136,128]{3,2,1,0:T(8,128)(2,1)S(1)} %bitcast.27), channel_id=1, replica_groups={{0,1,8,9,16,17,24,25},{2,3,10,11,18,19,26,27},{4,5,12,13,20,21,28,29},{..., dimensions={0} | all-to-all | bytes 2228224 | tf_op jit(solution)/shard_map/all_to_all | solution.py:246
  99.1 0.4 sum_first.4
  99.4 11.6 %all_to_all.50.arrived_ref = s16[4,136,128]{2,1,0:T(8,128)(2,1)S(1)} all-to-all(s16[4,136,128]{2,1,0:T(8,128)(2,1)S(1)} %sum_first.4), channel_id=1, replica_groups={{0,2,4,6},{1,3,5,7},{8,10,12,14},{9,11,13,15},{16,18,20,22},{17,19,21,2..., dimensions={0} | all-to-all | bytes 278528 | tf_op jit(solution)/shard_map/all_to_all | solution.py:246
  111.1 0.2 solve.3
  111.3 13.1 %all_to_all.51 = bf16[8,2,64,128]{3,2,1,0:T(8,128)(2,1)S(1)} all-to-all(bf16[8,2,64,128]{3,2,1,0:T(8,128)(2,1)S(1)} %get-tuple-element.28), channel_id=1, replica_groups=mesh['y'=8,'core'=2,'x'=4,'z'=8] {'y'}, dimensions={0} | all-to-all | bytes 524288 | tf_op jit(solution)/shard_map/all_to_all | solution.py:295
  124.5 2.2 %local_terms.5 = s16[32,136,128]{2,1,0:T(8,128)(2,1)S(1)} custom-call(s32[2,16,128]{2,1,0:T(8,128)S(1)} %get-tuple-element.22.table_ref, bf16[6,32,64,128]{3,2,1,0:T(8,128)(2,1)S(1)} %bitcast.20, bf16[6,32,64,128]{3,2,1,0:T(8,128)(2,1)S(1)} %collective-permute-done.refs_1_, bf16[16,64,128]{2,1,0:T(8,128)(2,1)S(1)} %bitcast.30, ...), custom_call_target="tpu_custom_call" | custom-call | tf_op jit(solution)/shard_map/local_terms/pallas_call | solution.py:299
  126.7 17.9 %all_to_all.52.arrived_ref = s16[8,4,136,128]{3,2,1,0:T(8,128)(2,1)S(1)} all-to-all(s16[8,4,136,128]{3,2,1,0:T(8,128)(2,1)S(1)} %bitcast.26), channel_id=1, replica_groups={{0,1,8,9,16,17,24,25},{2,3,10,11,18,19,26,27},{4,5,12,13,20,21,28,29},{..., dimensions={0} | all-to-all | bytes 2228224 | tf_op jit(solution)/shard_map/all_to_all | solution.py:246
  144.7 0.4 sum_first.5
  145.0 9.7 %all_to_all.53.arrived_ref = s16[4,136,128]{2,1,0:T(8,128)(2,1)S(1)} all-to-all(s16[4,136,128]{2,1,0:T(8,128)(2,1)S(1)} %sum_first.5), channel_id=1, replica_groups={{0,2,4,6},{1,3,5,7},{8,10,12,14},{9,11,13,15},{16,18,20,22},{17,19,21,2..., dimensions={0} | all-to-all | bytes 278528 | tf_op jit(solution)/shard_map/all_to_all | solution.py:246
  154.7 0.2 solve_last.1
  155.0 6.4 %all-gather.1 = f32[6,64,128]{2,1,0:T(8,128)S(1)} all-gather(f32[3,64,128]{2,1,0:T(8,128)S(1)} %get-tuple-element.32), channel_id=3, replica_groups=mesh['y'=8,'core'=2,'x'=4,'z'=8] {'core'}, dimensions={0}, use_global_device_ids=true | all-gather | bytes 294912 | tf_op jit(solution)/shard_map/all_gather | solution.py:341
  161.4 0.7 join.1
  (1 shorter events, 0.0 us)
Async XLA Ops:
  0.0 10.8 %copy-start.2 = (s32[6,1,1,32,2]{3,4,2,1,0:T(2,128)S(1)}, s32[6,1,1,32,2]{3,4,2,1,0:T(2,128)}, u32[]{:S(2)}) copy-start(s32[6,1,1,32,2]{3,4,2,1,0:T(2,128)} %param.7) | copy-start | bytes 4612
  0.0 10.9 %copy-start = (bf16[6,1,1,32,64,128]{5,4,3,2,1,0:T(8,128)(2,1)S(1)}, bf16[6,1,1,32,64,128]{5,4,3,2,1,0:T(8,128)(2,1)}, u32[]{:S(2)}) copy-start(bf16[6,1,1,32,64,128]{5,4,3,2,1,0:T(8,128)(2,1)} %param.6) | copy-start | bytes 9437188
  10.9 17.1 %collective-permute-start = (bf16[6,32,64,128]{3,2,1,0:T(8,128)(2,1)S(1)}, bf16[6,32,64,128]{3,2,1,0:T(8,128)(2,1)S(1)}, u32[]{:S(2)}, u32[]{:S(2)}) collective-permute-start(bf16[6,32,64,128]{3,2,1,0:T(8,128)(2,1)S(1)} %bitcast.18), channel_id=1, source_target_pairs={{0,32},{32,0},{1,33},{33,1},{2,34},{34,2},{3,35},{35,3},{4,36},{36... | collective-permute-start | bytes 9437192 | tf_op jit(solution)/shard_map/ppermute | solution.py:291
  51.6 14.9 %copy-start.1 = (f32[4,1,1,64,64]{4,3,2,1,0:T(8,128)S(1)}, f32[4,1,1,64,64]{4,3,2,1,0:T(8,128)}, u32[]{:S(2)}) copy-start(f32[4,1,1,64,64]{4,3,2,1,0:T(8,128)} %param.5) | copy-start | bytes 196612

commit v11 on v8

--- a/solution.py
+++ b/solution.py
@@ -25,14 +25,19 @@
     return pltpu.with_memory_space_constraint(array, pltpu.HBM)
 
 
+def code(part):
+    largest = jnp.max(jnp.abs(part), axis=0, keepdims=True)
+    power = jnp.ceil(jnp.log2(jnp.maximum(largest * 1.001, 1e-30)))
+    coded = jnp.round(part * jnp.exp2(15.0 - power)).astype(jnp.int32)
+    return coded.astype(jnp.int16), power
+
+
 def encode(parts, out_ref, index):
     powers = []
     for side, part in enumerate(parts):
         rows = part.shape[0]
-        largest = jnp.max(jnp.abs(part), axis=0, keepdims=True)
-        power = jnp.ceil(jnp.log2(jnp.maximum(largest * 1.001, 1e-30)))
-        coded = jnp.round(part * jnp.exp2(15.0 - power)).astype(jnp.int32)
-        out_ref[index, side * rows : (side + 1) * rows, :] = coded.astype(jnp.int16)
+        coded, power = code(part)
+        out_ref[index, side * rows : (side + 1) * rows, :] = coded
         powers.append(jnp.broadcast_to(power, (PAD // len(parts), LANES)))
     powers = jnp.concatenate(powers, axis=0).astype(jnp.int32)
     out_ref[index, len(parts) * rows : len(parts) * rows + PAD, :] = powers.astype(jnp.int16)
@@ -125,39 +130,56 @@
     _, targets, block_rows, depth = lowers[0].shape
     per = depth // block_rows
     za_size, zb_size = z_sizes
-    z_size = za_size * zb_size
     none = blocks_ref.shape[1] - 1
     for place, block in enumerate(gathered):
         blocks_ref[place, 0:none] = block[...]
         blocks_ref[place, none] = jnp.zeros(blocks_ref.shape[2:], blocks_ref.dtype)
 
-    def one(target, carry):
-        z = lax.rem(target, z_size)
-        slot = target - z + lax.rem(z, zb_size) * za_size + lax.div(z, zb_size)
-        parts = []
+    def sums(target):
         for side in range(SIDES):
             factors, picked = [], []
             for place, pair in enumerate(pairs):
                 factors.append(lowers[side][pair, target])
                 for entry in range(per):
                     picked.append(blocks_ref[place, table_ref[side, pair * per + entry, target]])
-            parts.append(
-                jnp.dot(
-                    jnp.concatenate(factors, axis=1),
-                    jnp.concatenate(picked, axis=0),
-                    preferred_element_type=jnp.float32,
-                )
+            yield jnp.dot(
+                jnp.concatenate(factors, axis=1),
+                jnp.concatenate(picked, axis=0),
+                preferred_element_type=jnp.float32,
             )
-        encode(parts, out_ref, slot)
-        return carry
-
-    lax.fori_loop(0, targets, one, 0, unroll=True)
-
-
-def middle_kernel(arrived_ref, out_ref):
-    peers, targets = arrived_ref.shape[:2]
-    for target in range(targets):
-        encode(add_peers(peers, lambda peer: arrived_ref[peer, target]), out_ref, target)
+
+    tail = za_size * SIDES * block_rows
+    for peer in range(targets // za_size):
+        x, zb = divmod(peer, zb_size)
+        powers, row = [], 0
+        for za in range(za_size):
+            for part in sums((x * za_size + za) * zb_size + zb):
+                coded, power = code(part)
+                out_ref[peer, row : row + block_rows, :] = coded
+                powers.append(power)
+                row += block_rows
+        powers = jnp.concatenate(powers, axis=0).astype(jnp.int32)
+        out_ref[peer, tail : tail + za_size * SIDES, :] = powers.astype(jnp.int16)
+
+
+def middle_kernel(za_size, arrived_ref, out_ref):
+    peers = arrived_ref.shape[0]
+    places = za_size * SIDES
+    block_rows = arrived_ref.shape[1] // places - 1
+    scales = []
+    for peer in range(peers):
+        powers = arrived_ref[peer, places * block_rows :, :].astype(jnp.int32)
+        scales.append(jnp.exp2(powers.astype(jnp.float32) - 15.0))
+    for za in range(za_size):
+        parts = []
+        for place in range(za * SIDES, (za + 1) * SIDES):
+            total = None
+            for peer in range(peers):
+                block = arrived_ref[peer, place * block_rows : (place + 1) * block_rows, :]
+                part = block.astype(jnp.int32).astype(jnp.float32) * scales[peer][place : place + 1, :]
+                total = part if total is None else total + part
+            parts.append(total)
+        encode(parts, out_ref, za)
 
 
 def solve_parts(level, mine_ref, swapped_ref, dinv_ref, arrived_ref):
@@ -221,6 +243,7 @@
     sources = jnp.swapaxes(sources[:, 0, 0], 1, 2)
     targets = lower.shape[1]
     coded_rows = SIDES * block_rows + PAD
+    near_rows = za_size * SIDES * (block_rows + 1)
     copies_shape = pltpu.VMEM((y_size, SIDES, block_rows, LANES), jnp.bfloat16)
 
     table_rows = -(-sources.shape[0] * sources.shape[1] // PAD) * PAD
@@ -264,7 +287,7 @@
         own = early if level == 1 else lower
         coded = pl.pallas_call(
             functools.partial(terms_kernel, pairs, (za_size, zb_size)),
-            out_shape=pltpu.VMEM((targets, coded_rows, LANES), jnp.int16),
+            out_shape=pltpu.VMEM((x_size * zb_size, near_rows, LANES), jnp.int16),
             in_specs=[SMEM] + [VMEM] * (SIDES + len(gathered)),
             out_specs=VMEM,
             scratch_shapes=[
@@ -273,10 +296,9 @@
             compiler_params=PARAMS,
             name="local_terms",
         )(table, in_vmem(own), in_vmem(other_lower), *gathered)
-        coded = coded.reshape(x_size * zb_size, za_size, coded_rows, LANES)
         arrived = lax.all_to_all(coded, ("x", "zb"), split_axis=0, concat_axis=0, tiled=True)
         coded = pl.pallas_call(
-            middle_kernel,
+            functools.partial(middle_kernel, za_size),
             out_shape=pltpu.VMEM((za_size, coded_rows, LANES), jnp.int16),
             in_specs=[VMEM],
             out_specs=VMEM,

time: 158 us -> 157 us (level)
  no operation moved by 1% of the time
where the time goes in v11:
time: 157 us; the launch traced here: 156 us
  blocking collectives  143 us (91%)
  Pallas kernels  10.3 us (7%)
  starting transfers between devices  2.28 us (1%)
    all_to_all x3, blocking collectives, on_device(): lax.all_to_all(coded, ('x', 'zb'), split_axis=0, concat_axis=0, tiled=True)  46.6 us
    all_to_all x3, blocking collectives, on_device(): lax.all_to_all(copies, 'y', split_axis=0, concat_axis=0, tiled=True)  38.4 us
    all_to_all x3, blocking collectives, on_device(): lax.all_to_all(coded, 'za', split_axis=0, concat_axis=0, tiled=True)  36 us
    all_gather x1, blocking collectives, on_device(): halves = lax.all_gather(parts[1], 'core', axis=0, tiled=False)  13.9 us
    all_gather x1, blocking collectives, on_device(): swapped = in_vmem(lax.all_gather(sent, 'core', axis=0, tiled=False))  8.65 us
    pallas_call x3, Pallas kernels, on_device(): pl.pallas_call(functools.partial(terms_kernel, pairs, (za_size, zb_size))...  5.67 us
  transfers between devices with their start and end apart: 1, of which 0 were waited for; matrix products, arithmetic and copies ran while one was open for 0% of the time, Pallas kernels for 0%

profile of v11, /device:TPU:1, one launch (start us, length us, event | category | flops | bytes accessed | tf_op | source)
XLA Modules:
  0.0 156.1 jit_solution(12079856447827737790)
XLA Ops:
  0.0 0.0 copy-start.2
  0.0 0.0 copy-start
  0.0 2.2 %first.1 = (f32[64,256]{1,0:T(8,128)S(1)}, bf16[4,64,128]{2,1,0:T(8,128)(2,1)S(1)}, f32[464,128]{1,0:T(8,128)S(1)}, bf16[1,32,64,128]{3,2,1,0:T(8,128)(2,1)S(1)}) custom-call(bf16[4,64,256]{2,1,0:T(8,128)(2,1)} %bitcast.35, f32[4,64,64]{2,1,0:T(8,128)} %bitcast.27, bf16[6,32,64,128]{3,2,1,0:T(8,128)(2,1)} %bitcast.14, s32[6,2,32]{2,1,0:T(2,128)} %bitcast.33), custom_call_target="tpu_custom_call" | custom-call | tf_op jit(solution)/shard_map/first/pallas_call | solution.py:251
  2.2 8.7 %all-gather = f32[928,128]{1,0:T(8,128)S(1)} all-gather(f32[464,128]{1,0:T(8,128)S(1)} %get-tuple-element.21), channel_id=2, replica_groups=mesh['y'=8,'core'=2,'x'=4,'za'=4,'zb'=2] {'core'}, dimensions={0}, use_global_device_ids=true | all-gather | bytes 712704 | tf_op jit(solution)/shard_map/all_gather | solution.py:269
  10.8 0.0 copy-done.2
  10.9 0.0 copy-done
  10.9 2.3 %collective-permute-start = (bf16[6,32,64,128]{3,2,1,0:T(8,128)(2,1)S(1)}, bf16[6,32,64,128]{3,2,1,0:T(8,128)(2,1)S(1)}, u32[]{:S(2)}, u32[]{:S(2)}) collective-permute-start(bf16[6,32,64,128]{3,2,1,0:T(8,128)(2,1)S(1)} %bitcast.15), channel_id=1, source_target_pairs={{0,32},{32,0},{1,33},{33,1},{2,34},{34,2},{3,35},{35,3},{4,36},{36... | collective-permute-start | bytes 9437192 | tf_op jit(solution)/shard_map/ppermute | solution.py:280
  13.2 14.8 %all_to_all.45 = bf16[8,2,64,128]{3,2,1,0:T(8,128)(2,1)S(1)} all-to-all(bf16[8,2,64,128]{3,2,1,0:T(8,128)(2,1)S(1)} %get-tuple-element.25), channel_id=1, replica_groups=mesh['y'=8,'core'=2,'x'=4,'za'=4,'zb'=2] {'y'}, dimensions={0} | all-to-all | bytes 524288 | tf_op jit(solution)/shard_map/all_to_all | solution.py:284
  27.9 0.0 collective-permute-done.refs_1_
  28.0 1.6 local_terms.3
  29.5 19.4 %all_to_all.46.arrived_ref = s16[8,520,128]{2,1,0:T(8,128)(2,1)S(1)} all-to-all(s16[8,520,128]{2,1,0:T(8,128)(2,1)S(1)} %local_terms.3), channel_id=1, replica_groups=mesh['y'=8,'core'=2,'x'=4,'za'=4,'zb'=2] {'x','zb'}, dimensions={0} | all-to-all | bytes 2129920 | tf_op jit(solution)/shard_map/all_to_all | solution.py:299
  48.9 0.0 copy-start.1
  48.9 0.3 sum_near.3
  49.2 16.3 %all_to_all.47.arrived_ref = s16[4,136,128]{2,1,0:T(8,128)(2,1)S(1)} all-to-all(s16[4,136,128]{2,1,0:T(8,128)(2,1)S(1)} %sum_near.3), channel_id=1, replica_groups=mesh['y'=8,'core'=2,'x'=4,'za'=4,'zb'=2] {'za'}, dimensions={0} | all-to-all | bytes 278528 | tf_op jit(solution)/shard_map/all_to_all | solution.py:308
  65.5 0.0 copy-done.1
  65.5 0.2 solve.2
  65.8 11.8 %all_to_all.48 = bf16[8,2,64,128]{3,2,1,0:T(8,128)(2,1)S(1)} all-to-all(bf16[8,2,64,128]{3,2,1,0:T(8,128)(2,1)S(1)} %get-tuple-element.27), channel_id=1, replica_groups=mesh['y'=8,'core'=2,'x'=4,'za'=4,'zb'=2] {'y'}, dimensions={0} | all-to-all | bytes 524288 | tf_op jit(solution)/shard_map/all_to_all | solution.py:284
  77.6 1.8 %local_terms.4 = s16[8,520,128]{2,1,0:T(8,128)(2,1)S(1)} custom-call(s32[2,16,128]{2,1,0:T(8,128)S(1)} %get-tuple-element.22.table_ref, bf16[6,32,64,128]{3,2,1,0:T(8,128)(2,1)S(1)} %bitcast.16, bf16[6,32,64,128]{3,2,1,0:T(8,128)(2,1)S(1)} %collective-permute-done.refs_1_, bf16[16,64,128]{2,1,0:T(8,128)(2,1)S(1)} %bitcast.23, bf16[16,64,128]{2,1,0:T(8,128)(2,1)S(1)} %bitcast.25), custom_call_target="tpu_custom_call" | custom-call | tf_op jit(solution)/shard_map/local_terms/pallas_call | solution.py:288
  79.5 14.1 %all_to_all.49.arrived_ref = s16[8,520,128]{2,1,0:T(8,128)(2,1)S(1)} all-to-all(s16[8,520,128]{2,1,0:T(8,128)(2,1)S(1)} %local_terms.4), channel_id=1, replica_groups=mesh['y'=8,'core'=2,'x'=4,'za'=4,'zb'=2] {'x','zb'}, dimensions={0} | all-to-all | bytes 2129920 | tf_op jit(solution)/shard_map/all_to_all | solution.py:299
  93.5 0.3 sum_near.4
  93.9 9.7 %all_to_all.50.arrived_ref = s16[4,136,128]{2,1,0:T(8,128)(2,1)S(1)} all-to-all(s16[4,136,128]{2,1,0:T(8,128)(2,1)S(1)} %sum_near.4), channel_id=1, replica_groups=mesh['y'=8,'core'=2,'x'=4,'za'=4,'zb'=2] {'za'}, dimensions={0} | all-to-all | bytes 278528 | tf_op jit(solution)/shard_map/all_to_all | solution.py:308
  103.5 0.2 solve.3
  103.8 11.7 %all_to_all.51 = bf16[8,2,64,128]{3,2,1,0:T(8,128)(2,1)S(1)} all-to-all(bf16[8,2,64,128]{3,2,1,0:T(8,128)(2,1)S(1)} %get-tuple-element.28), channel_id=1, replica_groups=mesh['y'=8,'core'=2,'x'=4,'za'=4,'zb'=2] {'y'}, dimensions={0} | all-to-all | bytes 524288 | tf_op jit(solution)/shard_map/all_to_all | solution.py:284
  115.5 2.3 %local_terms.5 = s16[8,520,128]{2,1,0:T(8,128)(2,1)S(1)} custom-call(s32[2,16,128]{2,1,0:T(8,128)S(1)} %get-tuple-element.22.table_ref, bf16[6,32,64,128]{3,2,1,0:T(8,128)(2,1)S(1)} %bitcast.17, bf16[6,32,64,128]{3,2,1,0:T(8,128)(2,1)S(1)} %collective-permute-done.refs_1_, bf16[16,64,128]{2,1,0:T(8,128)(2,1)S(1)} %bitcast.24, ...), custom_call_target="tpu_custom_call" | custom-call | tf_op jit(solution)/shard_map/local_terms/pallas_call | solution.py:288
  117.8 13.1 %all_to_all.52.arrived_ref = s16[8,520,128]{2,1,0:T(8,128)(2,1)S(1)} all-to-all(s16[8,520,128]{2,1,0:T(8,128)(2,1)S(1)} %local_terms.5), channel_id=1, replica_groups=mesh['y'=8,'core'=2,'x'=4,'za'=4,'zb'=2] {'x','zb'}, dimensions={0} | all-to-all | bytes 2129920 | tf_op jit(solution)/shard_map/all_to_all | solution.py:299
  130.9 0.3 sum_near.5
  131.3 10.0 %all_to_all.53.arrived_ref = s16[4,136,128]{2,1,0:T(8,128)(2,1)S(1)} all-to-all(s16[4,136,128]{2,1,0:T(8,128)(2,1)S(1)} %sum_near.5), channel_id=1, replica_groups=mesh['y'=8,'core'=2,'x'=4,'za'=4,'zb'=2] {'za'}, dimensions={0} | all-to-all | bytes 278528 | tf_op jit(solution)/shard_map/all_to_all | solution.py:308
  141.3 0.2 solve_last.1
  141.5 13.9 %all-gather.1 = f32[6,64,128]{2,1,0:T(8,128)S(1)} all-gather(f32[3,64,128]{2,1,0:T(8,128)S(1)} %get-tuple-element.32), channel_id=3, replica_groups=mesh['y'=8,'core'=2,'x'=4,'za'=4,'zb'=2] {'core'}, dimensions={0}, use_global_device_ids=true | all-gather | bytes 294912 | tf_op jit(solution)/shard_map/all_gather | solution.py:329
  155.4 0.7 join.1
  (1 shorter events, 0.0 us)
Async XLA Ops:
  0.0 10.8 %copy-start.2 = (s32[6,1,1,32,2]{3,4,2,1,0:T(2,128)S(1)}, s32[6,1,1,32,2]{3,4,2,1,0:T(2,128)}, u32[]{:S(2)}) copy-start(s32[6,1,1,32,2]{3,4,2,1,0:T(2,128)} %param.7) | copy-start | bytes 4612
  0.0 10.9 %copy-start = (bf16[6,1,1,32,64,128]{5,4,3,2,1,0:T(8,128)(2,1)S(1)}, bf16[6,1,1,32,64,128]{5,4,3,2,1,0:T(8,128)(2,1)}, u32[]{:S(2)}) copy-start(bf16[6,1,1,32,64,128]{5,4,3,2,1,0:T(8,128)(2,1)} %param.6) | copy-start | bytes 9437188
  10.9 17.1 %collective-permute-start = (bf16[6,32,64,128]{3,2,1,0:T(8,128)(2,1)S(1)}, bf16[6,32,64,128]{3,2,1,0:T(8,128)(2,1)S(1)}, u32[]{:S(2)}, u32[]{:S(2)}) collective-permute-start(bf16[6,32,64,128]{3,2,1,0:T(8,128)(2,1)S(1)} %bitcast.15), channel_id=1, source_target_pairs={{0,32},{32,0},{1,33},{33,1},{2,34},{34,2},{3,35},{35,3},{4,36},{36... | collective-permute-start | bytes 9437192 | tf_op jit(solution)/shard_map/ppermute | solution.py:280
  48.9 16.6 %copy-start.1 = (f32[4,1,1,64,64]{4,3,2,1,0:T(8,128)S(1)}, f32[4,1,1,64,64]{4,3,2,1,0:T(8,128)}, u32[]{:S(2)}) copy-start(f32[4,1,1,64,64]{4,3,2,1,0:T(8,128)} %param.5) | copy-start | bytes 196612

commit v12 on v11

--- a/solution.py
+++ b/solution.py
@@ -11,6 +11,7 @@
 PAD = 8
 SIDES = 2
 KERNEL_VMEM = 12 << 20
+SMALLEST = 2.0**-111
 VMEM = pl.BlockSpec(memory_space=pltpu.VMEM)
 SMEM = pl.BlockSpec(memory_space=pltpu.SMEM)
 ANY = pl.BlockSpec(memory_space=pl.ANY)
@@ -27,7 +28,7 @@
 
 def code(part):
     largest = jnp.max(jnp.abs(part), axis=0, keepdims=True)
-    power = jnp.ceil(jnp.log2(jnp.maximum(largest * 1.001, 1e-30)))
+    power = jnp.ceil(jnp.log2(jnp.maximum(largest * 1.001, SMALLEST)))
     coded = jnp.round(part * jnp.exp2(15.0 - power)).astype(jnp.int32)
     return coded.astype(jnp.int16), power
 

time: 157 us -> 157 us (level)
  no operation moved by 1% of the time
where the time goes in v12:
time: 157 us; the launch traced here: 156 us
  blocking collectives  143 us (91%)
  Pallas kernels  10.3 us (7%)
  starting transfers between devices  2.28 us (1%)
    all_to_all x3, blocking collectives, on_device(): lax.all_to_all(coded, ('x', 'zb'), split_axis=0, concat_axis=0, tiled=True)  46.6 us
    all_to_all x3, blocking collectives, on_device(): lax.all_to_all(copies, 'y', split_axis=0, concat_axis=0, tiled=True)  38.4 us
    all_to_all x3, blocking collectives, on_device(): lax.all_to_all(coded, 'za', split_axis=0, concat_axis=0, tiled=True)  36 us
    all_gather x1, blocking collectives, on_device(): halves = lax.all_gather(parts[1], 'core', axis=0, tiled=False)  13.9 us
    all_gather x1, blocking collectives, on_device(): swapped = in_vmem(lax.all_gather(sent, 'core', axis=0, tiled=False))  8.65 us
    pallas_call x3, Pallas kernels, on_device(): pl.pallas_call(functools.partial(terms_kernel, pairs, (za_size, zb_size))...  5.66 us
  transfers between devices with their start and end apart: 1, of which 0 were waited for; matrix products, arithmetic and copies ran while one was open for 0% of the time, Pallas kernels for 0%

profile of v12, /device:TPU:1, one launch (start us, length us, event | category | flops | bytes accessed | tf_op | source)
XLA Modules:
  0.0 156.1 jit_solution(9623425830633335032)
XLA Ops:
  0.0 0.0 copy-start.2
  0.0 0.0 copy-start
  0.0 2.2 %first.1 = (f32[64,256]{1,0:T(8,128)S(1)}, bf16[4,64,128]{2,1,0:T(8,128)(2,1)S(1)}, f32[464,128]{1,0:T(8,128)S(1)}, bf16[1,32,64,128]{3,2,1,0:T(8,128)(2,1)S(1)}) custom-call(bf16[4,64,256]{2,1,0:T(8,128)(2,1)} %bitcast.35, f32[4,64,64]{2,1,0:T(8,128)} %bitcast.27, bf16[6,32,64,128]{3,2,1,0:T(8,128)(2,1)} %bitcast.14, s32[6,2,32]{2,1,0:T(2,128)} %bitcast.33), custom_call_target="tpu_custom_call" | custom-call | tf_op jit(solution)/shard_map/first/pallas_call | solution.py:252
  2.2 8.7 %all-gather = f32[928,128]{1,0:T(8,128)S(1)} all-gather(f32[464,128]{1,0:T(8,128)S(1)} %get-tuple-element.21), channel_id=2, replica_groups=mesh['y'=8,'core'=2,'x'=4,'za'=4,'zb'=2] {'core'}, dimensions={0}, use_global_device_ids=true | all-gather | bytes 712704 | tf_op jit(solution)/shard_map/all_gather | solution.py:270
  10.8 0.0 copy-done.2
  10.9 0.0 copy-done
  10.9 2.3 %collective-permute-start = (bf16[6,32,64,128]{3,2,1,0:T(8,128)(2,1)S(1)}, bf16[6,32,64,128]{3,2,1,0:T(8,128)(2,1)S(1)}, u32[]{:S(2)}, u32[]{:S(2)}) collective-permute-start(bf16[6,32,64,128]{3,2,1,0:T(8,128)(2,1)S(1)} %bitcast.15), channel_id=1, source_target_pairs={{0,32},{32,0},{1,33},{33,1},{2,34},{34,2},{3,35},{35,3},{4,36},{36... | collective-permute-start | bytes 9437192 | tf_op jit(solution)/shard_map/ppermute | solution.py:281
  13.2 14.8 %all_to_all.45 = bf16[8,2,64,128]{3,2,1,0:T(8,128)(2,1)S(1)} all-to-all(bf16[8,2,64,128]{3,2,1,0:T(8,128)(2,1)S(1)} %get-tuple-element.25), channel_id=1, replica_groups=mesh['y'=8,'core'=2,'x'=4,'za'=4,'zb'=2] {'y'}, dimensions={0} | all-to-all | bytes 524288 | tf_op jit(solution)/shard_map/all_to_all | solution.py:285
  27.9 0.0 collective-permute-done.refs_1_
  28.0 1.6 local_terms.3
  29.5 19.4 %all_to_all.46.arrived_ref = s16[8,520,128]{2,1,0:T(8,128)(2,1)S(1)} all-to-all(s16[8,520,128]{2,1,0:T(8,128)(2,1)S(1)} %local_terms.3), channel_id=1, replica_groups=mesh['y'=8,'core'=2,'x'=4,'za'=4,'zb'=2] {'x','zb'}, dimensions={0} | all-to-all | bytes 2129920 | tf_op jit(solution)/shard_map/all_to_all | solution.py:300
  48.9 0.0 copy-start.1
  48.9 0.3 sum_near.3
  49.2 16.3 %all_to_all.47.arrived_ref = s16[4,136,128]{2,1,0:T(8,128)(2,1)S(1)} all-to-all(s16[4,136,128]{2,1,0:T(8,128)(2,1)S(1)} %sum_near.3), channel_id=1, replica_groups=mesh['y'=8,'core'=2,'x'=4,'za'=4,'zb'=2] {'za'}, dimensions={0} | all-to-all | bytes 278528 | tf_op jit(solution)/shard_map/all_to_all | solution.py:309
  65.5 0.0 copy-done.1
  65.5 0.2 solve.2
  65.8 11.8 %all_to_all.48 = bf16[8,2,64,128]{3,2,1,0:T(8,128)(2,1)S(1)} all-to-all(bf16[8,2,64,128]{3,2,1,0:T(8,128)(2,1)S(1)} %get-tuple-element.27), channel_id=1, replica_groups=mesh['y'=8,'core'=2,'x'=4,'za'=4,'zb'=2] {'y'}, dimensions={0} | all-to-all | bytes 524288 | tf_op jit(solution)/shard_map/all_to_all | solution.py:285
  77.6 1.8 %local_terms.4 = s16[8,520,128]{2,1,0:T(8,128)(2,1)S(1)} custom-call(s32[2,16,128]{2,1,0:T(8,128)S(1)} %get-tuple-element.22.table_ref, bf16[6,32,64,128]{3,2,1,0:T(8,128)(2,1)S(1)} %bitcast.16, bf16[6,32,64,128]{3,2,1,0:T(8,128)(2,1)S(1)} %collective-permute-done.refs_1_, bf16[16,64,128]{2,1,0:T(8,128)(2,1)S(1)} %bitcast.23, bf16[16,64,128]{2,1,0:T(8,128)(2,1)S(1)} %bitcast.25), custom_call_target="tpu_custom_call" | custom-call | tf_op jit(solution)/shard_map/local_terms/pallas_call | solution.py:289
  79.4 14.1 %all_to_all.49.arrived_ref = s16[8,520,128]{2,1,0:T(8,128)(2,1)S(1)} all-to-all(s16[8,520,128]{2,1,0:T(8,128)(2,1)S(1)} %local_terms.4), channel_id=1, replica_groups=mesh['y'=8,'core'=2,'x'=4,'za'=4,'zb'=2] {'x','zb'}, dimensions={0} | all-to-all | bytes 2129920 | tf_op jit(solution)/shard_map/all_to_all | solution.py:300
  93.5 0.3 sum_near.4
  93.9 9.7 %all_to_all.50.arrived_ref = s16[4,136,128]{2,1,0:T(8,128)(2,1)S(1)} all-to-all(s16[4,136,128]{2,1,0:T(8,128)(2,1)S(1)} %sum_near.4), channel_id=1, replica_groups=mesh['y'=8,'core'=2,'x'=4,'za'=4,'zb'=2] {'za'}, dimensions={0} | all-to-all | bytes 278528 | tf_op jit(solution)/shard_map/all_to_all | solution.py:309
  103.5 0.2 solve.3
  103.8 11.7 %all_to_all.51 = bf16[8,2,64,128]{3,2,1,0:T(8,128)(2,1)S(1)} all-to-all(bf16[8,2,64,128]{3,2,1,0:T(8,128)(2,1)S(1)} %get-tuple-element.28), channel_id=1, replica_groups=mesh['y'=8,'core'=2,'x'=4,'za'=4,'zb'=2] {'y'}, dimensions={0} | all-to-all | bytes 524288 | tf_op jit(solution)/shard_map/all_to_all | solution.py:285
  115.5 2.3 %local_terms.5 = s16[8,520,128]{2,1,0:T(8,128)(2,1)S(1)} custom-call(s32[2,16,128]{2,1,0:T(8,128)S(1)} %get-tuple-element.22.table_ref, bf16[6,32,64,128]{3,2,1,0:T(8,128)(2,1)S(1)} %bitcast.17, bf16[6,32,64,128]{3,2,1,0:T(8,128)(2,1)S(1)} %collective-permute-done.refs_1_, bf16[16,64,128]{2,1,0:T(8,128)(2,1)S(1)} %bitcast.24, ...), custom_call_target="tpu_custom_call" | custom-call | tf_op jit(solution)/shard_map/local_terms/pallas_call | solution.py:289
  117.8 13.1 %all_to_all.52.arrived_ref = s16[8,520,128]{2,1,0:T(8,128)(2,1)S(1)} all-to-all(s16[8,520,128]{2,1,0:T(8,128)(2,1)S(1)} %local_terms.5), channel_id=1, replica_groups=mesh['y'=8,'core'=2,'x'=4,'za'=4,'zb'=2] {'x','zb'}, dimensions={0} | all-to-all | bytes 2129920 | tf_op jit(solution)/shard_map/all_to_all | solution.py:300
  130.9 0.3 sum_near.5
  131.3 10.0 %all_to_all.53.arrived_ref = s16[4,136,128]{2,1,0:T(8,128)(2,1)S(1)} all-to-all(s16[4,136,128]{2,1,0:T(8,128)(2,1)S(1)} %sum_near.5), channel_id=1, replica_groups=mesh['y'=8,'core'=2,'x'=4,'za'=4,'zb'=2] {'za'}, dimensions={0} | all-to-all | bytes 278528 | tf_op jit(solution)/shard_map/all_to_all | solution.py:309
  141.3 0.2 solve_last.1
  141.5 13.9 %all-gather.1 = f32[6,64,128]{2,1,0:T(8,128)S(1)} all-gather(f32[3,64,128]{2,1,0:T(8,128)S(1)} %get-tuple-element.32), channel_id=3, replica_groups=mesh['y'=8,'core'=2,'x'=4,'za'=4,'zb'=2] {'core'}, dimensions={0}, use_global_device_ids=true | all-gather | bytes 294912 | tf_op jit(solution)/shard_map/all_gather | solution.py:330
  155.4 0.7 join.1
  (1 shorter events, 0.0 us)
Async XLA Ops:
  0.0 10.8 %copy-start.2 = (s32[6,1,1,32,2]{3,4,2,1,0:T(2,128)S(1)}, s32[6,1,1,32,2]{3,4,2,1,0:T(2,128)}, u32[]{:S(2)}) copy-start(s32[6,1,1,32,2]{3,4,2,1,0:T(2,128)} %param.7) | copy-start | bytes 4612
  0.0 10.9 %copy-start = (bf16[6,1,1,32,64,128]{5,4,3,2,1,0:T(8,128)(2,1)S(1)}, bf16[6,1,1,32,64,128]{5,4,3,2,1,0:T(8,128)(2,1)}, u32[]{:S(2)}) copy-start(bf16[6,1,1,32,64,128]{5,4,3,2,1,0:T(8,128)(2,1)} %param.6) | copy-start | bytes 9437188
  10.9 17.1 %collective-permute-start = (bf16[6,32,64,128]{3,2,1,0:T(8,128)(2,1)S(1)}, bf16[6,32,64,128]{3,2,1,0:T(8,128)(2,1)S(1)}, u32[]{:S(2)}, u32[]{:S(2)}) collective-permute-start(bf16[6,32,64,128]{3,2,1,0:T(8,128)(2,1)S(1)} %bitcast.15), channel_id=1, source_target_pairs={{0,32},{32,0},{1,33},{33,1},{2,34},{34,2},{3,35},{35,3},{4,36},{36... | collective-permute-start | bytes 9437192 | tf_op jit(solution)/shard_map/ppermute | solution.py:281
  48.9 16.6 %copy-start.1 = (f32[4,1,1,64,64]{4,3,2,1,0:T(8,128)S(1)}, f32[4,1,1,64,64]{4,3,2,1,0:T(8,128)}, u32[]{:S(2)}) copy-start(f32[4,1,1,64,64]{4,3,2,1,0:T(8,128)} %param.5) | copy-start | bytes 196612
